TPU v7x, 32 devices: a whole 2x2x4 slice. The times are simulated.
32 devices in a mesh: dp: 8 (over y, x, core), tensor: 4 (over z).
Axes of the slice: x: 2, y: 2, z: 4, core: 2. Of those that a mesh axis runs over, the one named last changes fastest.
Arguments:
- layer_input: bfloat16 [32768, 768], P('dp'), may hold values from -6 to 6
- segments: int32 [32, 1024], P('dp'), may hold values from 0 to 7, never falling along the last dimension, each value on 1 to 512 neighbouring positions
- query_weight: bfloat16 [768, 768], P(None, 'tensor'), may hold values from -0.21875 to 0.21875
- query_bias: float32 [768], P('tensor'), may hold values from -3 to 3
- key_weight: bfloat16 [768, 768], P(None, 'tensor'), may hold values from -0.21875 to 0.21875
- value_weight: bfloat16 [768, 768], P(None, 'tensor'), may hold values from -0.21875 to 0.21875
- value_bias: float32 [768], P('tensor'), may hold values from -3 to 3
- output_weight: bfloat16 [768, 768], P('tensor'), may hold values from -0.875 to 0.875
- output_bias: float32 [768], replicated, may hold values from -3 to 3
- first_gain: float32 [768], replicated, may hold values from 0.5 to 1.5
- first_shift: float32 [768], replicated, may hold values from -3 to 3
- up_weight: bfloat16 [768, 3072], P(None, 'tensor'), may hold values from -0.21875 to 0.21875
- up_bias: float32 [3072], P('tensor'), may hold values from -3 to 3
- down_weight: bfloat16 [3072, 768], P('tensor'), may hold values from -0.109375 to 0.109375
- down_bias: float32 [768], replicated, may hold values from -3 to 3
- second_gain: float32 [768], replicated, may hold values from 0.5 to 1.5
- second_shift: float32 [768], replicated, may hold values from -3 to 3
- output_grad: bfloat16 [32768, 768], P('dp'), may hold values from -6 to 6
Outputs:
- layer_output: bfloat16 [32768, 768], P(('dp', 'tensor'))
- input_grad: float32 [32768, 768], P(('dp', 'tensor'))
- grad_query_weight: float32 [768, 768], P('dp', 'tensor')
- grad_query_bias: float32 [768], P('tensor')
- grad_key_weight: float32 [768, 768], P('dp', 'tensor')
- grad_value_weight: float32 [768, 768], P('dp', 'tensor')
- grad_value_bias: float32 [768], P('tensor')
- grad_output_weight: float32 [768, 768], P('tensor', 'dp')
- grad_output_bias: float32 [768], P(('dp', 'tensor'))
- grad_first_gain: float32 [768], P(('dp', 'tensor'))
- grad_first_shift: float32 [768], P(('dp', 'tensor'))
- grad_up_weight: float32 [768, 3072], P('dp', 'tensor')
- grad_up_bias: float32 [3072], P('tensor')
- grad_down_weight: float32 [3072, 768], P('tensor', 'dp')
- grad_down_bias: float32 [768], P(('dp', 'tensor'))
- grad_second_gain: float32 [768], P(('dp', 'tensor'))
- grad_second_shift: float32 [768], P(('dp', 'tensor'))
Inputs may be any that keep to these rules, and one draw needn't show every extreme that they name: `segments`: segment numbers restart in every packed row; a token attends exactly to the tokens of its own row that carry its segment number.
All inputs are finite; a program needn't handle non-finite values.
Results may differ from a plain program's by a relative error of at most 0.02.
The roundings to bfloat16 on the way count: a program that leaves them out, or rounds other values in their place, can miss the bound.
Values may be sent and summed in bfloat16 or wider, within the bound.
A program may use at most 256 MiB of HBM per device.

v0:
```python
import jax
import jax.numpy as jnp
from jax import lax
from jax.sharding import PartitionSpec as P

HEAD_DIM = 64


norm_eps = 1e-06


def product(left_side, right_side):
    return jnp.dot(left_side, right_side, preferred_element_type=jnp.float32)


def contract_rows(left_side, right_side):
    return lax.dot_general(
        left_side, right_side, (((0,), (0,)), ((), ())), preferred_element_type=jnp.float32
    )


def contract_last(left_side, right_side):
    return lax.dot_general(
        left_side, right_side, (((1,), (1,)), ((), ())), preferred_element_type=jnp.float32
    )


def normalize(summed, norm_gain, offset):
    centred = summed - jnp.mean(summed, -1, keepdims=True)
    inverse = lax.rsqrt(jnp.mean(centred * centred, -1, keepdims=True) + norm_eps)
    scaled = centred * inverse
    return (scaled * norm_gain + offset, scaled, inverse)


def normalize_back(grad_out, scaled, inverse, norm_gain):
    grad_scaled = grad_out * norm_gain
    mean_grad = jnp.mean(grad_scaled, -1, keepdims=True)
    mean_cross = jnp.mean(grad_scaled * scaled, -1, keepdims=True)
    return inverse * (grad_scaled - mean_grad - scaled * mean_cross)


def gelu_tanh(pre_act):
    return jax.nn.gelu(pre_act, approximate=True)


def score_block(query_block, key_row, query_segment, key_segment):
    scores = jnp.einsum(
        "qhd,khd->hqk", query_block, key_row, preferred_element_type=jnp.float32
    ) * HEAD_DIM ** (-0.5)
    linked = query_segment[:, None] == key_segment[None, :]
    return jnp.where(linked[None], scores, -1e30)


def attend(queries, key_side, value_proj, segments, block_rows):
    row_count, row_len = segments.shape
    head_count = queries.shape[1] // HEAD_DIM
    key_rows = key_side.reshape(row_count, row_len, head_count, HEAD_DIM)
    value_rows = value_proj.reshape(row_count, row_len, head_count, HEAD_DIM)
    block_count = row_count * row_len // block_rows
    query_blocks = queries.reshape(block_count, block_rows, head_count, HEAD_DIM)
    segment_blocks = segments.reshape(block_count, block_rows)
    row_ids = jnp.arange(block_count, dtype=jnp.int32) // (row_len // block_rows)

    def one_block(inputs):
        query_block, query_segment, row_id = inputs
        scores = score_block(query_block, key_rows[row_id], query_segment, segments[row_id])
        row_max = jnp.max(scores, -1, keepdims=True)
        exp_scores = jnp.exp(scores - row_max)
        row_total = jnp.sum(exp_scores, -1, keepdims=True)
        prob_low = (exp_scores / row_total).astype(jnp.bfloat16)
        context = jnp.einsum(
            "hqk,khd->qhd", prob_low, value_rows[row_id], preferred_element_type=jnp.float32
        )
        return (context.astype(jnp.bfloat16), (row_max + jnp.log(row_total))[..., 0])

    context, log_total = lax.map(one_block, (query_blocks, segment_blocks, row_ids))
    return (context.reshape(row_count * row_len, head_count * HEAD_DIM), log_total)


def attend_back(queries, key_side, value_proj, segments, log_total, grad_context, block_rows):
    row_count, row_len = segments.shape
    head_count = queries.shape[1] // HEAD_DIM
    local_width = head_count * HEAD_DIM
    key_rows = key_side.reshape(row_count, row_len, head_count, HEAD_DIM)
    value_rows = value_proj.reshape(row_count, row_len, head_count, HEAD_DIM)
    block_count = row_count * row_len // block_rows
    per_row = row_len // block_rows
    query_blocks = queries.reshape(block_count, block_rows, head_count, HEAD_DIM)
    grad_blocks = grad_context.reshape(block_count, block_rows, head_count, HEAD_DIM)
    segment_blocks = segments.reshape(block_count, block_rows)
    row_ids = jnp.arange(block_count, dtype=jnp.int32) // per_row

    def one_block(inputs):
        query_block, query_segment, row_id, log_block, grad_block = inputs
        scores = score_block(query_block, key_rows[row_id], query_segment, segments[row_id])
        probs_full = jnp.exp(scores - log_block[..., None])
        grad_probs = jnp.einsum(
            "qhd,khd->hqk", grad_block, value_rows[row_id], preferred_element_type=jnp.float32
        )
        inner_sum = jnp.sum(probs_full * grad_probs, -1, keepdims=True)
        grad_scores = (probs_full * (grad_probs - inner_sum)).astype(jnp.bfloat16)
        grad_query = jnp.einsum(
            "hqk,khd->qhd", grad_scores, key_rows[row_id], preferred_element_type=jnp.float32
        ) * HEAD_DIM ** (-0.5)
        grad_key = jnp.einsum(
            "hqk,qhd->khd", grad_scores, query_block, preferred_element_type=jnp.float32
        ) * HEAD_DIM ** (-0.5)
        grad_value = jnp.einsum(
            "hqk,qhd->khd",
            probs_full.astype(jnp.bfloat16),
            grad_block,
            preferred_element_type=jnp.float32,
        )
        return (grad_query, grad_key, grad_value)

    grad_query, grad_key, grad_value = lax.map(
        one_block, (query_blocks, segment_blocks, row_ids, log_total, grad_blocks)
    )
    grad_query = grad_query.reshape(row_count * row_len, local_width)
    grad_key = (
        grad_key.reshape(row_count, per_row, row_len, local_width)
        .sum(1)
        .reshape(row_count * row_len, local_width)
    )
    grad_value = (
        grad_value.reshape(row_count, per_row, row_len, local_width)
        .sum(1)
        .reshape(row_count * row_len, local_width)
    )
    return (grad_query, grad_key, grad_value)


def on_device(
    layer_input,
    segments,
    query_weight,
    query_bias,
    key_weight,
    value_weight,
    value_bias,
    output_weight,
    output_bias,
    first_gain,
    first_shift,
    up_weight,
    up_bias,
    down_weight,
    down_bias,
    second_gain,
    second_shift,
    output_grad,
):
    part_count = lax.axis_size("tensor")
    part_id = lax.axis_index("tensor")
    tok_count = layer_input.shape[0]
    share_rows = tok_count // part_count
    block_rows = min(512, segments.shape[1])

    def own_rows(full_array):
        return lax.dynamic_slice_in_dim(full_array, part_id * share_rows, share_rows, 0)

    input_f32 = layer_input.astype(jnp.float32)
    queries = (product(layer_input, query_weight) + query_bias).astype(jnp.bfloat16)
    key_side = product(layer_input, key_weight).astype(jnp.bfloat16)
    value_proj = (product(layer_input, value_weight) + value_bias).astype(jnp.bfloat16)
    context, log_total = attend(queries, key_side, value_proj, segments, block_rows)
    attn_total = lax.psum(product(context, output_weight).astype(jnp.bfloat16), "tensor").astype(
        jnp.float32
    )
    first_in = input_f32 + attn_total + output_bias
    first_out, first_unit, first_inv = normalize(first_in, first_gain, first_shift)
    first_low = first_out.astype(jnp.bfloat16)
    first_mine = own_rows(first_out)
    pre_act = product(first_low, up_weight) + up_bias
    gelu_out, pull_gelu = jax.vjp(gelu_tanh, pre_act)
    hidden_low = gelu_out.astype(jnp.bfloat16)
    down_mine = lax.psum_scatter(
        product(hidden_low, down_weight).astype(jnp.bfloat16),
        "tensor",
        scatter_dimension=0,
        tiled=True,
    ).astype(jnp.float32)
    second_in = first_mine + down_mine + down_bias
    second_out, second_unit, second_inv = normalize(second_in, second_gain, second_shift)
    layer_output = second_out.astype(jnp.bfloat16)
    grad_out_mine = own_rows(output_grad).astype(jnp.float32)
    grad_second = normalize_back(grad_out_mine, second_unit, second_inv, second_gain)
    grad_second_gain = jnp.sum(grad_out_mine * second_unit, 0)
    grad_second_shift = jnp.sum(grad_out_mine, 0)
    grad_down_bias = jnp.sum(grad_second, 0)
    down_low = lax.all_gather(grad_second.astype(jnp.bfloat16), "tensor", axis=0, tiled=True)
    grad_down_weight = contract_rows(hidden_low, down_low)
    grad_hidden = contract_last(down_low, down_weight)
    grad_pre = pull_gelu(grad_hidden)[0].astype(jnp.bfloat16)
    grad_up_weight = contract_rows(first_low, grad_pre)
    grad_up_bias = jnp.sum(grad_pre, 0, dtype=jnp.float32)
    up_back = contract_last(grad_pre, up_weight)
    mine_rows = own_rows(up_back) + grad_second
    first_grad = lax.psum(
        lax.dynamic_update_slice_in_dim(up_back, mine_rows, part_id * share_rows, 0).astype(
            jnp.bfloat16
        ),
        "tensor",
    ).astype(jnp.float32)
    attn_grad = normalize_back(first_grad, first_unit, first_inv, first_gain)
    attn_grad_low = attn_grad.astype(jnp.bfloat16)
    attn_grad_mine = own_rows(attn_grad)
    first_grad_mine = own_rows(first_grad)
    unit_mine = own_rows(first_unit)
    grad_first_gain = jnp.sum(first_grad_mine * unit_mine, 0)
    grad_first_shift = jnp.sum(first_grad_mine, 0)
    grad_output_bias = jnp.sum(attn_grad_mine, 0)
    grad_output_weight = contract_rows(context, attn_grad_low)
    grad_context = contract_last(attn_grad_low, output_weight).astype(jnp.bfloat16)
    grad_query, grad_key, grad_value = attend_back(
        queries, key_side, value_proj, segments, log_total, grad_context, block_rows
    )
    query_low = grad_query.astype(jnp.bfloat16)
    key_low = grad_key.astype(jnp.bfloat16)
    value_low = grad_value.astype(jnp.bfloat16)
    grad_query_weight = contract_rows(layer_input, query_low)
    grad_key_weight = contract_rows(layer_input, key_low)
    grad_value_weight = contract_rows(layer_input, value_low)
    grad_query_bias = jnp.sum(query_low, 0, dtype=jnp.float32)
    grad_value_bias = jnp.sum(value_low, 0, dtype=jnp.float32)
    total = contract_last(query_low, query_weight)
    total = total + contract_last(key_low, key_weight)
    input_grad = (
        lax.psum_scatter(
            (total + contract_last(value_low, value_weight)).astype(jnp.bfloat16),
            "tensor",
            scatter_dimension=0,
            tiled=True,
        ).astype(jnp.float32)
        + attn_grad_mine
    )
    summed_weights = (
        lax.psum_scatter(grad_query_weight, "dp", scatter_dimension=0, tiled=True),
        lax.psum_scatter(grad_key_weight, "dp", scatter_dimension=0, tiled=True),
        lax.psum_scatter(grad_value_weight, "dp", scatter_dimension=0, tiled=True),
        lax.psum_scatter(grad_up_weight, "dp", scatter_dimension=0, tiled=True),
        lax.psum_scatter(grad_output_weight, "dp", scatter_dimension=1, tiled=True),
        lax.psum_scatter(grad_down_weight, "dp", scatter_dimension=1, tiled=True),
    )
    summed_shared = (
        lax.psum_scatter(grad_output_bias, ("dp", "tensor"), scatter_dimension=0, tiled=True),
        lax.psum_scatter(grad_first_gain, ("dp", "tensor"), scatter_dimension=0, tiled=True),
        lax.psum_scatter(grad_first_shift, ("dp", "tensor"), scatter_dimension=0, tiled=True),
        lax.psum_scatter(grad_down_bias, ("dp", "tensor"), scatter_dimension=0, tiled=True),
        lax.psum_scatter(grad_second_gain, ("dp", "tensor"), scatter_dimension=0, tiled=True),
        lax.psum_scatter(grad_second_shift, ("dp", "tensor"), scatter_dimension=0, tiled=True),
    )
    summed_biases = lax.psum((grad_query_bias, grad_value_bias, grad_up_bias), "dp")
    return (
        layer_output,
        input_grad,
        summed_weights[0],
        summed_biases[0],
        summed_weights[1],
        summed_weights[2],
        summed_biases[1],
        summed_weights[4],
        summed_shared[0],
        summed_shared[1],
        summed_shared[2],
        summed_weights[3],
        summed_biases[2],
        summed_weights[5],
        summed_shared[3],
        summed_shared[4],
        summed_shared[5],
    )


def solution(mesh):
    in_specs = (
        P("dp", None),
        P("dp", None),
        P(None, "tensor"),
        P("tensor"),
        P(None, "tensor"),
        P(None, "tensor"),
        P("tensor"),
        P("tensor", None),
        P(),
        P(),
        P(),
        P(None, "tensor"),
        P("tensor"),
        P("tensor", None),
        P(),
        P(),
        P(),
        P("dp", None),
    )
    out_specs = (
        P(("dp", "tensor"), None),
        P(("dp", "tensor"), None),
        P("dp", "tensor"),
        P("tensor"),
        P("dp", "tensor"),
        P("dp", "tensor"),
        P("tensor"),
        P("tensor", "dp"),
        P(("dp", "tensor")),
        P(("dp", "tensor")),
        P(("dp", "tensor")),
        P("dp", "tensor"),
        P("tensor"),
        P("tensor", "dp"),
        P(("dp", "tensor")),
        P(("dp", "tensor")),
        P(("dp", "tensor")),
    )
    return jax.shard_map(
        on_device, mesh=mesh, in_specs=in_specs, out_specs=out_specs, check_vma=False
    )
```

profile of v0, /device:TPU:0, one launch (start us, length us, event | category | flops | bytes accessed | tf_op | source)
XLA Modules:
  0.0 1443.5 jit_solution(3081273717691375530)
XLA Ops:
  8.2 5.2 fusion.63
  33.0 86.0 %while.26 = (s32[]{:T(128)}, bf16[8,512,3,64]{1,3,2,0:T(8,128)(2,1)}, f32[8,3,512]{2,1,0:T(4,128)S(1)}, s32[8]{0:T(128)S(1)}, bf16[4,1024,3,64]{1,3,2,0:T(8,128)...) while((s32[]{:T(128)}, ...), condition=%wide.region_3.4_spmd, body=%wide.region_0.3_spmd.sunk | while | flops 422148608 | bytes 22225096 | solution.py:76
  128.5 225.4 %all-reduce.11.cloned.1.call-done = bf16[4096,768]{1,0:T(8,128)(2,1)} async-done(((bf16[4096,768]{1,0:T(8,128)(2,1)}), bf16[4096,768]{1,0:T(8,128)(2,1)}) %all-reduce.11.cloned.1.call-update) | async-done | bytes 6291472 | tf_op jit(solution)/shard_map/psum | solution.py:167
  353.9 6.9 fusion.61
  360.8 6.1 multiply_reduce_fusion.2
  367.0 6.1 multiply_add_fusion
  373.1 11.8 multiply_convert_fusion.1
  384.9 9.7 convolution_convert_fusion.1
  395.1 109.4 %reduce-scatter.17.cloned.1.call-done = bf16[1024,768]{1,0:T(8,128)(2,1)} async-done(((bf16[4096,768]{1,0:T(8,128)(2,1)}), bf16[1024,768]{1,0:T(8,128)(2,1)}) %reduce-scatter.17.cloned.1.call-update) | async-done | bytes 1572880 | tf_op jit(solution)/shard_map/reduce_scatter | solution.py:177
  518.2 116.0 %all-gather.2.cloned.1.call-done = bf16[4096,768]{1,0:T(8,128)(2,1)} async-done(((bf16[1024,768]{1,0:T(8,128)(2,1)}), bf16[4096,768]{1,0:T(8,128)(2,1)}) %all-gather.2.cloned.1.call-update) | async-done | bytes 6291472 | tf_op jit(solution)/shard_map/all_gather | solution.py:191
  634.2 16.9 %convert_reduce_fusion = (f32[768]{0:T(1024)}, bf16[4096,768]{1,0:T(8,128)(2,1)S(1)}) fusion(f32[4096,768]{1,0:T(8,128)} %get-tuple-element.361, f32[768]{0:T(1024)S(1)} %copy-done.34, bf16[4096,768]{1,0:T(8,128)(2,1)} %all-gather.2.cloned.1.call-done, bf16[768,768]{1,0:T(8,128)(2,1)S(1)} %copy-done.33), kind=kOutput, calls=%fused_computation.74 | convolution fusion | flops 4904188928 | bytes 26351616 | tf_op jit(solution)/shard_map/dot_general | solution.py:23
  651.2 8.3 fusion.85
  663.8 7.8 convert_element_type.120
  671.8 220.9 %all-reduce.13.cloned.1.call-done = bf16[4096,768]{1,0:T(8,128)(2,1)} async-done(((bf16[4096,768]{1,0:T(8,128)(2,1)}), bf16[4096,768]{1,0:T(8,128)(2,1)}) %all-reduce.13.cloned.1.call-update) | async-done | bytes 6291472 | tf_op jit(solution)/shard_map/psum | solution.py:199
  892.7 8.8 multiply_reduce_fusion.3
  901.5 7.9 subtract_multiply_fusion
  917.4 7.9 convolution_convert_fusion.2
  929.5 147.2 %while.27 = (s32[]{:T(128)}, bf16[8,512,3,64]{1,3,2,0:T(8,128)(2,1)}, f32[8,1024,3,64]{1,3,2,0:T(8,128)}, f32[8,1024,3,64]{1,3,2,0:T(8,128)}, s32[8]{0:T(128)S(1...) while((s32[]{:T(128)}, ...), condition=%wide.region_17.18_spmd, body=%wide.region_15.17_spmd.sunk | while | flops 1031043584 | bytes 53278952 | solution.py:116
  1080.6 5.1 reduce_sum.199
  1091.0 6.4 fusion.87
  1097.4 6.3 fusion.86
  1103.7 12.8 add_convert_fusion
  1116.7 11.4 fusion.74
  1128.1 10.1 fusion.88
  1157.8 8.3 convert_element_type.121
  1166.4 15.1 %all-reduce.7 = (f32[192]{0:T(256)}, f32[192]{0:T(256)}, f32[768]{0:T(1024)}) all-reduce(f32[192]{0:T(256)S(1)} %reduce_sum.202, f32[192]{0:T(256)S(1)} %convert_reduce_fusion.2, f32[768]{0:T(1024)S(1)} %copy-done.32), channel_id=1, replica_groups=mesh['dp'=8,'tensor'=4] {'dp'}, use_global_device_ids=true, to_apply=%region_23.24 | all-reduce | flops 1152 | bytes 9216 | tf_op jit(solution)/shard_map/psum | solution.py:253
  1186.4 40.1 %reduce-scatter.19.cloned.1.call-done = bf16[1024,768]{1,0:T(8,128)(2,1)} async-done(((bf16[4096,768]{1,0:T(8,128)(2,1)}), bf16[1024,768]{1,0:T(8,128)(2,1)}) %reduce-scatter.19.cloned.1.call-update) | async-done | bytes 1572880 | tf_op jit(solution)/shard_map/reduce_scatter | solution.py:229
  1230.9 41.2 %all-reduce.6 = (f32[768]{0:T(1024)S(1)}, f32[768]{0:T(1024)S(1)}, f32[768]{0:T(1024)S(1)}, f32[768]{0:T(1024)S(1)}, f32[768]{0:T(1024)S(1)}, /*index=5*/f32[768]{0:T(1024)S(1)}) all-reduce(f32[768]{0:T(1024)S(1)} %get-tuple-element.357, f32[768]{0:T(1024)S(1)} %get-tuple-element.287, ...), channel_id=8, replica_groups=mesh['dp'=8,'tensor'=4] {'dp','tensor'}, use_global_device_ids=true, to_apply=%region_30.31.clone | all-reduce | flops 4608 | bytes 36864
  1275.6 45.1 %reduce-scatter.23.cloned.1.call-done = f32[768,96]{0,1:T(8,128)} async-done(((f32[768,768]{0,1:T(8,128)}), f32[768,96]{0,1:T(8,128)}) %reduce-scatter.23.cloned.1.call-update) | async-done | bytes 294928 | tf_op jit(solution)/shard_map/reduce_scatter | solution.py:243
  1320.7 38.7 %reduce-scatter.25.cloned.1.call-done = f32[96,192]{1,0:T(8,128)} async-done(((f32[768,192]{1,0:T(8,128)}), f32[96,192]{1,0:T(8,128)}) %reduce-scatter.25.cloned.1.call-update) | async-done | bytes 73744
  1359.4 38.6 %reduce-scatter.27.cloned.1.call-done = f32[96,192]{1,0:T(8,128)} async-done(((f32[768,192]{1,0:T(8,128)}), f32[96,192]{1,0:T(8,128)}) %reduce-scatter.27.cloned.1.call-update) | async-done | bytes 73744
  1398.0 38.7 %reduce-scatter.29.cloned.1.call-done = f32[96,192]{1,0:T(8,128)} async-done(((f32[768,192]{1,0:T(8,128)}), f32[96,192]{1,0:T(8,128)}) %reduce-scatter.29.cloned.1.call-update) | async-done | bytes 73744
  (315 shorter events, 303.9 us)
Async XLA Ops:
  7.2 365.9 %copy-start = (bf16[768,768]{1,0:T(8,128)(2,1)S(1)}, bf16[768,768]{1,0:T(8,128)(2,1)}, u32[]{:S(2)}) copy-start(bf16[768,768]{1,0:T(8,128)(2,1)} %param.33) | copy-start | bytes 3538948
  7.2 346.7 %all-reduce.11.cloned.1.call-start = ((), (), s32[]{:S(2)}) async-start(), calls=%async_computation.8 | async-start | bytes 12582912 | tf_op jit(solution)/shard_map/psum | solution.py:167
  7.3 8.5 slice-start
  23.8 9.2 copy-start.22
  119.0 9.2 copy-start.6
  123.6 230.3 %copy-start.23 = (f32[768]{0:T(1024)S(1)}, f32[768]{0:T(1024)}, u32[]{:S(2)}) copy-start(f32[768]{0:T(1024)} %param.30) | copy-start | bytes 9220
  128.2 376.2 %reduce-scatter.17.cloned.1.call-start = ((), (), s32[]{:S(2)}) async-start(), calls=%async_computation.9 | async-start | bytes 7864320 | tf_op jit(solution)/shard_map/reduce_scatter | solution.py:177
  353.9 13.0 slice-start.2
  373.1 11.8 copy-start.3
  373.1 11.8 copy-start.33
  394.6 109.9 %copy-start.31 = (f32[768]{0:T(1024)S(1)}, f32[768]{0:T(1024)}, u32[]{:S(2)}) copy-start(f32[768]{0:T(1024)} %param.36) | copy-start | bytes 9220
  394.6 113.2 %copy-start.26 = (f32[768]{0:T(1024)S(1)}, f32[768]{0:T(1024)}, u32[]{:S(2)}) copy-start(f32[768]{0:T(1024)} %param.37) | copy-start | bytes 9220
  394.6 239.6 %all-gather.2.cloned.1.call-start = ((), (), s32[]{:S(2)}) async-start(), calls=%async_computation.10 | async-start | bytes 7864320 | tf_op jit(solution)/shard_map/all_gather | solution.py:191
  395.1 116.2 %copy-start.29 = (f32[768]{0:T(1024)S(1)}, f32[768]{0:T(1024)}, u32[]{:S(2)}) copy-start(f32[768]{0:T(1024)} %param.38) | copy-start | bytes 9220
  518.2 374.5 %all-reduce.13.cloned.1.call-start = ((), (), s32[]{:S(2)}) async-start(), calls=%async_computation.11 | async-start | bytes 12582912 | tf_op jit(solution)/shard_map/psum | solution.py:199
  651.2 8.3 copy-start.10
  651.2 8.3 copy-start.9
  671.5 513.2 %reduce-scatter.31.cloned.1.call-start = ((), (), s32[]{:S(2)}) async-start(), calls=%async_computation.18 | async-start | bytes 884736
  901.5 12.5 copy-start.12
  925.4 301.1 %reduce-scatter.19.cloned.1.call-start = ((), (), s32[]{:S(2)}) async-start(), calls=%async_computation.12 | async-start | bytes 7864320 | tf_op jit(solution)/shard_map/reduce_scatter | solution.py:229
  1087.3 10.1 copy-start.13
  1091.0 12.7 copy-start.15
  1116.6 159.0 %reduce-scatter.21.cloned.1.call-start = ((), (), s32[]{:S(2)}) async-start(), calls=%async_computation.13 | async-start | bytes 2654208 | tf_op jit(solution)/shard_map/reduce_scatter | solution.py:241
  1128.1 192.6 %reduce-scatter.23.cloned.1.call-start = ((), (), s32[]{:S(2)}) async-start(), calls=%async_computation.14 | async-start | bytes 2654208 | tf_op jit(solution)/shard_map/reduce_scatter | solution.py:243
  1138.2 221.2 %reduce-scatter.25.cloned.1.call-start = ((), (), s32[]{:S(2)}) async-start(), calls=%async_computation.15 | async-start | bytes 884736
  1144.1 253.9 %reduce-scatter.27.cloned.1.call-start = ((), (), s32[]{:S(2)}) async-start(), calls=%async_computation.16 | async-start | bytes 884736
  1150.0 286.7 %reduce-scatter.29.cloned.1.call-start = ((), (), s32[]{:S(2)}) async-start(), calls=%async_computation.17 | async-start | bytes 884736
  1157.8 8.6 copy-start.32
  1166.4 270.4 %copy-start.1 = (bf16[768,768]{1,0:T(8,128)(2,1)S(1)}, bf16[768,768]{1,0:T(8,128)(2,1)}, u32[]{:S(2)}) copy-start(bf16[768,768]{1,0:T(8,128)(2,1)} %param.33) | copy-start | bytes 3538948
  1181.5 49.4 %copy-start.25 = (f32[768]{0:T(1024)S(1)}, f32[768]{0:T(1024)}, u32[]{:S(2)}) copy-start(f32[768]{0:T(1024)} %get-tuple-element.345) | copy-start | bytes 9220
  1181.5 49.4 %copy-start.27 = (f32[768]{0:T(1024)S(1)}, f32[768]{0:T(1024)}, u32[]{:S(2)}) copy-start(f32[768]{0:T(1024)} %get-tuple-element.288) | copy-start | bytes 9220
  1181.5 49.4 %copy-start.28 = (f32[768]{0:T(1024)S(1)}, f32[768]{0:T(1024)}, u32[]{:S(2)}) copy-start(f32[768]{0:T(1024)} %get-tuple-element.293) | copy-start | bytes 9220
  (19 other events, 105.8 us)
Sparse Core Ops, SparseCore 0:
  128.3 225.5 all-reduce.10
  394.7 109.6 reduce-scatter.16
  518.3 115.8 all-gather.1
  671.7 220.9 all-reduce.12
  925.5 33.9 reduce-scatter.30
  1116.7 109.7 reduce-scatter.18
  1230.4 43.4 reduce-scatter.20
  1278.2 42.4 reduce-scatter.22
  1324.4 34.9 reduce-scatter.24
  1363.0 34.9 reduce-scatter.26
  1401.7 34.9 reduce-scatter.28
where the time goes:
time: 1450 us; the launch traced here: 1440 us
  waiting for transfers between devices  873 us (60%)
  matrix products  294 us (20%)
  other arithmetic  121 us (8%)
  blocking collectives  56.3 us (4%)
  local copies, waits for them, and re-layouts  50.7 us (3%)
  loops' own time  32.2 us (2%)
  between operations  14.6 us (1%)
    psum x1, waiting for transfers between devices, on_device(): lax.psum(product(context, output_weight).astype(jnp.bfloat16), 'tensor')  225 us
    psum x1, waiting for transfers between devices, on_device(): lax.psum(lax.dynamic_update_slice_in_dim(up_back, mine_rows, part_id * sh...  221 us
    unnamed x15, waiting for transfers between devices  116 us
    all_gather x1, waiting for transfers between devices, on_device(): lax.all_gather(grad_second.astype(jnp.bfloat16), 'tensor', axis=0, tiled=...  116 us
    reduce_scatter x1, waiting for transfers between devices, on_device(): lax.psum_scatter(product(hidden_low, down_weight).astype(jnp.bfloat16), '...  109 us
    dot_general x6, matrix products, contract_last(): lax.dot_general(left_side, right_side, (((1,), (1,)), ((), ())), preferre...  58.7 us
    reduce_scatter x1, waiting for transfers between devices, on_device(): lax.psum_scatter(grad_down_weight, 'dp', scatter_dimension=1, tiled=True)  45.1 us
    unnamed x1, blocking collectives  41.2 us
  transfers between devices with their start and end apart: 11, of which 9 were waited for; matrix products, arithmetic and copies ran while one was open for 16% of the time, Pallas kernels for 0%

commit v1 on v0

v1 whole, which is shorter than its diff:
```python
import jax
import jax.numpy as jnp
from jax import lax
from jax.sharding import PartitionSpec as P

HEAD_DIM = 64
GROUP_HEADS = 3

norm_eps = 1e-06


def product(left_side, right_side):
    return jnp.dot(left_side, right_side, preferred_element_type=jnp.float32)


def contract_rows(left_side, right_side):
    return lax.dot_general(
        left_side, right_side, (((0,), (0,)), ((), ())), preferred_element_type=jnp.float32
    )


def contract_last(left_side, right_side):
    return lax.dot_general(
        left_side, right_side, (((1,), (1,)), ((), ())), preferred_element_type=jnp.float32
    )


def normalize(summed, norm_gain, offset):
    centred = summed - jnp.mean(summed, -1, keepdims=True)
    inverse = lax.rsqrt(jnp.mean(centred * centred, -1, keepdims=True) + norm_eps)
    scaled = centred * inverse
    return (scaled * norm_gain + offset, scaled, inverse)


def normalize_back(grad_out, scaled, inverse, norm_gain):
    grad_scaled = grad_out * norm_gain
    mean_grad = jnp.mean(grad_scaled, -1, keepdims=True)
    mean_cross = jnp.mean(grad_scaled * scaled, -1, keepdims=True)
    return inverse * (grad_scaled - mean_grad - scaled * mean_cross)


def gelu_tanh(pre_act):
    return jax.nn.gelu(pre_act, approximate=True)


def score_group(query_group, key_group, segment_row):
    scores = jnp.einsum(
        "qhd,khd->hqk", query_group, key_group, preferred_element_type=jnp.float32
    ) * HEAD_DIM ** (-0.5)
    linked = segment_row[:, None] == segment_row[None, :]
    return jnp.where(linked[None], scores, -1e30)


def split_groups(rows_by_width):
    length, width = rows_by_width.shape
    groups = width // (GROUP_HEADS * HEAD_DIM)
    return rows_by_width.reshape(length, groups, GROUP_HEADS, HEAD_DIM).transpose(1, 0, 2, 3)


def join_groups(grouped):
    groups, length, heads, dim = grouped.shape
    return grouped.transpose(1, 0, 2, 3).reshape(length, groups * heads * dim)


def attend(queries, key_side, value_proj, segment_row):
    def one_group(inputs):
        query_group, key_group, value_group = inputs
        scores = score_group(query_group, key_group, segment_row)
        row_max = jnp.max(scores, -1, keepdims=True)
        exp_scores = jnp.exp(scores - row_max)
        row_total = jnp.sum(exp_scores, -1, keepdims=True)
        prob_low = (exp_scores / row_total).astype(jnp.bfloat16)
        context = jnp.einsum(
            "hqk,khd->qhd", prob_low, value_group, preferred_element_type=jnp.float32
        )
        return (context.astype(jnp.bfloat16), (row_max + jnp.log(row_total))[..., 0])

    context, log_total = lax.map(
        one_group, (split_groups(queries), split_groups(key_side), split_groups(value_proj))
    )
    return (join_groups(context), log_total)


def attend_back(queries, key_side, value_proj, segment_row, log_total, grad_context):
    def one_group(inputs):
        query_group, key_group, value_group, log_group, grad_group = inputs
        scores = score_group(query_group, key_group, segment_row)
        probs_full = jnp.exp(scores - log_group[..., None])
        grad_probs = jnp.einsum(
            "qhd,khd->hqk", grad_group, value_group, preferred_element_type=jnp.float32
        )
        inner_sum = jnp.sum(probs_full * grad_probs, -1, keepdims=True)
        grad_scores = (probs_full * (grad_probs - inner_sum)).astype(jnp.bfloat16)
        grad_query = jnp.einsum(
            "hqk,khd->qhd", grad_scores, key_group, preferred_element_type=jnp.float32
        ) * HEAD_DIM ** (-0.5)
        grad_key = jnp.einsum(
            "hqk,qhd->khd", grad_scores, query_group, preferred_element_type=jnp.float32
        ) * HEAD_DIM ** (-0.5)
        grad_value = jnp.einsum(
            "hqk,qhd->khd",
            probs_full.astype(jnp.bfloat16),
            grad_group,
            preferred_element_type=jnp.float32,
        )
        return (
            grad_query.astype(jnp.bfloat16),
            grad_key.astype(jnp.bfloat16),
            grad_value.astype(jnp.bfloat16),
        )

    grad_query, grad_key, grad_value = lax.map(
        one_group,
        (
            split_groups(queries),
            split_groups(key_side),
            split_groups(value_proj),
            log_total,
            split_groups(grad_context),
        ),
    )
    return (join_groups(grad_query), join_groups(grad_key), join_groups(grad_value))


def gather_shards(pieces):
    flat = jnp.concatenate([piece.reshape(-1) for piece in pieces])
    dp_count = lax.axis_size("dp")
    core = lax.rem(lax.axis_index("dp"), 2)
    half = flat.shape[0] // 2
    mine = lax.dynamic_slice_in_dim(flat, core * half, half, 0)
    gathered = lax.all_gather(mine, "tensor", axis=0, tiled=False)
    other = lax.ppermute(gathered, "dp", perm=[(i, i ^ 1) for i in range(dp_count)])
    both = jnp.where(
        core == 0,
        jnp.concatenate([gathered, other], axis=1),
        jnp.concatenate([other, gathered], axis=1),
    )
    shards = []
    start = 0
    for piece in pieces:
        size = piece.size
        shards.append(both[:, start : start + size].reshape((both.shape[0],) + piece.shape))
        start += size
    return shards


def join_columns(shards):
    count, rows, cols = shards.shape
    return shards.transpose(1, 0, 2).reshape(rows, count * cols)


def join_rows(shards):
    count, rows, cols = shards.shape
    return shards.reshape(count * rows, cols)


def scatter_blocks(full, row_axis, col_axis):
    row_parts = lax.axis_size(row_axis)
    col_parts = lax.axis_size(col_axis)
    rows, cols = full.shape
    blocks = full.reshape(row_parts, rows // row_parts, col_parts, cols // col_parts)
    if row_axis == "dp":
        blocks = blocks.transpose(0, 2, 1, 3)
    else:
        blocks = blocks.transpose(2, 0, 1, 3)
    blocks = blocks.reshape(row_parts * col_parts * (rows // row_parts), cols // col_parts)
    return lax.psum_scatter(blocks, ("dp", "tensor"), scatter_dimension=0, tiled=True)


def on_device(
    layer_input,
    segments,
    query_weight,
    query_bias,
    key_weight,
    value_weight,
    value_bias,
    output_weight,
    output_bias,
    first_gain,
    first_shift,
    up_weight,
    up_bias,
    down_weight,
    down_bias,
    second_gain,
    second_shift,
    output_grad,
):
    part_count = lax.axis_size("tensor")
    part_id = lax.axis_index("tensor")
    row_len = segments.shape[1]
    dp_count = lax.axis_size("dp")

    input_rows = lax.dynamic_slice_in_dim(layer_input, part_id * row_len, row_len, 0)
    segment_row = lax.dynamic_index_in_dim(segments, part_id, 0, keepdims=False)
    grad_out = lax.dynamic_slice_in_dim(output_grad, part_id * row_len, row_len, 0).astype(
        jnp.float32
    )

    q_sh, k_sh, v_sh, o_sh = gather_shards([query_weight, key_weight, value_weight, output_weight])
    u_sh, d_sh = gather_shards([up_weight, down_weight])
    bias_sh = lax.all_gather(
        jnp.concatenate([query_bias, value_bias, up_bias]), "tensor", axis=0, tiled=False
    )
    qw = join_columns(q_sh)
    kw = join_columns(k_sh)
    vw = join_columns(v_sh)
    ow = join_rows(o_sh)
    uw = join_columns(u_sh)
    dw = join_rows(d_sh)
    head_width = query_bias.shape[0]
    qb = bias_sh[:, :head_width].reshape(-1)
    vb = bias_sh[:, head_width : 2 * head_width].reshape(-1)
    ub = bias_sh[:, 2 * head_width :].reshape(-1)

    input_f32 = input_rows.astype(jnp.float32)
    queries = (product(input_rows, qw) + qb).astype(jnp.bfloat16)
    key_side = product(input_rows, kw).astype(jnp.bfloat16)
    value_proj = (product(input_rows, vw) + vb).astype(jnp.bfloat16)
    context, log_total = attend(queries, key_side, value_proj, segment_row)

    group_width = ow.shape[0] // part_count
    attn_total = input_f32
    for member in range(part_count):
        cols = slice(member * group_width, (member + 1) * group_width)
        attn_total = attn_total + product(context[:, cols], ow[cols]).astype(
            jnp.bfloat16
        ).astype(jnp.float32)
    first_in = attn_total + output_bias
    first_out, first_unit, first_inv = normalize(first_in, first_gain, first_shift)
    first_low = first_out.astype(jnp.bfloat16)
    pre_act = product(first_low, uw) + ub
    gelu_out, pull_gelu = jax.vjp(gelu_tanh, pre_act)
    hidden_low = gelu_out.astype(jnp.bfloat16)
    unit_width = dw.shape[0] // part_count
    second_in = first_out
    for member in range(part_count):
        units = slice(member * unit_width, (member + 1) * unit_width)
        second_in = second_in + product(hidden_low[:, units], dw[units]).astype(
            jnp.bfloat16
        ).astype(jnp.float32)
    second_in = second_in + down_bias
    second_out, second_unit, second_inv = normalize(second_in, second_gain, second_shift)
    layer_output = second_out.astype(jnp.bfloat16)

    grad_second = normalize_back(grad_out, second_unit, second_inv, second_gain)
    grad_second_gain = jnp.sum(grad_out * second_unit, 0)
    grad_second_shift = jnp.sum(grad_out, 0)
    grad_down_bias = jnp.sum(grad_second, 0)
    down_low = grad_second.astype(jnp.bfloat16)
    grad_down_weight = contract_rows(hidden_low, down_low)
    grad_hidden = contract_last(down_low, dw)
    grad_pre = pull_gelu(grad_hidden)[0].astype(jnp.bfloat16)
    grad_up_weight = contract_rows(first_low, grad_pre)
    grad_up_bias = jnp.sum(grad_pre, 0, dtype=jnp.float32)
    first_grad = contract_last(grad_pre, uw) + grad_second
    grad_first_gain = jnp.sum(first_grad * first_unit, 0)
    grad_first_shift = jnp.sum(first_grad, 0)
    attn_grad = normalize_back(first_grad, first_unit, first_inv, first_gain)
    grad_output_bias = jnp.sum(attn_grad, 0)
    attn_grad_low = attn_grad.astype(jnp.bfloat16)
    grad_output_weight = contract_rows(context, attn_grad_low)
    grad_context = contract_last(attn_grad_low, ow).astype(jnp.bfloat16)
    query_low, key_low, value_low = attend_back(
        queries, key_side, value_proj, segment_row, log_total, grad_context
    )
    grad_query_weight = contract_rows(input_rows, query_low)
    grad_key_weight = contract_rows(input_rows, key_low)
    grad_value_weight = contract_rows(input_rows, value_low)
    grad_query_bias = jnp.sum(query_low, 0, dtype=jnp.float32)
    grad_value_bias = jnp.sum(value_low, 0, dtype=jnp.float32)
    input_grad = (
        attn_grad
        + contract_last(query_low, qw)
        + contract_last(key_low, kw)
        + contract_last(value_low, vw)
    )

    summed_weights = (
        scatter_blocks(grad_query_weight, "dp", "tensor"),
        scatter_blocks(grad_key_weight, "dp", "tensor"),
        scatter_blocks(grad_value_weight, "dp", "tensor"),
        scatter_blocks(grad_output_weight, "tensor", "dp"),
        scatter_blocks(grad_up_weight, "dp", "tensor"),
        scatter_blocks(grad_down_weight, "tensor", "dp"),
    )
    shared = jnp.stack(
        [
            grad_output_bias,
            grad_first_gain,
            grad_first_shift,
            grad_down_bias,
            grad_second_gain,
            grad_second_shift,
        ]
    )
    shared_parts = dp_count * part_count
    shared = shared.reshape(6, shared_parts, -1).transpose(1, 0, 2)
    shared = lax.psum_scatter(shared, ("dp", "tensor"), scatter_dimension=0, tiled=True)[0]
    split = jnp.concatenate(
        [
            grad_query_bias.reshape(part_count, -1),
            grad_value_bias.reshape(part_count, -1),
            grad_up_bias.reshape(part_count, -1),
        ],
        axis=1,
    )
    split = lax.psum(
        lax.psum_scatter(split, "tensor", scatter_dimension=0, tiled=True)[0], "dp"
    )
    return (
        layer_output,
        input_grad,
        summed_weights[0],
        split[:head_width],
        summed_weights[1],
        summed_weights[2],
        split[head_width : 2 * head_width],
        summed_weights[3],
        shared[0],
        shared[1],
        shared[2],
        summed_weights[4],
        split[2 * head_width :],
        summed_weights[5],
        shared[3],
        shared[4],
        shared[5],
    )


def solution(mesh):
    in_specs = (
        P("dp", None),
        P("dp", None),
        P(None, "tensor"),
        P("tensor"),
        P(None, "tensor"),
        P(None, "tensor"),
        P("tensor"),
        P("tensor", None),
        P(),
        P(),
        P(),
        P(None, "tensor"),
        P("tensor"),
        P("tensor", None),
        P(),
        P(),
        P(),
        P("dp", None),
    )
    out_specs = (
        P(("dp", "tensor"), None),
        P(("dp", "tensor"), None),
        P("dp", "tensor"),
        P("tensor"),
        P("dp", "tensor"),
        P("dp", "tensor"),
        P("tensor"),
        P("tensor", "dp"),
        P(("dp", "tensor")),
        P(("dp", "tensor")),
        P(("dp", "tensor")),
        P("dp", "tensor"),
        P("tensor"),
        P("tensor", "dp"),
        P(("dp", "tensor")),
        P(("dp", "tensor")),
        P(("dp", "tensor")),
    )
    return jax.shard_map(
        on_device, mesh=mesh, in_specs=in_specs, out_specs=out_specs, check_vma=False
    )
```

time: 1450 us -> 1200 us (0.83)
  waiting for transfers between devices: 873 us -> 465 us
  local copies, waits for them, and re-layouts: 50.7 us -> 220 us
  matrix products: 294 us -> 247 us
  other arithmetic: 121 us -> 158 us
  loops' own time: 32.2 us -> 0.7 us
  blocking collectives: 56.3 us -> 80.9 us
    psum x2 -> x0, waiting for transfers between devices: 446 us -> none  [the longest x1 225 us: on_device(): lax.psum(product(context, output_weight).astype(jnp.bfloat16), 'tensor')]
    reduce_scatter x4 -> x5, waiting for transfers between devices: 195 us -> 415 us  [scatter_blocks(): lax.psum_scatter(blocks, ('dp', 'tensor'), scatter_dimension=0, tiled=True)]
    unnamed x15 -> x9, waiting for transfers between devices: 116 us -> 0.13 us
    select_n x1 -> x2, other arithmetic: 0.01 us -> 89.7 us  [gather_shards(): jnp.where(core == 0, jnp.concatenate([gathered, other], axis=1), jnp.conc...]
    slice x0 -> x16, local copies, waits for them, and re-layouts: none -> 67.5 us  [the longest x5 42.3 us: on_device(): dw[units]]
    all_gather x1 -> x2, waiting for transfers between devices: 116 us -> 50 us  [gather_shards(): gathered = lax.all_gather(mine, 'tensor', axis=0, tiled=False)]
    reshape x3 -> x15, local copies, waits for them, and re-layouts: 6.28 us -> 50.7 us  [the longest x2 25.1 us: scatter_blocks(): full.reshape(row_parts, rows // row_parts, col_parts, cols // col_parts)]
    another operation x2, loops' own time: 32.2 us -> 0.7 us  [the longest x1 0.38 us: attend_back(): lax.map(one_group, (split_groups(queries), split_groups(key_side), split_...]
  transfers between devices with their start and end apart: 11 -> 10, of which waited for: 9 -> 6; matrix products, arithmetic and copies ran while one was open for 16% -> 34% of each run, Pallas kernels for 0% -> 0%
where the time goes in v1:
time: 1200 us; the launch traced here: 1190 us
  waiting for transfers between devices  465 us (39%)
  matrix products  247 us (21%)
  local copies, waits for them, and re-layouts  220 us (18%)
  other arithmetic  158 us (13%)
  blocking collectives  80.9 us (7%)
  between operations  15.6 us (1%)
    reduce_scatter x5, waiting for transfers between devices, scatter_blocks(): lax.psum_scatter(blocks, ('dp', 'tensor'), scatter_dimension=0, tiled=True)  415 us
    select_n x2, other arithmetic, gather_shards(): jnp.where(core == 0, jnp.concatenate([gathered, other], axis=1), jnp.conc...  89.7 us
    unnamed x2, blocking collectives  55.2 us
    all_gather x2, waiting for transfers between devices, gather_shards(): gathered = lax.all_gather(mine, 'tensor', axis=0, tiled=False)  50 us
    dot_general x12, matrix products, product(): return jnp.dot(left_side, right_side, preferred_element_type=jnp.float32)  43.9 us
    slice x5, local copies, waits for them, and re-layouts, on_device(): dw[units]  42.3 us
    dot_general x6, matrix products, contract_last(): lax.dot_general(left_side, right_side, (((1,), (1,)), ((), ())), preferre...  40.6 us
    unnamed x150, local copies, waits for them, and re-layouts  39.8 us
  transfers between devices with their start and end apart: 10, of which 6 were waited for; matrix products, arithmetic and copies ran while one was open for 34% of the time, Pallas kernels for 0%

profile of v1, /device:TPU:0, one launch (start us, length us, event | category | flops | bytes accessed | tf_op | source)
XLA Modules:
  0.0 1188.4 jit_solution(2619913281555036576)
XLA Ops:
  21.6 48.9 %all-gather.7.cloned.1.call-done = bf16[1179648]{0:T(1024)(128)(2,1)} async-done(((bf16[294912]{0:T(1024)(128)(2,1)}), bf16[1179648]{0:T(1024)(128)(2,1)}) %all-gather.7.cloned.1.call-update) | async-done | bytes 2359312 | tf_op jit(solution)/shard_map/all_gather | solution.py:131
  77.3 13.4 %all-gather.3 = f32[4,1,1152]{2,1,0:T(1,128)S(1)} all-gather(f32[1,1,1152]{2,1,0:T(1,128)S(1)} %reshape.350), channel_id=3, replica_groups=mesh['dp'=8,'tensor'=4] {'tensor'}, dimensions={0}, use_global_device_ids=true | all-gather | bytes 23040 | tf_op jit(solution)/shard_map/all_gather | solution.py:203
  100.6 31.7 %maximum_select_fusion.1 = bf16[4,589824]{1,0:T(4,128)(2,1)S(1)} fusion(bf16[4,294912]{1,0:T(4,128)(2,1)} %collective-permute-done, bf16[4,294912]{1,0:T(4,128)(2,1)S(1)} %reshape.347, pred[]{:T(512)S(6)} %eq.38), kind=kLoop, calls=%fused_computation.80 | loop fusion | flops 21233664 | bytes 9437185 | tf_op jit(solution)/shard_map/jit(_where)/select_n | solution.py:133
  173.9 58.3 %while.26 = (s32[]{:T(128)}, bf16[4,1024,3,64]{1,3,2,0:T(8,128)(2,1)}, f32[4,3,1024]{2,1,0:T(4,128)S(1)}, bf16[4,1024,3,64]{1,3,2,0:T(8,128)(2,1)}, s32[1024]{0:...) while((s32[]{:T(128)}, ...), condition=%wide.region_3.4_spmd, body=%wide.region_0.3_spmd.sunk | while | flops 844297216 | bytes 47827060 | solution.py:78
  232.2 10.6 slice_reduce_fusion.4
  256.5 57.9 %maximum_select_fusion = bf16[4,1179648]{1,0:T(4,128)(2,1)S(1)} fusion(bf16[4,589824]{1,0:T(4,128)(2,1)} %collective-permute-done.1, bf16[4,589824]{1,0:T(4,128)(2,1)S(1)} %bitcast.258, pred[]{:T(512)S(6)} %eq.38), kind=kLoop, calls=%fused_computation.75 | loop fusion | flops 42467328 | bytes 18874368 | tf_op jit(solution)/shard_map/jit(_where)/select_n | solution.py:133
  319.3 28.7 %slice_reduce_fusion = (bf16[589824]{0:T(1024)(128)(2,1)}, bf16[589824]{0:T(1024)(128)(2,1)}, bf16[589824]{0:T(1024)(128)(2,1)}, bf16[589824]{0:T(1024)(128)(2,1)}) fusion(bf16[4,1179648]{1,0:T(4,128)(2,1)S(1)} %maximum_select_fusion), kind=kLoop, calls=%fused_computation.106 | loop fusion | bytes 9437184 | tf_op jit(solution)/shard_map/slice | solution.py:240
  364.1 13.6 %multiply_convert_fusion.1 = (bf16[1024,3072]{1,0:T(8,128)(2,1)S(1)}, f32[1024,3072]{1,0:T(8,128)}) fusion(f32[3072]{0:T(1024)S(1)} %copy-done.52, bf16[768,3072]{0,1:T(8,128)(2,1)} %bitcast.278, f32[1024,768]{0,1:T(8,128)S(1)} %get-tuple-element.257, f32[768]{0:T(1024)S(1)} %copy-done.60, f32[768]{0:T(1024)S(1)} %copy-done.54, ...), kind=kOutput, calls=%fused_computation.74 | convolution fusion | flops 4867227648 | bytes 26765312 | tf_op jit(solution)/shard_map/dot_general | solution.py:13
  403.8 9.0 reshape_reshape.6
  412.9 22.3 %convert_reduce_fusion = (f32[3072]{0:T(1024)}, bf16[1024,3072]{1,0:T(8,128)(2,1)}) fusion(f32[1024,3072]{1,0:T(8,128)} %get-tuple-element.259, f32[3072]{0:T(1024)S(1)} %copy-done.52, bf16[3072,768]{1,0:T(8,128)(2,1)} %reshape_reshape.6, f32[1024]{0:T(1024)S(1)} %broadcast_multiply_fusion.2, f32[1024,768]{0,1:T(8,128)} %copy-done.6, ...), kind=kOutput, calls=%fused_computation.73 | convolution fusion | flops 4911264768 | bytes 28355584 | tf_op jit(solution)/shard_map/dot_general | solution.py:23
  435.2 11.3 multiply_reduce_fusion.1
  461.2 117.3 %while.27 = (s32[]{:T(128)}, bf16[4,1024,3,64]{1,3,2,0:T(8,128)(2,1)}, bf16[4,1024,3,64]{1,3,2,0:T(8,128)(2,1)}, bf16[4,1024,3,64]{1,3,2,0:T(8,128)(2,1)S(1)}, b...) while((s32[]{:T(128)}, ...), condition=%wide.region_14.15_spmd, body=%wide.region_12.14_spmd.sunk | while | flops 2062480384 | bytes 102597744 | solution.py:112
  464.9 8.2 multiply_reduce_fusion.7
  473.1 7.1 multiply_convert_fusion.3
  494.3 8.2 multiply_reduce_fusion.7
  523.5 8.2 multiply_reduce_fusion.7
  531.7 7.0 multiply_convert_fusion.3
  552.8 8.2 multiply_reduce_fusion.7
  596.2 10.3 fusion.81
  606.5 12.6 %reshape.345 = f32[4,768,8,96]{1,0,3,2:T(4,128)} reshape(f32[3072,768]{0,1:T(8,128)} %fusion.81) | data formatting | bytes 18874368 | tf_op jit(solution)/shard_map/reshape | solution.py:161
  619.2 10.3 copy.111
  629.5 10.9 reshape.346
  642.4 10.6 fusion.97
  653.0 12.5 %reshape.343 = f32[8,96,4,768]{3,2,1,0:T(4,128)} reshape(f32[768,3072]{1,0:T(8,128)} %fusion.97) | data formatting | bytes 18874368 | tf_op jit(solution)/shard_map/reshape | solution.py:161
  665.5 9.1 copy.109
  684.7 16.2 %all-reduce = f32[4,1152]{1,0:T(4,128)S(1)} all-reduce(f32[4,1152]{1,0:T(4,128)S(1)} %concatenate.32), channel_id=6, replica_groups=mesh['dp'=8,'tensor'=4] {'tensor'}, use_global_device_ids=true, to_apply=%region_19.20.clone | all-reduce | flops 4608 | bytes 36864
  701.6 12.3 %psum.7 = f32[1152]{0:T(1024)S(1)} all-reduce(f32[1152]{0:T(1024)S(1)} %dynamic-slice_reduce_fusion), channel_id=1, replica_groups=mesh['dp'=8,'tensor'=4] {'dp'}, use_global_device_ids=true, to_apply=%region_20.21 | all-reduce | flops 1152 | bytes 9216 | tf_op jit(solution)/shard_map/psum | solution.py:309
  725.7 38.9 %all-reduce.1 = f32[32,6,24]{2,0,1:T(8,128)S(1)} all-reduce(f32[32,6,24]{2,0,1:T(8,128)S(1)} %bitcast.295), channel_id=10, replica_groups=mesh['dp'=8,'tensor'=4] {'dp','tensor'}, use_global_device_ids=true, to_apply=%region_30.31.clone | all-reduce | flops 4608 | bytes 36864
  765.9 25.6 %reduce-scatter.12.cloned.1.call-done = f32[96,192]{1,0:T(8,128)} async-done(((f32[3072,192]{1,0:T(8,128)}), f32[96,192]{1,0:T(8,128)}) %reduce-scatter.12.cloned.1.call-update) | async-done | bytes 73744 | tf_op jit(solution)/shard_map/reduce_scatter | solution.py:167
  791.5 106.4 %reduce-scatter.14.cloned.1.call-done = f32[96,192]{1,0:T(8,128)} async-done(((f32[3072,192]{1,0:T(8,128)}), f32[96,192]{1,0:T(8,128)}) %reduce-scatter.14.cloned.1.call-update) | async-done | bytes 73744 | tf_op jit(solution)/shard_map/reduce_scatter | solution.py:167
  897.9 141.0 %reduce-scatter.18.cloned.1.call-done = f32[768,96]{0,1:T(8,128)} async-done(((f32[24576,96]{0,1:T(8,128)}), f32[768,96]{0,1:T(8,128)}) %reduce-scatter.18.cloned.1.call-update) | async-done | bytes 294928 | tf_op jit(solution)/shard_map/reduce_scatter | solution.py:167
  1038.9 142.1 %reduce-scatter.16.cloned.1.call-done = f32[96,768]{1,0:T(8,128)} async-done(((f32[3072,768]{1,0:T(8,128)}), f32[96,768]{1,0:T(8,128)}) %reduce-scatter.16.cloned.1.call-update) | async-done | bytes 294928 | tf_op jit(solution)/shard_map/reduce_scatter | solution.py:167
  (319 shorter events, 318.7 us)
Async XLA Ops:
  7.2 93.3 %copy-start = (s32[4,1024]{1,0:T(4,128)S(1)}, s32[4,1024]{1,0:T(4,128)}, u32[]{:S(2)}) copy-start(s32[4,1024]{1,0:T(4,128)} %param.23) | copy-start | bytes 49156
  7.2 63.3 %all-gather.7.cloned.1.call-start = ((), (), s32[]{:S(2)}) async-start(), calls=%async_computation.11 | async-start | bytes 2949120 | tf_op jit(solution)/shard_map/all_gather | solution.py:131
  8.4 8.8 copy-start.28
  17.1 149.1 %all-gather.9.cloned.1.call-start = ((), (), s32[]{:S(2)}) async-start(), calls=%async_computation.12 | async-start | bytes 5898240 | tf_op jit(solution)/shard_map/all_gather | solution.py:131
  73.0 27.5 %collective-permute-start = (bf16[4,294912]{1,0:T(4,128)(2,1)S(1)}, bf16[4,294912]{1,0:T(4,128)(2,1)}, u32[]{:S(2)}, u32[]{:S(2)}) collective-permute-start(bf16[4,294912]{1,0:T(4,128)(2,1)S(1)} %reshape.347), channel_id=1, source_target_pairs={{0,4},{4,0},{8,12},{12,8},{16,20},{20,16},{24,28},{28,24},{1,5},{5... | collective-permute-start | bytes 7077896 | tf_op jit(solution)/shard_map/ppermute | solution.py:132
  76.5 689.4 %reduce-scatter.20.cloned.1.call-start = ((), (), s32[]{:S(2)}) async-start(), calls=%async_computation.13 | async-start | bytes 3244032
  172.6 83.8 %collective-permute-start.1 = (bf16[4,589824]{1,0:T(4,128)(2,1)}, bf16[4,589824]{1,0:T(4,128)(2,1)}, u32[]{:S(2)}, u32[]{:S(2)}) collective-permute-start(bf16[4,589824]{1,0:T(4,128)(2,1)} %reshape.349), channel_id=1, source_target_pairs={{0,4},{4,0},{8,12},{12,8},{16,20},{20,16},{24,28},{28,24},{1,5},{5... | collective-permute-start | bytes 14155784 | tf_op jit(solution)/shard_map/ppermute | solution.py:132
  232.2 16.2 %copy-start.23 = (bf16[4,147456]{1,0:T(4,128)(2,1)S(1)}, bf16[4,147456]{1,0:T(4,128)(2,1)}, u32[]{:S(2)}) copy-start(bf16[4,147456]{1,0:T(4,128)(2,1)} %get-tuple-element.241) | copy-start | bytes 3538948
  242.9 7.6 copy-start.18
  256.0 190.5 %copy-start.4 = (f32[1024,768]{0,1:T(8,128)}, f32[1024,768]{0,1:T(8,128)S(1)}, u32[]{:S(2)}) copy-start(f32[1024,768]{0,1:T(8,128)S(1)} %get-tuple-element.257) | copy-start | bytes 9437188
  256.0 190.4 %copy-start.38 = (f32[1024]{0:T(1024)}, f32[1024]{0:T(1024)S(1)}, u32[]{:S(2)}) copy-start(f32[1024]{0:T(1024)S(1)} %broadcast_multiply_fusion.5) | copy-start | bytes 12292
  256.4 190.0 %copy-start.43 = (f32[1024]{0:T(1024)}, f32[1024]{0:T(1024)S(1)}, u32[]{:S(2)}) copy-start(f32[1024]{0:T(1024)S(1)} %add_rsqrt_fusion.1) | copy-start | bytes 12292
  357.3 6.7 copy-start.52
  357.3 6.8 copy-start.54
  357.3 6.8 copy-start.60
  364.1 13.6 %copy-start.30 = (bf16[768,768]{1,0:T(8,128)(2,1)S(1)}, bf16[768,768]{1,0:T(8,128)(2,1)}, u32[]{:S(2)}) copy-start(bf16[768,768]{1,0:T(8,128)(2,1)} %slice.161) | copy-start | bytes 3538948
  386.8 7.9 copy-start.59
  400.5 34.6 %copy-start.36 = (f32[1024]{0:T(1024)}, f32[1024]{0:T(1024)S(1)}, u32[]{:S(2)}) copy-start(f32[1024]{0:T(1024)S(1)} %broadcast_multiply_fusion.4) | copy-start | bytes 12292
  403.0 32.1 %copy-start.40 = (f32[1024]{0:T(1024)}, f32[1024]{0:T(1024)S(1)}, u32[]{:S(2)}) copy-start(f32[1024]{0:T(1024)S(1)} %add_rsqrt_fusion) | copy-start | bytes 12292
  403.8 31.3 %copy-start.45 = (f32[1024]{0:T(1024)}, f32[1024]{0:T(1024)S(1)}, u32[]{:S(2)}) copy-start(f32[1024]{0:T(1024)S(1)} %broadcast_multiply_fusion.2) | copy-start | bytes 12292
  403.8 31.3 %copy-start.47 = (f32[1024]{0:T(1024)}, f32[1024]{0:T(1024)S(1)}, u32[]{:S(2)}) copy-start(f32[1024]{0:T(1024)S(1)} %broadcast_multiply_fusion.3) | copy-start | bytes 12292
  412.9 22.3 %copy-start.7 = (f32[1024,768]{0,1:T(8,128)S(1)}, f32[1024,768]{0,1:T(8,128)}, u32[]{:S(2)}) copy-start(f32[1024,768]{0,1:T(8,128)} %copy-done.6) | copy-start | bytes 9437188
  412.9 22.3 %copy-start.15 = (bf16[1024,768]{0,1:T(8,128)(2,1)S(1)}, bf16[1024,768]{0,1:T(8,128)(2,1)}, u32[]{:S(2)}) copy-start(bf16[1024,768]{0,1:T(8,128)(2,1)} %copy.133) | copy-start | bytes 4718596
  454.6 311.3 %reduce-scatter.10.cloned.1.call-start = ((), (), s32[]{:S(2)}) async-start(), calls=%async_computation.6 | async-start | bytes 3244032 | tf_op jit(solution)/shard_map/reduce_scatter | solution.py:167
  578.5 12.3 %copy-start.12 = (bf16[4,1024,3,64]{1,3,2,0:T(8,128)(2,1)}, bf16[4,1024,3,64]{1,3,2,0:T(8,128)(2,1)S(1)}, u32[]{:S(2)}) copy-start(bf16[4,1024,3,64]{1,3,2,0:T(8,128)(2,1)S(1)} %get-tuple-element.113) | copy-start | bytes 4718596
  584.4 207.1 %reduce-scatter.12.cloned.1.call-start = ((), (), s32[]{:S(2)}) async-start(), calls=%async_computation.7 | async-start | bytes 3244032 | tf_op jit(solution)/shard_map/reduce_scatter | solution.py:167
  590.7 307.2 %reduce-scatter.14.cloned.1.call-start = ((), (), s32[]{:S(2)}) async-start(), calls=%async_computation.8 | async-start | bytes 3244032 | tf_op jit(solution)/shard_map/reduce_scatter | solution.py:167
  594.3 444.6 %reduce-scatter.18.cloned.1.call-start = ((), (), s32[]{:S(2)}) async-start(), calls=%async_computation.10 | async-start | bytes 9732096 | tf_op jit(solution)/shard_map/reduce_scatter | solution.py:167
  640.5 540.6 %reduce-scatter.16.cloned.1.call-start = ((), (), s32[]{:S(2)}) async-start(), calls=%async_computation.9 | async-start | bytes 9732096 | tf_op jit(solution)/shard_map/reduce_scatter | solution.py:167
  680.6 33.9 %copy-start.17 = (bf16[4,1024,3,64]{1,3,2,0:T(8,128)(2,1)S(1)}, bf16[4,1024,3,64]{1,3,2,0:T(8,128)(2,1)}, u32[]{:S(2)}) copy-start(bf16[4,1024,3,64]{1,3,2,0:T(8,128)(2,1)} %get-tuple-element.111) | copy-start | bytes 4718596
  680.6 33.9 %copy-start.33 = (bf16[768,4,192]{0,2,1:T(8,128)(2,1)S(1)}, bf16[768,4,192]{0,2,1:T(8,128)(2,1)}, u32[]{:S(2)}) copy-start(bf16[768,4,192]{0,2,1:T(8,128)(2,1)} %copy.101) | copy-start | bytes 3538948
  720.7 460.3 %copy-start.1 = (s32[4,1024]{1,0:T(4,128)S(1)}, s32[4,1024]{1,0:T(4,128)}, u32[]{:S(2)}) copy-start(s32[4,1024]{1,0:T(4,128)} %param.23) | copy-start | bytes 49156
  (47 other events, 128.8 us)
Sparse Core Ops, SparseCore 0:
  17.3 53.1 all-gather.6
  76.6 89.6 all-gather.8
  454.7 100.0 reduce-scatter.19
  584.5 100.3 reduce-scatter.9
  690.8 100.5 reduce-scatter.11
  797.3 100.5 reduce-scatter.13
  904.4 134.5 reduce-scatter.17
  1046.4 134.6 reduce-scatter.15

commit v2 on v1

--- a/solution.py
+++ b/solution.py
@@ -122,25 +122,26 @@
     return (join_groups(grad_query), join_groups(grad_key), join_groups(grad_value))
 
 
-def gather_shards(pieces):
-    flat = jnp.concatenate([piece.reshape(-1) for piece in pieces])
+def gather_shards(first_pieces, second_pieces):
     dp_count = lax.axis_size("dp")
     core = lax.rem(lax.axis_index("dp"), 2)
-    half = flat.shape[0] // 2
-    mine = lax.dynamic_slice_in_dim(flat, core * half, half, 0)
+
+    def flat(pieces):
+        return jnp.concatenate([piece.reshape(-1) for piece in pieces]).reshape(-1, 128)
+
+    first, second = flat(first_pieces), flat(second_pieces)
+    mine = jnp.where(core == 0, first, second)
     gathered = lax.all_gather(mine, "tensor", axis=0, tiled=False)
     other = lax.ppermute(gathered, "dp", perm=[(i, i ^ 1) for i in range(dp_count)])
-    both = jnp.where(
-        core == 0,
-        jnp.concatenate([gathered, other], axis=1),
-        jnp.concatenate([other, gathered], axis=1),
-    )
+    halves = (jnp.where(core == 0, gathered, other), jnp.where(core == 0, other, gathered))
     shards = []
-    start = 0
-    for piece in pieces:
-        size = piece.size
-        shards.append(both[:, start : start + size].reshape((both.shape[0],) + piece.shape))
-        start += size
+    for half, pieces in zip(halves, (first_pieces, second_pieces)):
+        half = half.reshape(half.shape[0], -1)
+        start = 0
+        for piece in pieces:
+            size = piece.size
+            shards.append(half[:, start : start + size].reshape((half.shape[0],) + piece.shape))
+            start += size
     return shards
 
 
@@ -154,17 +155,41 @@
     return shards.reshape(count * rows, cols)
 
 
-def scatter_blocks(full, row_axis, col_axis):
+def blocked_grad(left_side, right_side, row_axis, col_axis):
     row_parts = lax.axis_size(row_axis)
     col_parts = lax.axis_size(col_axis)
-    rows, cols = full.shape
-    blocks = full.reshape(row_parts, rows // row_parts, col_parts, cols // col_parts)
-    if row_axis == "dp":
-        blocks = blocks.transpose(0, 2, 1, 3)
-    else:
-        blocks = blocks.transpose(2, 0, 1, 3)
-    blocks = blocks.reshape(row_parts * col_parts * (rows // row_parts), cols // col_parts)
-    return lax.psum_scatter(blocks, ("dp", "tensor"), scatter_dimension=0, tiled=True)
+    tokens, rows = left_side.shape
+    cols = right_side.shape[1]
+    left = left_side.reshape(tokens, row_parts, rows // row_parts)
+    right = right_side.reshape(tokens, col_parts, cols // col_parts)
+    spec = "nai,nbj->abij" if row_axis == "dp" else "nbi,naj->abij"
+    return jnp.einsum(spec, left, right, preferred_element_type=jnp.float32)
+
+
+def join_grads(blocks):
+    parts = blocks[0].shape[0] * blocks[0].shape[1]
+    joined = jnp.concatenate([block.reshape(parts, -1, 128) for block in blocks], axis=1)
+    return joined.reshape(-1, 128)
+
+
+def scatter_grads(joined, blocks):
+    summed = lax.psum_scatter(joined, ("dp", "tensor"), scatter_dimension=0, tiled=True)
+    summed = summed.reshape(-1)
+    pieces = []
+    start = 0
+    for block in blocks:
+        size = block[0, 0].size
+        pieces.append(summed[start : start + size].reshape(block.shape[2:]))
+        start += size
+    return pieces
+
+
+def shared_blocks(vectors):
+    parts = lax.axis_size("dp") * lax.axis_size("tensor")
+    stacked = jnp.stack(vectors)
+    return stacked.reshape(len(vectors), lax.axis_size("dp"), lax.axis_size("tensor"), -1).transpose(
+        1, 2, 0, 3
+    )
 
 
 def on_device(
@@ -190,7 +215,6 @@
     part_count = lax.axis_size("tensor")
     part_id = lax.axis_index("tensor")
     row_len = segments.shape[1]
-    dp_count = lax.axis_size("dp")
 
     input_rows = lax.dynamic_slice_in_dim(layer_input, part_id * row_len, row_len, 0)
     segment_row = lax.dynamic_index_in_dim(segments, part_id, 0, keepdims=False)
@@ -198,8 +222,10 @@
         jnp.float32
     )
 
-    q_sh, k_sh, v_sh, o_sh = gather_shards([query_weight, key_weight, value_weight, output_weight])
-    u_sh, d_sh = gather_shards([up_weight, down_weight])
+    q_sh, k_sh, v_sh, o_sh = gather_shards(
+        [query_weight, key_weight], [value_weight, output_weight]
+    )
+    u_sh, d_sh = gather_shards([up_weight], [down_weight])
     bias_sh = lax.all_gather(
         jnp.concatenate([query_bias, value_bias, up_bias]), "tensor", axis=0, tiled=False
     )
@@ -249,81 +275,87 @@
     grad_second_shift = jnp.sum(grad_out, 0)
     grad_down_bias = jnp.sum(grad_second, 0)
     down_low = grad_second.astype(jnp.bfloat16)
-    grad_down_weight = contract_rows(hidden_low, down_low)
     grad_hidden = contract_last(down_low, dw)
     grad_pre = pull_gelu(grad_hidden)[0].astype(jnp.bfloat16)
-    grad_up_weight = contract_rows(first_low, grad_pre)
     grad_up_bias = jnp.sum(grad_pre, 0, dtype=jnp.float32)
+    ffn_blocks = [
+        blocked_grad(first_low, grad_pre, "dp", "tensor"),
+        blocked_grad(hidden_low, down_low, "tensor", "dp"),
+    ]
     first_grad = contract_last(grad_pre, uw) + grad_second
     grad_first_gain = jnp.sum(first_grad * first_unit, 0)
     grad_first_shift = jnp.sum(first_grad, 0)
     attn_grad = normalize_back(first_grad, first_unit, first_inv, first_gain)
     grad_output_bias = jnp.sum(attn_grad, 0)
     attn_grad_low = attn_grad.astype(jnp.bfloat16)
-    grad_output_weight = contract_rows(context, attn_grad_low)
     grad_context = contract_last(attn_grad_low, ow).astype(jnp.bfloat16)
+    ffn_blocks.append(blocked_grad(context, attn_grad_low, "tensor", "dp"))
+    ffn_joined, grad_context = lax.optimization_barrier((join_grads(ffn_blocks), grad_context))
+    ffn_summed = scatter_grads(ffn_joined, ffn_blocks)
     query_low, key_low, value_low = attend_back(
         queries, key_side, value_proj, segment_row, log_total, grad_context
     )
-    grad_query_weight = contract_rows(input_rows, query_low)
-    grad_key_weight = contract_rows(input_rows, key_low)
-    grad_value_weight = contract_rows(input_rows, value_low)
+    ffn_summed, query_low, key_low, value_low = lax.optimization_barrier(
+        (ffn_summed, query_low, key_low, value_low)
+    )
     grad_query_bias = jnp.sum(query_low, 0, dtype=jnp.float32)
     grad_value_bias = jnp.sum(value_low, 0, dtype=jnp.float32)
+    attn_blocks = [
+        blocked_grad(input_rows, query_low, "dp", "tensor"),
+        blocked_grad(input_rows, key_low, "dp", "tensor"),
+        blocked_grad(input_rows, value_low, "dp", "tensor"),
+    ]
+    attn_summed = scatter_grads(join_grads(attn_blocks), attn_blocks)
     input_grad = (
         attn_grad
         + contract_last(query_low, qw)
         + contract_last(key_low, kw)
         + contract_last(value_low, vw)
     )
-
-    summed_weights = (
-        scatter_blocks(grad_query_weight, "dp", "tensor"),
-        scatter_blocks(grad_key_weight, "dp", "tensor"),
-        scatter_blocks(grad_value_weight, "dp", "tensor"),
-        scatter_blocks(grad_output_weight, "tensor", "dp"),
-        scatter_blocks(grad_up_weight, "dp", "tensor"),
-        scatter_blocks(grad_down_weight, "tensor", "dp"),
-    )
-    shared = jnp.stack(
-        [
-            grad_output_bias,
-            grad_first_gain,
-            grad_first_shift,
-            grad_down_bias,
-            grad_second_gain,
-            grad_second_shift,
-        ]
-    )
-    shared_parts = dp_count * part_count
-    shared = shared.reshape(6, shared_parts, -1).transpose(1, 0, 2)
-    shared = lax.psum_scatter(shared, ("dp", "tensor"), scatter_dimension=0, tiled=True)[0]
-    split = jnp.concatenate(
-        [
-            grad_query_bias.reshape(part_count, -1),
-            grad_value_bias.reshape(part_count, -1),
-            grad_up_bias.reshape(part_count, -1),
-        ],
-        axis=1,
-    )
-    split = lax.psum(
-        lax.psum_scatter(split, "tensor", scatter_dimension=0, tiled=True)[0], "dp"
-    )
+    small = lax.psum(
+        jnp.concatenate(
+            [
+                grad_query_bias,
+                grad_value_bias,
+                grad_up_bias,
+                grad_output_bias,
+                grad_first_gain,
+                grad_first_shift,
+                grad_down_bias,
+                grad_second_gain,
+                grad_second_shift,
+            ]
+        ),
+        ("dp", "tensor"),
+    )
+    split_width = 2 * head_width * part_count + up_bias.shape[0] * part_count
+    split = small[:split_width]
+    shared = small[split_width:].reshape(6, -1)
+    device_id = lax.axis_index("dp") * part_count + part_id
+    piece = shared.shape[1] // (lax.axis_size("dp") * part_count)
+    shared = lax.dynamic_slice_in_dim(shared, device_id * piece, piece, 1)
+
+    def own_block(vector, offset, width):
+        return lax.dynamic_slice_in_dim(vector, offset + part_id * width, width, 0)
+
+    query_bias_grad = own_block(split, 0, head_width)
+    value_bias_grad = own_block(split, head_width * part_count, head_width)
+    up_bias_grad = own_block(split, 2 * head_width * part_count, up_bias.shape[0])
     return (
         layer_output,
         input_grad,
-        summed_weights[0],
-        split[:head_width],
-        summed_weights[1],
-        summed_weights[2],
-        split[head_width : 2 * head_width],
-        summed_weights[3],
+        attn_summed[0],
+        query_bias_grad,
+        attn_summed[1],
+        attn_summed[2],
+        value_bias_grad,
+        ffn_summed[2],
         shared[0],
         shared[1],
         shared[2],
-        summed_weights[4],
-        split[2 * head_width :],
-        summed_weights[5],
+        ffn_summed[0],
+        up_bias_grad,
+        ffn_summed[1],
         shared[3],
         shared[4],
         shared[5],

time: 1200 us -> 872 us (0.73)
  waiting for transfers between devices: 465 us -> 210 us
  other arithmetic: 158 us -> 93.7 us
  local copies, waits for them, and re-layouts: 220 us -> 246 us
  blocking collectives: 80.9 us -> 55.2 us
    reduce_scatter x5 -> x2, waiting for transfers between devices: 415 us -> 138 us  [scatter_grads(): lax.psum_scatter(joined, ('dp', 'tensor'), scatter_dimension=0, tiled=True)]
    select_n x2 -> x3, other arithmetic: 89.7 us -> 8.77 us  [the longest x1 6.63 us: gather_shards(): jnp.where(core == 0, gathered, other)]
    unnamed x2 -> x0, blocking collectives: 55.2 us -> none
    reshape x15 -> x17, local copies, waits for them, and re-layouts: 50.7 us -> 79 us  [the longest x6 42.3 us: join_grads(): block.reshape(parts, -1, 128)]
    psum x1, blocking collectives: 12.3 us -> 40.5 us  [on_device(): lax.psum(jnp.concatenate([grad_query_bias, grad_value_bias, grad_up_bias,...]
    slice x5, local copies, waits for them, and re-layouts: 42.3 us -> 16.2 us  [on_device(): dw[units]]
    all_gather x2, waiting for transfers between devices: 50 us -> 71 us  [gather_shards(): gathered = lax.all_gather(mine, 'tensor', axis=0, tiled=False)]
    transpose x2 -> x6, local copies, waits for them, and re-layouts: 19.4 us -> 30.2 us  [blocked_grad(): return jnp.einsum(spec, left, right, preferred_element_type=jnp.float32)]
  transfers between devices with their start and end apart: 10 -> 6, of which waited for: 6 -> 4; matrix products, arithmetic and copies ran while one was open for 34% -> 35% of each run, Pallas kernels for 0% -> 0%
where the time goes in v2:
time: 872 us; the launch traced here: 864 us
  local copies, waits for them, and re-layouts  246 us (28%)
  matrix products  244 us (28%)
  waiting for transfers between devices  210 us (24%)
  other arithmetic  93.7 us (11%)
  blocking collectives  55.2 us (6%)
  between operations  14.7 us (2%)
    reduce_scatter x2, waiting for transfers between devices, scatter_grads(): lax.psum_scatter(joined, ('dp', 'tensor'), scatter_dimension=0, tiled=True)  138 us
    all_gather x2, waiting for transfers between devices, gather_shards(): gathered = lax.all_gather(mine, 'tensor', axis=0, tiled=False)  71 us
    unnamed x133, local copies, waits for them, and re-layouts  45.7 us
    reshape x6, local copies, waits for them, and re-layouts, join_grads(): block.reshape(parts, -1, 128)  42.3 us
    dot_general x12, matrix products, product(): return jnp.dot(left_side, right_side, preferred_element_type=jnp.float32)  40.9 us
    psum x1, blocking collectives, on_device(): lax.psum(jnp.concatenate([grad_query_bias, grad_value_bias, grad_up_bias,...  40.5 us
    dot_general x6, matrix products, contract_last(): lax.dot_general(left_side, right_side, (((1,), (1,)), ((), ())), preferre...  39.9 us
    dot_general x6, matrix products, blocked_grad(): return jnp.einsum(spec, left, right, preferred_element_type=jnp.float32)  35.9 us
  transfers between devices with their start and end apart: 6, of which 4 were waited for; matrix products, arithmetic and copies ran while one was open for 35% of the time, Pallas kernels for 0%

profile of v2, /device:TPU:0, one launch (start us, length us, event | category | flops | bytes accessed | tf_op | source)
XLA Modules:
  0.0 863.5 jit_solution(2216635679349058741)
XLA Ops:
  17.1 53.3 %all-gather.5.cloned.1.call-done = bf16[4,2304,128]{2,1,0:T(8,128)(2,1)} async-done(((bf16[1,2304,128]{2,1,0:T(8,128)(2,1)}), bf16[4,2304,128]{2,1,0:T(8,128)(2,1)}) %all-gather.5.cloned.1.call-update) | async-done | bytes 2359312 | tf_op jit(solution)/shard_map/all_gather | solution.py:134
  76.3 14.7 %all-gather.1 = f32[4,1,1152]{2,1,0:T(1,128)S(1)} all-gather(f32[1,1,1152]{2,1,0:T(1,128)S(1)} %reshape.452), channel_id=2, replica_groups=mesh['dp'=8,'tensor'=4] {'tensor'}, dimensions={0}, use_global_device_ids=true | all-gather | bytes 23040 | tf_op jit(solution)/shard_map/all_gather | solution.py:229
  96.2 12.2 %copy_bitcast_fusion = (bf16[4,294912]{1,0:T(4,128)(2,1)S(1)}, bf16[4,294912]{1,0:T(4,128)(2,1)S(1)}) fusion(bf16[1,4,2304,128]{3,2,1,0:T(8,128)(2,1)S(1)} %get-tuple-element.258, bf16[1,4,2304,128]{3,2,1,0:T(8,128)(2,1)S(1)} %get-tuple-element.259), kind=kLoop, calls=%fused_computation.114 | loop fusion | bytes 9437184 | tf_op jit(solution)/shard_map/reshape | solution.py:139
  143.3 17.7 %all-gather.7.cloned.1.call-done = bf16[4,4608,128]{2,1,0:T(8,128)(2,1)} async-done(((bf16[1,4608,128]{2,1,0:T(8,128)(2,1)}), bf16[4,4608,128]{2,1,0:T(8,128)(2,1)}) %all-gather.7.cloned.1.call-update) | async-done | bytes 4718608 | tf_op jit(solution)/shard_map/all_gather | solution.py:134
  162.4 60.5 %while.26 = (s32[]{:T(128)}, bf16[4,1024,3,64]{1,3,2,0:T(8,128)(2,1)}, f32[4,3,1024]{2,1,0:T(4,128)}, bf16[4,1024,3,64]{1,3,2,0:T(8,128)(2,1)}, s32[1024]{0:T(10...) while((s32[]{:T(128)}, bf16[4,1024,3,64]{1,3,2,0:T(8,128)(2,1)}, ...), condition=%wide.region_3.4_spmd, body=%wide.region_0.3_spmd.sunk | while | flops 844297216 | bytes 47818876 | solution.py:78
  222.9 10.5 %slice_reduce_fusion.3 = (bf16[147456]{0:T(1024)(128)(2,1)}, bf16[147456]{0:T(1024)(128)(2,1)}, bf16[147456]{0:T(1024)(128)(2,1)}, bf16[147456]{0:T(1024)(128)(2,1)S(1)}) fusion(bf16[4,294912]{1,0:T(4,128)(2,1)} %copy-done.7), kind=kLoop, calls=%fused_computation.141 | loop fusion | bytes 2359296 | tf_op jit(solution)/shard_map/slice | solution.py:253
  248.6 6.6 broadcast_select_fusion.1
  259.6 9.2 %reshape_reshape_reshape.3 = bf16[3072,768]{1,0:T(8,128)(2,1)} reshape(bf16[4,4608,128]{2,1,0:T(8,128)(2,1)} %copy-done.3) | data formatting | bytes 9437184 | tf_op jit(solution)/shard_map/reshape;reshape;reshape | solution.py:155
  272.4 9.2 %reshape_reshape.11 = bf16[4,768,768]{2,1,0:T(8,128)(2,1)} reshape(bf16[4,4608,128]{2,1,0:T(8,128)(2,1)} %get-tuple-element.251) | data formatting | bytes 9437184 | tf_op jit(solution)/shard_map/reshape;reshape | solution.py:143
  281.6 6.6 copy.115
  295.0 13.3 %multiply_convert_fusion.1 = (bf16[1024,3072]{1,0:T(8,128)(2,1)S(1)}, f32[1024,3072]{1,0:T(8,128)}) fusion(f32[3072]{0:T(1024)S(1)} %copy-done.44, bf16[1024,768]{0,1:T(8,128)(2,1)} %fusion.81, bf16[768,3072]{0,1:T(8,128)(2,1)} %bitcast.292), kind=kOutput, calls=%fused_computation.75 | convolution fusion | flops 4863295488 | bytes 25178112 | tf_op jit(solution)/shard_map/dot_general | solution.py:13
  331.4 16.8 %convert_reduce_fusion = (f32[3072]{0:T(1024)}, bf16[1024,3072]{1,0:T(8,128)(2,1)S(1)}) fusion(f32[1024,3072]{1,0:T(8,128)} %get-tuple-element.285, f32[3072]{0:T(1024)S(1)} %copy-done.44, bf16[1024,768]{0,1:T(8,128)(2,1)S(1)} %get-tuple-element.253, bf16[3072,768]{1,0:T(8,128)(2,1)} %reshape_reshape_reshape.3), kind=kOutput, calls=%fused_computation.74 | convolution fusion | flops 4904186880 | bytes 25190400 | tf_op jit(solution)/shard_map/dot_general | solution.py:23
  350.8 10.8 %multiply_reduce_fusion.1 = (f32[768]{0:T(1024)}, f32[1024]{0:T(1024)S(1)}, f32[1024]{0:T(1024)S(1)}, f32[768]{0:T(1024)}, f32[1024,768]{0,1:T(8,128)}) fusion(f32[1024,768]{0,1:T(8,128)S(1)} %get-tuple-element.283, f32[1024]{0:T(1024)S(1)} %add_rsqrt_fusion.1, f32[1024]{0:T(1024)S(1)} %broadcast_multiply_fusion.5, f32[768]{0:T(1024)S(1)} %copy-done.41, ...), kind=kOutput, calls=%fused_computation.96 | convolution fusion | flops 4845989888 | bytes 22065152 | tf_op jit(solution)/shard_map/dot_general | solution.py:23
  361.6 12.3 %reshape.424 = bf16[1024,4,768]{2,1,0:T(4,128)(2,1)} reshape(bf16[1024,3072]{1,0:T(8,128)(2,1)} %copy-done.11) | data formatting | bytes 12582912 | tf_op jit(solution)/shard_map/reshape | solution.py:164
  389.4 10.0 %fusion.76 = f32[8,4,768,96]{2,3,1,0:T(8,128)} fusion(bf16[1024,8,96,1]{0,2,3,1:T(8,128)(2,1)} %bitcast.298, bf16[128,4,8,768]{3,2,1,0:T(8,128)(2,1)} %bitcast.309), kind=kOutput, calls=%fused_computation.91 | convolution fusion | flops 4831838208 | bytes 17301504 | tf_op jit(solution)/shard_map/nbi,naj->abij/dot_general | solution.py:166
  399.4 11.5 %copy.120 = f32[8,4,768,96]{3,2,1,0:T(8,128)} copy(f32[8,4,768,96]{2,3,1,0:T(8,128)} %fusion.76) | data formatting | bytes 18874368 | tf_op jit(solution)/shard_map/nbi,naj->abij/transpose | solution.py:166
  410.9 14.3 %reshape.429 = f32[32,576,128]{2,1,0:T(8,128)} reshape(f32[8,4,768,96]{3,2,1,0:T(8,128)} %copy.120) | data formatting | bytes 18874368 | tf_op jit(solution)/shard_map/reshape | solution.py:171
  425.2 7.8 fusion.73
  437.7 11.2 %reshape.426 = f32[32,576,128]{2,1,0:T(8,128)} reshape(f32[8,4,96,768]{3,2,1,0:T(8,128)} %copy.118) | data formatting | bytes 18874368 | tf_op jit(solution)/shard_map/reshape | solution.py:171
  453.4 13.5 %pad_maximum_fusion = f32[32,1296,128]{2,1,0:T(8,128)} fusion(f32[32,144,128]{2,1,0:T(8,128)S(1)} %copy-done.10, f32[32,576,128]{2,1,0:T(8,128)} %reshape.429, f32[32,576,128]{2,1,0:T(8,128)S(1)} %copy-done.4), kind=kLoop, calls=%fused_computation.64 | loop fusion | flops 10616832 | bytes 42467328 | tf_op jit(solution)/shard_map/concatenate | solution.py:171
  472.9 121.8 %while.27 = (s32[]{:T(128)}, bf16[4,1024,3,64]{1,3,2,0:T(8,128)(2,1)}, bf16[4,1024,3,64]{1,3,2,0:T(8,128)(2,1)}, bf16[4,1024,3,64]{1,3,2,0:T(8,128)(2,1)S(1)}, b...) while((s32[]{:T(128)}, ...), condition=%wide.region_15.16_spmd, body=%wide.region_13.15_spmd.sunk | while | flops 2062480384 | bytes 102597752 | solution.py:112
  477.1 8.6 multiply_reduce_fusion.7
  485.7 7.8 multiply_convert_fusion.3
  508.4 8.3 multiply_reduce_fusion.7
  516.7 7.0 multiply_convert_fusion.3
  538.6 8.3 multiply_reduce_fusion.7
  546.8 7.1 multiply_convert_fusion.3
  568.7 8.3 multiply_reduce_fusion.7
  577.0 7.2 multiply_convert_fusion.3
  594.7 90.8 %reduce-scatter.3.cloned.1.call-done = f32[1296,128]{1,0:T(8,128)} async-done(((f32[41472,128]{1,0:T(8,128)}), f32[1296,128]{1,0:T(8,128)}) %reduce-scatter.3.cloned.1.call-update) | async-done | bytes 663568 | tf_op jit(solution)/shard_map/reduce_scatter | solution.py:176
  762.7 40.5 %psum.7 = f32[9216]{0:T(1024)S(1)} all-reduce(f32[9216]{0:T(1024)} %constant_dynamic-update-slice_fusion), channel_id=1, replica_groups=mesh['dp'=8,'tensor'=4] {'dp','tensor'}, use_global_device_ids=true, to_apply=%region_26.27 | all-reduce | flops 9216 | bytes 73728 | tf_op jit(solution)/shard_map/psum | solution.py:315
  806.0 47.6 %reduce-scatter.5.cloned.1.call-done = f32[432,128]{1,0:T(8,128)} async-done(((f32[13824,128]{1,0:T(8,128)}), f32[432,128]{1,0:T(8,128)}) %reduce-scatter.5.cloned.1.call-update) | async-done | bytes 221200 | tf_op jit(solution)/shard_map/reduce_scatter | solution.py:176
  (300 shorter events, 345.5 us)
Async XLA Ops:
  7.2 86.3 %copy-start = (s32[4,1024]{1,0:T(4,128)S(1)}, s32[4,1024]{1,0:T(4,128)}, u32[]{:S(2)}) copy-start(s32[4,1024]{1,0:T(4,128)} %param.23) | copy-start | bytes 49156
  7.2 63.2 %all-gather.5.cloned.1.call-start = ((), (), s32[]{:S(2)}) async-start(), calls=%async_computation.2 | async-start | bytes 2949120 | tf_op jit(solution)/shard_map/all_gather | solution.py:134
  8.4 62.0 %copy-start.33 = (bf16[768,768]{1,0:T(8,128)(2,1)S(1)}, bf16[768,768]{1,0:T(8,128)(2,1)}, u32[]{:S(2)}) copy-start(bf16[768,768]{1,0:T(8,128)(2,1)} %param.33) | copy-start | bytes 3538948
  8.4 62.0 %copy-start.34 = (bf16[768,768]{1,0:T(8,128)(2,1)S(1)}, bf16[768,768]{1,0:T(8,128)(2,1)}, u32[]{:S(2)}) copy-start(bf16[768,768]{1,0:T(8,128)(2,1)} %param.35) | copy-start | bytes 3538948
  17.0 144.0 %all-gather.7.cloned.1.call-start = ((), (), s32[]{:S(2)}) async-start(), calls=%async_computation.3 | async-start | bytes 5898240 | tf_op jit(solution)/shard_map/all_gather | solution.py:134
  70.4 23.1 %collective-permute-start = (bf16[4,2304,128]{2,1,0:T(8,128)(2,1)}, bf16[4,2304,128]{2,1,0:T(8,128)(2,1)}, u32[]{:S(2)}, u32[]{:S(2)}) collective-permute-start(bf16[4,2304,128]{2,1,0:T(8,128)(2,1)} %all-gather.5.cloned.1.call-done), channel_id=1, source_target_pairs={{0,4},{4,0},{8,12},{12,8},{16,20},{20,16},{24,28},{28,24},{1,5},{5... | collective-permute-start | bytes 7077896 | tf_op jit(solution)/shard_map/ppermute | solution.py:135
  72.4 613.1 %reduce-scatter.3.cloned.1.call-start = ((), (), s32[]{:S(2)}) async-start(), calls=%async_computation.4 | async-start | bytes 21897216 | tf_op jit(solution)/shard_map/reduce_scatter | solution.py:176
  161.0 87.6 %collective-permute-start.1 = (bf16[4,4608,128]{2,1,0:T(8,128)(2,1)}, bf16[4,4608,128]{2,1,0:T(8,128)(2,1)}, u32[]{:S(2)}, u32[]{:S(2)}) collective-permute-start(bf16[4,4608,128]{2,1,0:T(8,128)(2,1)} %all-gather.7.cloned.1.call-done), channel_id=1, source_target_pairs={{0,4},{4,0},{8,12},{12,8},{16,20},{20,16},{24,28},{28,24},{1,5},{5... | collective-permute-start | bytes 14155784 | tf_op jit(solution)/shard_map/ppermute | solution.py:135
  163.1 4.3 copy-start.2
  178.2 4.3 copy-start.2
  193.3 4.3 copy-start.2
  208.4 4.3 copy-start.2
  222.9 18.1 %copy-start.22 = (s32[1024]{0:T(1024)}, s32[1024]{0:T(1024)S(1)}, u32[]{:S(2)}) copy-start(s32[1024]{0:T(1024)S(1)} %get-tuple-element.483) | copy-start | bytes 12292
  222.9 16.0 %copy-start.19 = (bf16[4,147456]{1,0:T(4,128)(2,1)S(1)}, bf16[4,147456]{1,0:T(4,128)(2,1)}, u32[]{:S(2)}) copy-start(bf16[4,147456]{1,0:T(4,128)(2,1)} %get-tuple-element.261) | copy-start | bytes 3538948
  233.4 7.6 copy-start.15
  288.3 6.7 copy-start.44
  295.0 13.3 %copy-start.31 = (bf16[768,768]{1,0:T(8,128)(2,1)S(1)}, bf16[768,768]{1,0:T(8,128)(2,1)}, u32[]{:S(2)}) copy-start(bf16[768,768]{1,0:T(8,128)(2,1)} %slice.181) | copy-start | bytes 3538948
  331.4 16.8 %copy-start.24 = (bf16[1024,768]{0,1:T(8,128)(2,1)}, bf16[1024,768]{0,1:T(8,128)(2,1)S(1)}, u32[]{:S(2)}) copy-start(bf16[1024,768]{0,1:T(8,128)(2,1)S(1)} %get-tuple-element.253) | copy-start | bytes 4718596
  410.9 14.3 %copy-start.26 = (bf16[1024,768]{0,1:T(8,128)(2,1)S(1)}, bf16[1024,768]{0,1:T(8,128)(2,1)}, u32[]{:S(2)}) copy-start(bf16[1024,768]{0,1:T(8,128)(2,1)} %fusion.81) | copy-start | bytes 4718596
  437.7 11.2 %copy-start.29 = (bf16[768,768]{1,0:T(8,128)(2,1)S(1)}, bf16[768,768]{1,0:T(8,128)(2,1)}, u32[]{:S(2)}) copy-start(bf16[768,768]{1,0:T(8,128)(2,1)} %reshape_reshape.13) | copy-start | bytes 3538948
  437.7 15.4 %copy-start.10 = (f32[32,144,128]{2,1,0:T(8,128)S(1)}, f32[32,144,128]{2,1,0:T(8,128)}, u32[]{:S(2)}) copy-start(f32[32,144,128]{2,1,0:T(8,128)} %reshape.431) | copy-start | bytes 7077892
  448.9 4.5 copy-start.4
  466.9 386.7 %reduce-scatter.5.cloned.1.call-start = ((), (), s32[]{:S(2)}) async-start(), calls=%async_computation.5 | async-start | bytes 7299072 | tf_op jit(solution)/shard_map/reduce_scatter | solution.py:176
  698.0 4.7 copy-start.18
  711.4 4.7 copy-start.13
  746.7 110.0 %copy-start.1 = (s32[4,1024]{1,0:T(4,128)S(1)}, s32[4,1024]{1,0:T(4,128)}, u32[]{:S(2)}) copy-start(s32[4,1024]{1,0:T(4,128)} %param.23) | copy-start | bytes 49156
  750.4 4.5 copy-start.42
  750.4 5.8 copy-start.50
  750.4 7.1 copy-start.49
  750.4 8.4 copy-start.39
  750.4 9.7 %copy-start.38 = (f32[768]{0:T(1024)S(1)}, f32[768]{0:T(1024)}, u32[]{:S(2)}) copy-start(f32[768]{0:T(1024)} %get-tuple-element.200) | copy-start | bytes 9220
  750.4 11.0 %copy-start.37 = (f32[768]{0:T(1024)S(1)}, f32[768]{0:T(1024)}, u32[]{:S(2)}) copy-start(f32[768]{0:T(1024)} %get-tuple-element.210) | copy-start | bytes 9220
  (34 other events, 82.8 us)
Sparse Core Ops, SparseCore 0:
  17.1 53.1 all-gather.4
  72.5 88.4 all-gather.6
  467.0 218.4 reduce-scatter.2
  734.5 119.0 reduce-scatter.4

commit v3 on v2

--- a/solution.py
+++ b/solution.py
@@ -169,12 +169,12 @@
 def join_grads(blocks):
     parts = blocks[0].shape[0] * blocks[0].shape[1]
     joined = jnp.concatenate([block.reshape(parts, -1, 128) for block in blocks], axis=1)
-    return joined.reshape(-1, 128)
+    return joined.reshape(-1, 128).astype(jnp.bfloat16)
 
 
 def scatter_grads(joined, blocks):
     summed = lax.psum_scatter(joined, ("dp", "tensor"), scatter_dimension=0, tiled=True)
-    summed = summed.reshape(-1)
+    summed = summed.reshape(-1).astype(jnp.float32)
     pieces = []
     start = 0
     for block in blocks:

time: 872 us -> 747 us (0.86)
  waiting for transfers between devices: 210 us -> 117 us
  local copies, waits for them, and re-layouts: 246 us -> 224 us
    reduce_scatter x2, waiting for transfers between devices: 138 us -> 45.9 us  [scatter_grads(): lax.psum_scatter(joined, ('dp', 'tensor'), scatter_dimension=0, tiled=True)]
    transpose x6, local copies, waits for them, and re-layouts: 30.2 us -> 17.9 us  [blocked_grad(): return jnp.einsum(spec, left, right, preferred_element_type=jnp.float32)]
    unnamed x133 -> x125, local copies, waits for them, and re-layouts: 45.7 us -> 43.8 us
  transfers between devices with their start and end apart: 6 -> 6, of which waited for: 4 -> 4; matrix products, arithmetic and copies ran while one was open for 35% -> 41% of each run, Pallas kernels for 0% -> 0%
where the time goes in v3:
time: 747 us; the launch traced here: 738 us
  matrix products  239 us (32%)
  local copies, waits for them, and re-layouts  224 us (30%)
  waiting for transfers between devices  117 us (16%)
  other arithmetic  88.3 us (12%)
  blocking collectives  54.8 us (7%)
  between operations  14.7 us (2%)
    all_gather x2, waiting for transfers between devices, gather_shards(): gathered = lax.all_gather(mine, 'tensor', axis=0, tiled=False)  71 us
    reduce_scatter x2, waiting for transfers between devices, scatter_grads(): lax.psum_scatter(joined, ('dp', 'tensor'), scatter_dimension=0, tiled=True)  45.9 us
    unnamed x125, local copies, waits for them, and re-layouts  43.8 us
    dot_general x12, matrix products, product(): return jnp.dot(left_side, right_side, preferred_element_type=jnp.float32)  40.8 us
    psum x1, blocking collectives, on_device(): lax.psum(jnp.concatenate([grad_query_bias, grad_value_bias, grad_up_bias,...  40.2 us
    dot_general x6, matrix products, contract_last(): lax.dot_general(left_side, right_side, (((1,), (1,)), ((), ())), preferre...  39 us
    reshape x6, local copies, waits for them, and re-layouts, join_grads(): block.reshape(parts, -1, 128)  34.1 us
    dot_general x4, matrix products, one_group(): jnp.einsum('qhd,khd->hqk', grad_group, value_group, preferred_element_typ...  33.4 us
  transfers between devices with their start and end apart: 6, of which 4 were waited for; matrix products, arithmetic and copies ran while one was open for 41% of the time, Pallas kernels for 0%

profile of v3, /device:TPU:0, one launch (start us, length us, event | category | flops | bytes accessed | tf_op | source)
XLA Modules:
  0.0 738.3 jit_solution(15109338075984197618)
XLA Ops:
  17.1 53.3 %all-gather.5.cloned.1.call-done = bf16[4,2304,128]{2,1,0:T(8,128)(2,1)} async-done(((bf16[1,2304,128]{2,1,0:T(8,128)(2,1)}), bf16[4,2304,128]{2,1,0:T(8,128)(2,1)}) %all-gather.5.cloned.1.call-update) | async-done | bytes 2359312 | tf_op jit(solution)/shard_map/all_gather | solution.py:134
  76.3 14.7 %all-gather.1 = f32[4,1,1152]{2,1,0:T(1,128)S(1)} all-gather(f32[1,1,1152]{2,1,0:T(1,128)S(1)} %reshape.447), channel_id=2, replica_groups=mesh['dp'=8,'tensor'=4] {'tensor'}, dimensions={0}, use_global_device_ids=true | all-gather | bytes 23040 | tf_op jit(solution)/shard_map/all_gather | solution.py:229
  96.2 12.2 %copy_bitcast_fusion = (bf16[4,294912]{1,0:T(4,128)(2,1)S(1)}, bf16[4,294912]{1,0:T(4,128)(2,1)S(1)}) fusion(bf16[1,4,2304,128]{3,2,1,0:T(8,128)(2,1)S(1)} %get-tuple-element.258, bf16[1,4,2304,128]{3,2,1,0:T(8,128)(2,1)S(1)} %get-tuple-element.259), kind=kLoop, calls=%fused_computation.114 | loop fusion | bytes 9437184 | tf_op jit(solution)/shard_map/reshape | solution.py:139
  143.4 17.7 %all-gather.7.cloned.1.call-done = bf16[4,4608,128]{2,1,0:T(8,128)(2,1)} async-done(((bf16[1,4608,128]{2,1,0:T(8,128)(2,1)}), bf16[4,4608,128]{2,1,0:T(8,128)(2,1)}) %all-gather.7.cloned.1.call-update) | async-done | bytes 4718608 | tf_op jit(solution)/shard_map/all_gather | solution.py:134
  162.4 60.5 %while.26 = (s32[]{:T(128)}, bf16[4,1024,3,64]{1,3,2,0:T(8,128)(2,1)}, f32[4,3,1024]{2,1,0:T(4,128)}, bf16[4,1024,3,64]{1,3,2,0:T(8,128)(2,1)}, s32[1024]{0:T(10...) while((s32[]{:T(128)}, bf16[4,1024,3,64]{1,3,2,0:T(8,128)(2,1)}, ...), condition=%wide.region_3.4_spmd, body=%wide.region_0.3_spmd.sunk | while | flops 844297216 | bytes 47818876 | solution.py:78
  222.9 10.5 %slice_reduce_fusion.3 = (bf16[147456]{0:T(1024)(128)(2,1)}, bf16[147456]{0:T(1024)(128)(2,1)}, bf16[147456]{0:T(1024)(128)(2,1)}, bf16[147456]{0:T(1024)(128)(2,1)S(1)}) fusion(bf16[4,294912]{1,0:T(4,128)(2,1)} %copy-done.6), kind=kLoop, calls=%fused_computation.145 | loop fusion | bytes 2359296 | tf_op jit(solution)/shard_map/slice | solution.py:253
  248.6 6.5 broadcast_select_fusion.1
  259.5 9.3 %reshape_reshape_reshape.3 = bf16[3072,768]{1,0:T(8,128)(2,1)} reshape(bf16[4,4608,128]{2,1,0:T(8,128)(2,1)} %copy-done.3) | data formatting | bytes 9437184 | tf_op jit(solution)/shard_map/reshape;reshape;reshape | solution.py:155
  272.4 9.2 %reshape_reshape.11 = bf16[4,768,768]{2,1,0:T(8,128)(2,1)} reshape(bf16[4,4608,128]{2,1,0:T(8,128)(2,1)} %get-tuple-element.251) | data formatting | bytes 9437184 | tf_op jit(solution)/shard_map/reshape;reshape | solution.py:143
  281.6 6.7 copy.115
  295.0 13.2 %multiply_convert_fusion.1 = (bf16[1024,3072]{1,0:T(8,128)(2,1)S(1)}, f32[1024,3072]{1,0:T(8,128)}) fusion(f32[3072]{0:T(1024)S(1)} %copy-done.40, bf16[1024,768]{0,1:T(8,128)(2,1)} %fusion.79, bf16[768,3072]{0,1:T(8,128)(2,1)} %bitcast.292), kind=kOutput, calls=%fused_computation.74 | convolution fusion | flops 4863295488 | bytes 25178112 | tf_op jit(solution)/shard_map/dot_general | solution.py:13
  331.2 16.7 %convert_reduce_fusion = (f32[3072]{0:T(1024)}, bf16[1024,3072]{1,0:T(8,128)(2,1)S(1)}) fusion(f32[1024,3072]{1,0:T(8,128)} %get-tuple-element.283, f32[3072]{0:T(1024)S(1)} %copy-done.40, bf16[1024,768]{0,1:T(8,128)(2,1)S(1)} %get-tuple-element.253, bf16[3072,768]{1,0:T(8,128)(2,1)} %reshape_reshape_reshape.3), kind=kOutput, calls=%fused_computation.73 | convolution fusion | flops 4904186880 | bytes 25190400 | tf_op jit(solution)/shard_map/dot_general | solution.py:23
  350.7 10.8 %multiply_reduce_fusion.1 = (f32[768]{0:T(1024)}, f32[1024]{0:T(1024)S(1)}, f32[1024]{0:T(1024)S(1)}, f32[768]{0:T(1024)}, f32[1024,768]{0,1:T(8,128)}) fusion(f32[1024,768]{0,1:T(8,128)S(1)} %get-tuple-element.281, f32[1024]{0:T(1024)S(1)} %add_rsqrt_fusion.1, f32[1024]{0:T(1024)S(1)} %broadcast_multiply_fusion.5, f32[768]{0:T(1024)S(1)} %copy-done.37, ...), kind=kOutput, calls=%fused_computation.96 | convolution fusion | flops 4845989888 | bytes 22065152 | tf_op jit(solution)/shard_map/dot_general | solution.py:23
  361.4 12.3 %reshape.426 = bf16[1024,4,768]{2,1,0:T(4,128)(2,1)} reshape(bf16[1024,3072]{1,0:T(8,128)(2,1)} %copy-done.10) | data formatting | bytes 12582912 | tf_op jit(solution)/shard_map/reshape | solution.py:164
  385.3 9.1 %convert_bitcast_fusion = bf16[8,4,768,96]{2,3,1,0:T(8,128)(2,1)} fusion(bf16[1024,8,96,1]{0,2,3,1:T(8,128)(2,1)} %bitcast.298, bf16[128,4,8,768]{3,2,1,0:T(8,128)(2,1)} %bitcast.309), kind=kOutput, calls=%fused_computation.84 | convolution fusion | flops 4834197504 | bytes 12582912 | tf_op jit(solution)/shard_map/nbi,naj->abij/dot_general | solution.py:166
  394.4 7.9 %copy.120 = bf16[8,4,768,96]{3,2,1,0:T(8,128)(2,1)} copy(bf16[8,4,768,96]{2,3,1,0:T(8,128)(2,1)} %convert_bitcast_fusion) | data formatting | bytes 9437184 | tf_op jit(solution)/shard_map/nbi,naj->abij/transpose | solution.py:166
  402.3 12.9 %reshape.431 = bf16[32,576,128]{2,1,0:T(8,128)(2,1)} reshape(bf16[8,4,768,96]{3,2,1,0:T(8,128)(2,1)} %copy.120) | data formatting | bytes 9437184 | tf_op jit(solution)/shard_map/reshape | solution.py:171
  415.2 8.5 %convert_bitcast_fusion.1 = bf16[8,4,96,768]{3,2,0,1:T(8,128)(2,1)S(1)} fusion(bf16[1024,8,96,1]{0,2,1,3:T(8,128)(2,1)S(1)} %bitcast.301, bf16[1024,4,768,1]{2,1,0,3:T(4,128)(2,1)} %bitcast.277), kind=kOutput, calls=%fused_computation.85 | convolution fusion | flops 4834197504 | bytes 12582912 | tf_op jit(solution)/shard_map/nai,nbj->abij/dot_general | solution.py:166
  426.2 9.2 %reshape.428 = bf16[32,576,128]{2,1,0:T(8,128)(2,1)} reshape(bf16[8,4,96,768]{3,2,1,0:T(8,128)(2,1)} %copy.118) | data formatting | bytes 9437184 | tf_op jit(solution)/shard_map/reshape | solution.py:171
  438.8 9.3 %pad_maximum_fusion = bf16[32,1296,128]{2,1,0:T(8,128)(2,1)} fusion(bf16[32,144,128]{2,1,0:T(8,128)(2,1)S(1)} %reshape.433, bf16[32,576,128]{2,1,0:T(8,128)(2,1)} %reshape.431, bf16[32,576,128]{2,1,0:T(8,128)(2,1)S(1)} %copy-done.7), kind=kLoop, calls=%fused_computation.75 | loop fusion | flops 31850496 | bytes 21233664 | tf_op jit(solution)/shard_map/concatenate | solution.py:171
  452.9 121.4 %while.27 = (s32[]{:T(128)}, bf16[4,1024,3,64]{1,3,2,0:T(8,128)(2,1)}, bf16[4,1024,3,64]{1,3,2,0:T(8,128)(2,1)}, bf16[4,1024,3,64]{1,3,2,0:T(8,128)(2,1)S(1)}, b...) while((s32[]{:T(128)}, ...), condition=%wide.region_15.16_spmd, body=%wide.region_13.15_spmd.sunk | while | flops 2062480384 | bytes 102597752 | solution.py:112
  457.1 8.4 %multiply_reduce_fusion.7 = (f32[3,1024]{1,0:T(4,128)S(1)}, f32[3,1024,1024]{1,2,0:T(8,128)}) fusion(f32[3,1024,1024]{1,2,0:T(8,128)S(1)} %fusion.176, f32[3,1024]{1,0:T(4,128)S(1)} %dynamic-slice_bitcast_fusion.2, pred[1024,1024]{0,1:T(8,128)(4,1)S(1)} %broadcast_compare_fusion.5, bf16[4,1024,3,64]{1,3,2,0:T(8,128)(2,1)} %get-tuple-element.460, ...), kind=kOutput, calls=%fused_computation.23.clone.1 | convolution fusion | flops 418378752 | bytes 27026432 | tf_op jit(solution)/shard_map/while/body/eval_jaxpr/qhd,khd->hqk/dot_general | solution.py:89
  465.5 7.4 %multiply_convert_fusion.3 = bf16[3,1024,1024]{1,2,0:T(8,128)(2,1)S(1)} fusion(f32[3,1024,1024]{1,2,0:T(8,128)} %get-tuple-element.403, f32[3,1024,1024]{1,2,0:T(8,128)S(1)} %fusion.176, f32[3,1024]{1,0:T(4,128)S(1)} %get-tuple-element.404, f32[3,1024]{1,0:T(4,128)S(1)} %dynamic-slice_bitcast_fusion.2, pred[1024,1024]{0,1:T(8,128)(4,1)S(1)} %broadcast_compare_fusion.5), kind=kLoop, calls=%fused_computation.22.clone.1 | loop fusion | flops 18874368 | bytes 32530432 | tf_op jit(solution)/shard_map/while/body/eval_jaxpr/convert_element_type | solution.py:93
  487.8 8.4 %multiply_reduce_fusion.7 = (f32[3,1024]{1,0:T(4,128)S(1)}, f32[3,1024,1024]{1,2,0:T(8,128)}) fusion(f32[3,1024,1024]{1,2,0:T(8,128)S(1)} %fusion.176, f32[3,1024]{1,0:T(4,128)S(1)} %dynamic-slice_bitcast_fusion.2, pred[1024,1024]{0,1:T(8,128)(4,1)S(1)} %broadcast_compare_fusion.5, bf16[4,1024,3,64]{1,3,2,0:T(8,128)(2,1)} %get-tuple-element.460, ...), kind=kOutput, calls=%fused_computation.23.clone.1 | convolution fusion | flops 418378752 | bytes 27026432 | tf_op jit(solution)/shard_map/while/body/eval_jaxpr/qhd,khd->hqk/dot_general | solution.py:89
  496.1 7.1 multiply_convert_fusion.3
  518.0 8.3 %multiply_reduce_fusion.7 = (f32[3,1024]{1,0:T(4,128)S(1)}, f32[3,1024,1024]{1,2,0:T(8,128)}) fusion(f32[3,1024,1024]{1,2,0:T(8,128)S(1)} %fusion.176, f32[3,1024]{1,0:T(4,128)S(1)} %dynamic-slice_bitcast_fusion.2, pred[1024,1024]{0,1:T(8,128)(4,1)S(1)} %broadcast_compare_fusion.5, bf16[4,1024,3,64]{1,3,2,0:T(8,128)(2,1)} %get-tuple-element.460, ...), kind=kOutput, calls=%fused_computation.23.clone.1 | convolution fusion | flops 418378752 | bytes 27026432 | tf_op jit(solution)/shard_map/while/body/eval_jaxpr/qhd,khd->hqk/dot_general | solution.py:89
  526.3 7.2 multiply_convert_fusion.3
  548.3 8.3 %multiply_reduce_fusion.7 = (f32[3,1024]{1,0:T(4,128)S(1)}, f32[3,1024,1024]{1,2,0:T(8,128)}) fusion(f32[3,1024,1024]{1,2,0:T(8,128)S(1)} %fusion.176, f32[3,1024]{1,0:T(4,128)S(1)} %dynamic-slice_bitcast_fusion.2, pred[1024,1024]{0,1:T(8,128)(4,1)S(1)} %broadcast_compare_fusion.5, bf16[4,1024,3,64]{1,3,2,0:T(8,128)(2,1)} %get-tuple-element.460, ...), kind=kOutput, calls=%fused_computation.23.clone.1 | convolution fusion | flops 418378752 | bytes 27026432 | tf_op jit(solution)/shard_map/while/body/eval_jaxpr/qhd,khd->hqk/dot_general | solution.py:89
  556.6 7.1 multiply_convert_fusion.3
  574.2 14.5 %reduce-scatter.3.cloned.1.call-done = bf16[1296,128]{1,0:T(8,128)(2,1)} async-done(((bf16[41472,128]{1,0:T(8,128)(2,1)}), bf16[1296,128]{1,0:T(8,128)(2,1)}) %reduce-scatter.3.cloned.1.call-update) | async-done | bytes 331792 | tf_op jit(solution)/shard_map/reduce_scatter | solution.py:176
  654.2 40.2 %psum.7 = f32[9216]{0:T(1024)S(1)} all-reduce(f32[9216]{0:T(1024)} %constant_dynamic-update-slice_fusion), channel_id=1, replica_groups=mesh['dp'=8,'tensor'=4] {'dp','tensor'}, use_global_device_ids=true, to_apply=%region_26.27 | all-reduce | flops 9216 | bytes 73728 | tf_op jit(solution)/shard_map/psum | solution.py:315
  697.2 31.4 %reduce-scatter.5.cloned.1.call-done = bf16[432,128]{1,0:T(8,128)(2,1)} async-done(((bf16[13824,128]{1,0:T(8,128)(2,1)}), bf16[432,128]{1,0:T(8,128)(2,1)}) %reduce-scatter.5.cloned.1.call-update) | async-done | bytes 110608 | tf_op jit(solution)/shard_map/reduce_scatter | solution.py:176
  (293 shorter events, 324.9 us)
Async XLA Ops:
  7.2 86.3 %copy-start = (s32[4,1024]{1,0:T(4,128)S(1)}, s32[4,1024]{1,0:T(4,128)}, u32[]{:S(2)}) copy-start(s32[4,1024]{1,0:T(4,128)} %param.23) | copy-start | bytes 49156
  7.2 63.2 %all-gather.5.cloned.1.call-start = ((), (), s32[]{:S(2)}) async-start(), calls=%async_computation.2 | async-start | bytes 2949120 | tf_op jit(solution)/shard_map/all_gather | solution.py:134
  8.4 62.0 %copy-start.29 = (bf16[768,768]{1,0:T(8,128)(2,1)S(1)}, bf16[768,768]{1,0:T(8,128)(2,1)}, u32[]{:S(2)}) copy-start(bf16[768,768]{1,0:T(8,128)(2,1)} %param.33) | copy-start | bytes 3538948
  8.4 62.0 %copy-start.30 = (bf16[768,768]{1,0:T(8,128)(2,1)S(1)}, bf16[768,768]{1,0:T(8,128)(2,1)}, u32[]{:S(2)}) copy-start(bf16[768,768]{1,0:T(8,128)(2,1)} %param.35) | copy-start | bytes 3538948
  17.0 144.0 %all-gather.7.cloned.1.call-start = ((), (), s32[]{:S(2)}) async-start(), calls=%async_computation.3 | async-start | bytes 5898240 | tf_op jit(solution)/shard_map/all_gather | solution.py:134
  70.4 23.1 %collective-permute-start = (bf16[4,2304,128]{2,1,0:T(8,128)(2,1)}, bf16[4,2304,128]{2,1,0:T(8,128)(2,1)}, u32[]{:S(2)}, u32[]{:S(2)}) collective-permute-start(bf16[4,2304,128]{2,1,0:T(8,128)(2,1)} %all-gather.5.cloned.1.call-done), channel_id=1, source_target_pairs={{0,4},{4,0},{8,12},{12,8},{16,20},{20,16},{24,28},{28,24},{1,5},{5... | collective-permute-start | bytes 7077896 | tf_op jit(solution)/shard_map/ppermute | solution.py:135
  72.4 516.4 %reduce-scatter.3.cloned.1.call-start = ((), (), s32[]{:S(2)}) async-start(), calls=%async_computation.4 | async-start | bytes 10948608 | tf_op jit(solution)/shard_map/reduce_scatter | solution.py:176
  108.4 3.7 copy-start.6
  134.1 4.0 copy-start.18
  161.0 87.6 %collective-permute-start.1 = (bf16[4,4608,128]{2,1,0:T(8,128)(2,1)}, bf16[4,4608,128]{2,1,0:T(8,128)(2,1)}, u32[]{:S(2)}, u32[]{:S(2)}) collective-permute-start(bf16[4,4608,128]{2,1,0:T(8,128)(2,1)} %all-gather.7.cloned.1.call-done), channel_id=1, source_target_pairs={{0,4},{4,0},{8,12},{12,8},{16,20},{20,16},{24,28},{28,24},{1,5},{5... | collective-permute-start | bytes 14155784 | tf_op jit(solution)/shard_map/ppermute | solution.py:135
  163.0 4.3 copy-start.2
  178.1 4.3 copy-start.2
  193.3 4.3 copy-start.2
  208.4 4.3 copy-start.2
  222.8 18.1 %copy-start.20 = (s32[1024]{0:T(1024)}, s32[1024]{0:T(1024)S(1)}, u32[]{:S(2)}) copy-start(s32[1024]{0:T(1024)S(1)} %get-tuple-element.481) | copy-start | bytes 12292
  222.9 16.0 %copy-start.17 = (bf16[4,147456]{1,0:T(4,128)(2,1)S(1)}, bf16[4,147456]{1,0:T(4,128)(2,1)}, u32[]{:S(2)}) copy-start(bf16[4,147456]{1,0:T(4,128)(2,1)} %get-tuple-element.261) | copy-start | bytes 3538948
  233.4 7.6 %copy-start.14 = (bf16[4,1024,3,64]{1,3,2,0:T(8,128)(2,1)S(1)}, bf16[4,1024,3,64]{1,3,2,0:T(8,128)(2,1)}, u32[]{:S(2)}) copy-start(bf16[4,1024,3,64]{1,3,2,0:T(8,128)(2,1)} %get-tuple-element.117) | copy-start | bytes 4718596
  288.3 6.7 copy-start.40
  295.0 13.2 %copy-start.27 = (bf16[768,768]{1,0:T(8,128)(2,1)S(1)}, bf16[768,768]{1,0:T(8,128)(2,1)}, u32[]{:S(2)}) copy-start(bf16[768,768]{1,0:T(8,128)(2,1)} %slice.202) | copy-start | bytes 3538948
  331.2 16.8 %copy-start.22 = (bf16[1024,768]{0,1:T(8,128)(2,1)}, bf16[1024,768]{0,1:T(8,128)(2,1)S(1)}, u32[]{:S(2)}) copy-start(bf16[1024,768]{0,1:T(8,128)(2,1)S(1)} %get-tuple-element.253) | copy-start | bytes 4718596
  402.3 12.9 %copy-start.23 = (bf16[1024,768]{0,1:T(8,128)(2,1)S(1)}, bf16[1024,768]{0,1:T(8,128)(2,1)}, u32[]{:S(2)}) copy-start(bf16[1024,768]{0,1:T(8,128)(2,1)} %fusion.79) | copy-start | bytes 4718596
  448.1 280.5 %reduce-scatter.5.cloned.1.call-start = ((), (), s32[]{:S(2)}) async-start(), calls=%async_computation.5 | async-start | bytes 3649536 | tf_op jit(solution)/shard_map/reduce_scatter | solution.py:176
  607.1 7.0 copy-start.12
  629.3 3.4 copy-start.13
  629.3 3.4 copy-start.32
  638.3 93.3 %copy-start.1 = (s32[4,1024]{1,0:T(4,128)S(1)}, s32[4,1024]{1,0:T(4,128)}, u32[]{:S(2)}) copy-start(s32[4,1024]{1,0:T(4,128)} %param.23) | copy-start | bytes 49156
  641.9 4.5 copy-start.38
  641.9 5.8 copy-start.46
  641.9 7.1 copy-start.45
  641.9 8.4 %copy-start.35 = (f32[768]{0:T(1024)S(1)}, f32[768]{0:T(1024)}, u32[]{:S(2)}) copy-start(f32[768]{0:T(1024)} %get-tuple-element.201) | copy-start | bytes 9220
  641.9 9.7 %copy-start.34 = (f32[768]{0:T(1024)S(1)}, f32[768]{0:T(1024)}, u32[]{:S(2)}) copy-start(f32[768]{0:T(1024)} %get-tuple-element.200) | copy-start | bytes 9220
  641.9 11.0 %copy-start.33 = (f32[768]{0:T(1024)S(1)}, f32[768]{0:T(1024)}, u32[]{:S(2)}) copy-start(f32[768]{0:T(1024)} %get-tuple-element.210) | copy-start | bytes 9220
  (30 other events, 70.4 us)
Sparse Core Ops, SparseCore 0:
  17.1 53.1 all-gather.4
  72.5 88.4 all-gather.6
  448.3 140.4 reduce-scatter.2
  626.5 102.0 reduce-scatter.4

commit v4 on v3

--- a/solution.py
+++ b/solution.py
@@ -155,41 +155,29 @@
     return shards.reshape(count * rows, cols)
 
 
-def blocked_grad(left_side, right_side, row_axis, col_axis):
-    row_parts = lax.axis_size(row_axis)
-    col_parts = lax.axis_size(col_axis)
-    tokens, rows = left_side.shape
-    cols = right_side.shape[1]
-    left = left_side.reshape(tokens, row_parts, rows // row_parts)
-    right = right_side.reshape(tokens, col_parts, cols // col_parts)
-    spec = "nai,nbj->abij" if row_axis == "dp" else "nbi,naj->abij"
-    return jnp.einsum(spec, left, right, preferred_element_type=jnp.float32)
-
-
-def join_grads(blocks):
-    parts = blocks[0].shape[0] * blocks[0].shape[1]
-    joined = jnp.concatenate([block.reshape(parts, -1, 128) for block in blocks], axis=1)
-    return joined.reshape(-1, 128).astype(jnp.bfloat16)
-
-
-def scatter_grads(joined, blocks):
-    summed = lax.psum_scatter(joined, ("dp", "tensor"), scatter_dimension=0, tiled=True)
-    summed = summed.reshape(-1).astype(jnp.float32)
+def scatter_rows(grads):
+    joined = jnp.concatenate(grads, axis=2).astype(jnp.bfloat16)
+    rows, parts, width = joined.shape
+    summed = lax.psum_scatter(joined.reshape(rows, parts * width), "dp", scatter_dimension=0, tiled=True)
+    return summed.reshape(-1, parts, width)
+
+
+def scatter_parts(partials, grads):
+    joined = jnp.concatenate(partials, axis=2)
+    summed = lax.psum_scatter(joined, "tensor", scatter_dimension=1, tiled=True)[:, 0]
     pieces = []
     start = 0
-    for block in blocks:
-        size = block[0, 0].size
-        pieces.append(summed[start : start + size].reshape(block.shape[2:]))
-        start += size
+    for grad in grads:
+        width = grad.shape[2]
+        pieces.append(summed[:, start : start + width].astype(jnp.float32))
+        start += width
     return pieces
 
 
-def shared_blocks(vectors):
-    parts = lax.axis_size("dp") * lax.axis_size("tensor")
-    stacked = jnp.stack(vectors)
-    return stacked.reshape(len(vectors), lax.axis_size("dp"), lax.axis_size("tensor"), -1).transpose(
-        1, 2, 0, 3
-    )
+def split_tensor(grad):
+    rows, cols = grad.shape
+    parts = lax.axis_size("tensor")
+    return grad.reshape(rows, parts, cols // parts)
 
 
 def on_device(
@@ -278,10 +266,6 @@
     grad_hidden = contract_last(down_low, dw)
     grad_pre = pull_gelu(grad_hidden)[0].astype(jnp.bfloat16)
     grad_up_bias = jnp.sum(grad_pre, 0, dtype=jnp.float32)
-    ffn_blocks = [
-        blocked_grad(first_low, grad_pre, "dp", "tensor"),
-        blocked_grad(hidden_low, down_low, "tensor", "dp"),
-    ]
     first_grad = contract_last(grad_pre, uw) + grad_second
     grad_first_gain = jnp.sum(first_grad * first_unit, 0)
     grad_first_shift = jnp.sum(first_grad, 0)
@@ -289,23 +273,30 @@
     grad_output_bias = jnp.sum(attn_grad, 0)
     attn_grad_low = attn_grad.astype(jnp.bfloat16)
     grad_context = contract_last(attn_grad_low, ow).astype(jnp.bfloat16)
-    ffn_blocks.append(blocked_grad(context, attn_grad_low, "tensor", "dp"))
-    ffn_joined, grad_context = lax.optimization_barrier((join_grads(ffn_blocks), grad_context))
-    ffn_summed = scatter_grads(ffn_joined, ffn_blocks)
+    ffn_grads = [
+        split_tensor(contract_rows(first_low, grad_pre)),
+        split_tensor(contract_rows(down_low, hidden_low)),
+        split_tensor(contract_rows(attn_grad_low, context)),
+    ]
+    ffn_grads, grad_context = lax.optimization_barrier((ffn_grads, grad_context))
+    ffn_rows = scatter_rows(ffn_grads)
     query_low, key_low, value_low = attend_back(
         queries, key_side, value_proj, segment_row, log_total, grad_context
     )
-    ffn_summed, query_low, key_low, value_low = lax.optimization_barrier(
-        (ffn_summed, query_low, key_low, value_low)
+    ffn_rows, query_low, key_low, value_low = lax.optimization_barrier(
+        (ffn_rows, query_low, key_low, value_low)
     )
     grad_query_bias = jnp.sum(query_low, 0, dtype=jnp.float32)
     grad_value_bias = jnp.sum(value_low, 0, dtype=jnp.float32)
-    attn_blocks = [
-        blocked_grad(input_rows, query_low, "dp", "tensor"),
-        blocked_grad(input_rows, key_low, "dp", "tensor"),
-        blocked_grad(input_rows, value_low, "dp", "tensor"),
-    ]
-    attn_summed = scatter_grads(join_grads(attn_blocks), attn_blocks)
+    qkv_low = jnp.stack([query_low, key_low, value_low], axis=1)
+    qkv_grads = lax.dot_general(
+        input_rows, qkv_low, (((0,), (0,)), ((), ())), preferred_element_type=jnp.float32
+    )
+    qkv_grads = qkv_grads.reshape(qkv_grads.shape[0], 3, part_count, -1).transpose(0, 2, 1, 3)
+    qkv_grads = qkv_grads.reshape(qkv_grads.shape[0], part_count, -1)
+    summed = scatter_parts([ffn_rows, scatter_rows([qkv_grads])], ffn_grads + [qkv_grads])
+    ffn_summed = summed[:3]
+    attn_summed = summed[3].reshape(summed[3].shape[0], 3, -1)
     input_grad = (
         attn_grad
         + contract_last(query_low, qw)
@@ -344,18 +335,18 @@
     return (
         layer_output,
         input_grad,
-        attn_summed[0],
+        attn_summed[:, 0],
         query_bias_grad,
-        attn_summed[1],
-        attn_summed[2],
+        attn_summed[:, 1],
+        attn_summed[:, 2],
         value_bias_grad,
-        ffn_summed[2],
+        ffn_summed[2].T,
         shared[0],
         shared[1],
         shared[2],
         ffn_summed[0],
         up_bias_grad,
-        ffn_summed[1],
+        ffn_summed[1].T,
         shared[3],
         shared[4],
         shared[5],

time: 747 us -> 715 us (0.957)
  local copies, waits for them, and re-layouts: 224 us -> 205 us
    reduce_scatter x2 -> x1, waiting for transfers between devices: 45.9 us -> 0.01 us  [scatter_parts(): lax.psum_scatter(joined, 'tensor', scatter_dimension=1, tiled=True)[:, 0]]
    unnamed x4 -> x7, waiting for transfers between devices: 0.07 us -> 39.4 us
    reshape x7 -> x5, local copies, waits for them, and re-layouts: 46.4 us -> 23 us  [the longest x2 19.5 us: split_tensor(): return grad.reshape(rows, parts, cols // parts)]
    transpose x6 -> x0, local copies, waits for them, and re-layouts: 17.9 us -> none  [blocked_grad(): return jnp.einsum(spec, left, right, preferred_element_type=jnp.float32)]
    optimization_barrier x1 -> x3, local copies, waits for them, and re-layouts: 1.71 us -> 18.7 us  [on_device(): lax.optimization_barrier((ffn_grads, grad_context))]
    unnamed x125 -> x146, local copies, waits for them, and re-layouts: 43.8 us -> 55.7 us
    dot_general x6 -> x4, matrix products: 33 us -> 26 us  [the longest x3 19.8 us: contract_rows(): lax.dot_general(left_side, right_side, (((0,), (0,)), ((), ())), preferre...]
  transfers between devices with their start and end apart: 6 -> 7, of which waited for: 4 -> 3; matrix products, arithmetic and copies ran while one was open for 41% -> 41% of each run, Pallas kernels for 0% -> 0%
where the time goes in v4:
time: 715 us; the launch traced here: 708 us
  matrix products  234 us (33%)
  local copies, waits for them, and re-layouts  205 us (29%)
  waiting for transfers between devices  111 us (16%)
  other arithmetic  86.3 us (12%)
  blocking collectives  55.8 us (8%)
  between operations  14.9 us (2%)
    all_gather x2, waiting for transfers between devices, gather_shards(): gathered = lax.all_gather(mine, 'tensor', axis=0, tiled=False)  71.2 us
    unnamed x146, local copies, waits for them, and re-layouts  55.7 us
    dot_general x12, matrix products, product(): return jnp.dot(left_side, right_side, preferred_element_type=jnp.float32)  41.7 us
    psum x1, blocking collectives, on_device(): lax.psum(jnp.concatenate([grad_query_bias, grad_value_bias, grad_up_bias,...  41.2 us
    dot_general x6, matrix products, contract_last(): lax.dot_general(left_side, right_side, (((1,), (1,)), ((), ())), preferre...  39.5 us
    unnamed x7, waiting for transfers between devices  39.4 us
    dot_general x4, matrix products, one_group(): jnp.einsum('qhd,khd->hqk', grad_group, value_group, preferred_element_typ...  33.8 us
    dot_general x8, matrix products, score_group(): jnp.einsum('qhd,khd->hqk', query_group, key_group, preferred_element_type...  28.3 us
  transfers between devices with their start and end apart: 7, of which 3 were waited for; matrix products, arithmetic and copies ran while one was open for 41% of the time, Pallas kernels for 0%

profile of v4, /device:TPU:0, one launch (start us, length us, event | category | flops | bytes accessed | tf_op | source)
XLA Modules:
  0.0 707.5 jit_solution(9200310641108072067)
XLA Ops:
  17.1 53.3 %all-gather.5.cloned.1.call-done = bf16[4,2304,128]{2,1,0:T(8,128)(2,1)} async-done(((bf16[1,2304,128]{2,1,0:T(8,128)(2,1)}), bf16[4,2304,128]{2,1,0:T(8,128)(2,1)}) %all-gather.5.cloned.1.call-update) | async-done | bytes 2359312 | tf_op jit(solution)/shard_map/all_gather | solution.py:134
  76.3 14.7 %all-gather.1 = f32[4,1,1152]{2,1,0:T(1,128)S(1)} all-gather(f32[1,1,1152]{2,1,0:T(1,128)S(1)} %reshape.381), channel_id=2, replica_groups=mesh['dp'=8,'tensor'=4] {'tensor'}, dimensions={0}, use_global_device_ids=true | all-gather | bytes 23040 | tf_op jit(solution)/shard_map/all_gather | solution.py:217
  96.2 12.2 %copy_bitcast_fusion = (bf16[4,294912]{1,0:T(4,128)(2,1)S(1)}, bf16[4,294912]{1,0:T(4,128)(2,1)S(1)}) fusion(bf16[1,4,2304,128]{3,2,1,0:T(8,128)(2,1)S(1)} %get-tuple-element.257, bf16[1,4,2304,128]{3,2,1,0:T(8,128)(2,1)S(1)} %get-tuple-element.258), kind=kLoop, calls=%fused_computation.113 | loop fusion | bytes 9437184 | tf_op jit(solution)/shard_map/reshape | solution.py:139
  143.1 18.0 %all-gather.7.cloned.1.call-done = bf16[4,4608,128]{2,1,0:T(8,128)(2,1)} async-done(((bf16[1,4608,128]{2,1,0:T(8,128)(2,1)}), bf16[4,4608,128]{2,1,0:T(8,128)(2,1)}) %all-gather.7.cloned.1.call-update) | async-done | bytes 4718608 | tf_op jit(solution)/shard_map/all_gather | solution.py:134
  162.4 60.6 %while.26 = (s32[]{:T(128)}, bf16[4,1024,3,64]{1,3,2,0:T(8,128)(2,1)}, f32[4,3,1024]{2,1,0:T(4,128)}, bf16[4,1024,3,64]{1,3,2,0:T(8,128)(2,1)}, s32[1024]{0:T(10...) while((s32[]{:T(128)}, bf16[4,1024,3,64]{1,3,2,0:T(8,128)(2,1)}, ...), condition=%wide.region_3.4_spmd, body=%wide.region_0.3_spmd.sunk | while | flops 844297216 | bytes 47818876 | solution.py:78
  222.9 10.5 %slice_reduce_fusion.3 = (bf16[147456]{0:T(1024)(128)(2,1)}, bf16[147456]{0:T(1024)(128)(2,1)}, bf16[147456]{0:T(1024)(128)(2,1)}, bf16[147456]{0:T(1024)(128)(2,1)S(1)}) fusion(bf16[4,294912]{1,0:T(4,128)(2,1)} %copy-done.6), kind=kLoop, calls=%fused_computation.145 | loop fusion | bytes 2359296 | tf_op jit(solution)/shard_map/slice | solution.py:241
  246.8 6.6 broadcast_select_fusion.1
  257.8 9.2 %reshape_reshape_reshape.3 = bf16[3072,768]{1,0:T(8,128)(2,1)} reshape(bf16[4,4608,128]{2,1,0:T(8,128)(2,1)} %copy-done.3) | data formatting | bytes 9437184 | tf_op jit(solution)/shard_map/reshape;reshape;reshape | solution.py:155
  270.3 9.6 %reshape_reshape.8 = bf16[4,768,768]{2,1,0:T(8,128)(2,1)} reshape(bf16[4,4608,128]{2,1,0:T(8,128)(2,1)} %get-tuple-element.251) | data formatting | bytes 9437184 | tf_op jit(solution)/shard_map/reshape;reshape | solution.py:143
  280.0 6.7 copy.141
  293.4 13.5 %multiply_convert_fusion.1 = (bf16[1024,3072]{1,0:T(8,128)(2,1)S(1)}, f32[1024,3072]{1,0:T(8,128)}) fusion(f32[3072]{0:T(1024)S(1)} %copy-done.45, bf16[768,3072]{0,1:T(8,128)(2,1)} %bitcast.241, f32[1024,768]{0,1:T(8,128)S(1)} %get-tuple-element.282, f32[768]{0:T(1024)S(1)} %copy-done.55, f32[768]{0:T(1024)S(1)} %copy-done.47, ...), kind=kOutput, calls=%fused_computation.74 | convolution fusion | flops 4867227648 | bytes 26765312 | tf_op jit(solution)/shard_map/dot_general | solution.py:13
  327.9 7.4 %fusion.94 = bf16[768,3072]{1,0:T(8,128)(2,1)} fusion(bf16[1024,3072]{1,0:T(8,128)(2,1)S(1)} %bitcast.262, bf16[1024,768]{0,1:T(8,128)(2,1)S(1)} %copy-done.9, f32[1024,768]{0,1:T(8,128)S(1)} %get-tuple-element.286, f32[1024]{0:T(1024)S(1)} %broadcast_multiply_fusion.2, f32[1024]{0:T(1024)S(1)} %broadcast_multiply_fusion.3, f32[768]{0:T(1024)S(1)} %copy-done.42, ...), kind=kOutput, calls=%fused_computation.139 | convolution fusion | flops 4838916096 | bytes 15748096 | tf_op jit(solution)/shard_map/dot_general | solution.py:17
  335.3 18.1 %convert_reduce_fusion = (f32[3072]{0:T(1024)}, bf16[1024,3072]{1,0:T(8,128)(2,1)}) fusion(f32[1024,3072]{1,0:T(8,128)} %get-tuple-element.284, f32[3072]{0:T(1024)S(1)} %copy-done.45, bf16[3072,768]{1,0:T(8,128)(2,1)} %reshape_reshape_reshape.3, f32[1024]{0:T(1024)S(1)} %broadcast_multiply_fusion.2, f32[1024,768]{0,1:T(8,128)S(1)} %get-tuple-element.286, ...), kind=kOutput, calls=%fused_computation.73 | convolution fusion | flops 4911264768 | bytes 28355584 | tf_op jit(solution)/shard_map/dot_general | solution.py:23
  353.4 9.9 %fusion.102 = bf16[768,3072]{1,0:T(8,128)(2,1)} fusion(bf16[1024,3072]{1,0:T(8,128)(2,1)} %get-tuple-element.289, f32[1024,768]{0,1:T(8,128)S(1)} %get-tuple-element.282, f32[768]{0:T(1024)S(1)} %copy-done.55, f32[768]{0:T(1024)S(1)} %copy-done.47, f32[1024]{0:T(1024)S(1)} %add_rsqrt_fusion.1, f32[1024]{0:T(1024)S(1)} %broadcast_multiply_fusion.5), kind=kOutput, calls=%fused_computation.187 | convolution fusion | flops 4835770368 | bytes 14170112 | tf_op jit(solution)/shard_map/dot_general | solution.py:17
  363.4 12.3 %multiply_reduce_fusion.1 = (f32[768]{0:T(1024)}, f32[1024]{0:T(1024)S(1)}, f32[1024]{0:T(1024)S(1)}, f32[768]{0:T(1024)}, f32[1024,768]{0,1:T(8,128)}) fusion(f32[1024,768]{0,1:T(8,128)S(1)} %get-tuple-element.282, f32[1024]{0:T(1024)S(1)} %add_rsqrt_fusion.1, f32[1024]{0:T(1024)S(1)} %broadcast_multiply_fusion.5, f32[768]{0:T(1024)S(1)} %copy-done.47, ...), kind=kOutput, calls=%fused_computation.94 | convolution fusion | flops 4845989888 | bytes 22065152 | tf_op jit(solution)/shard_map/dot_general | solution.py:23
  375.7 9.7 %reshape.368 = bf16[768,4,768]{2,1,0:T(4,128)(2,1)} reshape(bf16[768,3072]{1,0:T(8,128)(2,1)} %fusion.102) | data formatting | bytes 9437184 | tf_op jit(solution)/shard_map/reshape | solution.py:180
  385.4 9.7 %reshape.369 = bf16[768,4,768]{2,1,0:T(4,128)(2,1)} reshape(bf16[768,3072]{1,0:T(8,128)(2,1)} %fusion.94) | data formatting | bytes 9437184 | tf_op jit(solution)/shard_map/reshape | solution.py:180
  402.9 8.5 %copy.150 = bf16[768,4,768]{0,2,1:T(8,128)(2,1)} copy(bf16[768,4,768]{2,1,0:T(4,128)(2,1)} %reshape.369) | data formatting | bytes 9437184 | tf_op jit(solution)/shard_map/optimization_barrier | solution.py:281
  411.3 8.6 %copy.149 = bf16[768,4,768]{0,2,1:T(8,128)(2,1)} copy(bf16[768,4,768]{2,1,0:T(4,128)(2,1)} %reshape.368) | data formatting | bytes 9437184 | tf_op jit(solution)/shard_map/optimization_barrier | solution.py:281
  419.9 9.2 %pad_maximum_fusion = bf16[768,4,1728]{0,2,1:T(8,128)(2,1)} fusion(bf16[768,4,192]{0,2,1:T(8,128)(2,1)S(1)} %copy-done.32, bf16[768,4,768]{0,2,1:T(8,128)(2,1)} %copy.150, bf16[768,4,768]{0,2,1:T(8,128)(2,1)} %copy.149), kind=kLoop, calls=%fused_computation.75 | loop fusion | flops 31850496 | bytes 21233664 | tf_op jit(solution)/shard_map/concatenate | solution.py:159
  429.2 14.3 %copy.185 = bf16[768,6912]{1,0:T(8,128)(2,1)} copy(bf16[768,6912]{0,1:T(8,128)(2,1)} %bitcast.220) | data formatting | bytes 21233664
  448.1 120.7 %while.27 = (s32[]{:T(128)}, bf16[4,1024,3,64]{1,3,2,0:T(8,128)(2,1)}, bf16[4,1024,3,64]{1,3,2,0:T(8,128)(2,1)}, bf16[4,1024,3,64]{1,3,2,0:T(8,128)(2,1)S(1)}, b...) while((s32[]{:T(128)}, ...), condition=%wide.region_15.16_spmd, body=%wide.region_13.15_spmd.sunk | while | flops 2062480384 | bytes 102597752 | solution.py:112
  452.4 8.9 %multiply_reduce_fusion.7 = (f32[3,1024]{1,0:T(4,128)S(1)}, f32[3,1024,1024]{1,2,0:T(8,128)}) fusion(f32[3,1024,1024]{1,2,0:T(8,128)S(1)} %fusion.178, f32[3,1024]{1,0:T(4,128)S(1)} %dynamic-slice_bitcast_fusion.2, pred[1024,1024]{0,1:T(8,128)(4,1)S(1)} %broadcast_compare_fusion.5, bf16[4,1024,3,64]{1,3,2,0:T(8,128)(2,1)} %get-tuple-element.461, ...), kind=kOutput, calls=%fused_computation.23.clone.1 | convolution fusion | flops 418378752 | bytes 27026432 | tf_op jit(solution)/shard_map/while/body/eval_jaxpr/qhd,khd->hqk/dot_general | solution.py:89
  461.3 6.9 multiply_convert_fusion.3
  483.0 8.3 %multiply_reduce_fusion.7 = (f32[3,1024]{1,0:T(4,128)S(1)}, f32[3,1024,1024]{1,2,0:T(8,128)}) fusion(f32[3,1024,1024]{1,2,0:T(8,128)S(1)} %fusion.178, f32[3,1024]{1,0:T(4,128)S(1)} %dynamic-slice_bitcast_fusion.2, pred[1024,1024]{0,1:T(8,128)(4,1)S(1)} %broadcast_compare_fusion.5, bf16[4,1024,3,64]{1,3,2,0:T(8,128)(2,1)} %get-tuple-element.461, ...), kind=kOutput, calls=%fused_computation.23.clone.1 | convolution fusion | flops 418378752 | bytes 27026432 | tf_op jit(solution)/shard_map/while/body/eval_jaxpr/qhd,khd->hqk/dot_general | solution.py:89
  491.4 7.0 multiply_convert_fusion.3
  513.1 8.3 %multiply_reduce_fusion.7 = (f32[3,1024]{1,0:T(4,128)S(1)}, f32[3,1024,1024]{1,2,0:T(8,128)}) fusion(f32[3,1024,1024]{1,2,0:T(8,128)S(1)} %fusion.178, f32[3,1024]{1,0:T(4,128)S(1)} %dynamic-slice_bitcast_fusion.2, pred[1024,1024]{0,1:T(8,128)(4,1)S(1)} %broadcast_compare_fusion.5, bf16[4,1024,3,64]{1,3,2,0:T(8,128)(2,1)} %get-tuple-element.461, ...), kind=kOutput, calls=%fused_computation.23.clone.1 | convolution fusion | flops 418378752 | bytes 27026432 | tf_op jit(solution)/shard_map/while/body/eval_jaxpr/qhd,khd->hqk/dot_general | solution.py:89
  521.4 7.0 multiply_convert_fusion.3
  543.1 8.2 %multiply_reduce_fusion.7 = (f32[3,1024]{1,0:T(4,128)S(1)}, f32[3,1024,1024]{1,2,0:T(8,128)}) fusion(f32[3,1024,1024]{1,2,0:T(8,128)S(1)} %fusion.178, f32[3,1024]{1,0:T(4,128)S(1)} %dynamic-slice_bitcast_fusion.2, pred[1024,1024]{0,1:T(8,128)(4,1)S(1)} %broadcast_compare_fusion.5, bf16[4,1024,3,64]{1,3,2,0:T(8,128)(2,1)} %get-tuple-element.461, ...), kind=kOutput, calls=%fused_computation.23.clone.1 | convolution fusion | flops 418378752 | bytes 27026432 | tf_op jit(solution)/shard_map/while/body/eval_jaxpr/qhd,khd->hqk/dot_general | solution.py:89
  551.3 6.9 multiply_convert_fusion.3
  593.6 39.3 %reduce-scatter.12.cloned.1.call-done = bf16[96,2304]{1,0:T(8,128)(2,1)} async-done(((bf16[768,2304]{1,0:T(8,128)(2,1)}), bf16[96,2304]{1,0:T(8,128)(2,1)}) %reduce-scatter.12.cloned.1.call-update) | async-done | bytes 442384
  650.9 41.2 %psum.7 = f32[9216]{0:T(1024)S(1)} all-reduce(f32[9216]{0:T(1024)S(1)} %constant_dynamic-update-slice_fusion), channel_id=1, replica_groups=mesh['dp'=8,'tensor'=4] {'dp','tensor'}, use_global_device_ids=true, to_apply=%region_27.28 | all-reduce | flops 9216 | bytes 73728 | tf_op jit(solution)/shard_map/psum | solution.py:306
  (304 shorter events, 288.1 us)
Async XLA Ops:
  7.2 86.3 %copy-start = (s32[4,1024]{1,0:T(4,128)S(1)}, s32[4,1024]{1,0:T(4,128)}, u32[]{:S(2)}) copy-start(s32[4,1024]{1,0:T(4,128)} %param.23) | copy-start | bytes 49156
  7.2 63.2 %all-gather.5.cloned.1.call-start = ((), (), s32[]{:S(2)}) async-start(), calls=%async_computation.3 | async-start | bytes 2949120 | tf_op jit(solution)/shard_map/all_gather | solution.py:134
  8.4 62.0 %copy-start.28 = (bf16[768,768]{1,0:T(8,128)(2,1)S(1)}, bf16[768,768]{1,0:T(8,128)(2,1)}, u32[]{:S(2)}) copy-start(bf16[768,768]{1,0:T(8,128)(2,1)} %param.33) | copy-start | bytes 3538948
  8.4 62.0 %copy-start.29 = (bf16[768,768]{1,0:T(8,128)(2,1)S(1)}, bf16[768,768]{1,0:T(8,128)(2,1)}, u32[]{:S(2)}) copy-start(bf16[768,768]{1,0:T(8,128)(2,1)} %param.35) | copy-start | bytes 3538948
  17.0 144.0 %all-gather.7.cloned.1.call-start = ((), (), s32[]{:S(2)}) async-start(), calls=%async_computation.4 | async-start | bytes 5898240 | tf_op jit(solution)/shard_map/all_gather | solution.py:134
  70.4 23.1 %collective-permute-start = (bf16[4,2304,128]{2,1,0:T(8,128)(2,1)}, bf16[4,2304,128]{2,1,0:T(8,128)(2,1)}, u32[]{:S(2)}, u32[]{:S(2)}) collective-permute-start(bf16[4,2304,128]{2,1,0:T(8,128)(2,1)} %all-gather.5.cloned.1.call-done), channel_id=1, source_target_pairs={{0,4},{4,0},{8,12},{12,8},{16,20},{20,16},{24,28},{28,24},{1,5},{5... | collective-permute-start | bytes 7077896 | tf_op jit(solution)/shard_map/ppermute | solution.py:135
  72.4 496.4 %reduce-scatter.10.cloned.1.call-start = ((), (), s32[]{:S(2)}) async-start(), calls=%async_computation.6 | async-start | bytes 11943936
  74.6 65.9 %copy-start.16 = (bf16[1024,768]{1,0:T(8,128)(2,1)}, bf16[1024,768]{1,0:T(8,128)(2,1)S(1)}, u32[]{:S(2)}) copy-start(bf16[1024,768]{1,0:T(8,128)(2,1)S(1)} %get-tuple-element.293) | copy-start | bytes 4718596
  161.0 85.7 %collective-permute-start.1 = (bf16[4,4608,128]{2,1,0:T(8,128)(2,1)}, bf16[4,4608,128]{2,1,0:T(8,128)(2,1)}, u32[]{:S(2)}, u32[]{:S(2)}) collective-permute-start(bf16[4,4608,128]{2,1,0:T(8,128)(2,1)} %all-gather.7.cloned.1.call-done), channel_id=1, source_target_pairs={{0,4},{4,0},{8,12},{12,8},{16,20},{20,16},{24,28},{28,24},{1,5},{5... | collective-permute-start | bytes 14155784 | tf_op jit(solution)/shard_map/ppermute | solution.py:135
  163.0 4.3 copy-start.2
  178.2 4.3 copy-start.2
  193.3 4.3 copy-start.2
  208.5 4.3 copy-start.2
  222.9 16.1 %copy-start.19 = (bf16[4,147456]{1,0:T(4,128)(2,1)S(1)}, bf16[4,147456]{1,0:T(4,128)(2,1)}, u32[]{:S(2)}) copy-start(bf16[4,147456]{1,0:T(4,128)(2,1)} %get-tuple-element.260) | copy-start | bytes 3538948
  233.5 7.6 %copy-start.14 = (bf16[4,1024,3,64]{1,3,2,0:T(8,128)(2,1)S(1)}, bf16[4,1024,3,64]{1,3,2,0:T(8,128)(2,1)}, u32[]{:S(2)}) copy-start(bf16[4,1024,3,64]{1,3,2,0:T(8,128)(2,1)} %get-tuple-element.117) | copy-start | bytes 4718596
  286.7 6.7 copy-start.45
  286.7 6.7 copy-start.47
  286.7 6.7 copy-start.55
  293.4 13.5 %copy-start.26 = (bf16[768,768]{1,0:T(8,128)(2,1)S(1)}, bf16[768,768]{1,0:T(8,128)(2,1)}, u32[]{:S(2)}) copy-start(bf16[768,768]{1,0:T(8,128)(2,1)} %slice.178) | copy-start | bytes 3538948
  316.4 11.4 %slice-start = ((s8[6291456]{0:T(1024)(128)(4,1)}), s8[4194304]{0:T(1024)(128)(4,1)S(1)}, s32[]{:S(2)}) async-start(s8[6291456]{0:T(1024)(128)(4,1)} %bitcast.261), calls=%async_computation.8 | async-start | bytes 8388608
  319.8 8.0 %slice-start.1 = ((s8[6291456]{0:T(1024)(128)(4,1)}), s8[2097152]{0:T(1024)(128)(4,1)S(1)}, s32[]{:S(2)}) async-start(s8[6291456]{0:T(1024)(128)(4,1)} %bitcast.261), calls=%async_computation.9 | async-start | bytes 4194304
  324.4 38.9 %copy-start.4 = (f32[1024,768]{0,1:T(8,128)}, f32[1024,768]{0,1:T(8,128)S(1)}, u32[]{:S(2)}) copy-start(f32[1024,768]{0,1:T(8,128)S(1)} %get-tuple-element.286) | copy-start | bytes 9437188
  324.5 38.8 %copy-start.33 = (f32[1024]{0:T(1024)}, f32[1024]{0:T(1024)S(1)}, u32[]{:S(2)}) copy-start(f32[1024]{0:T(1024)S(1)} %broadcast_multiply_fusion.4) | copy-start | bytes 12292
  327.0 36.3 %copy-start.35 = (f32[1024]{0:T(1024)}, f32[1024]{0:T(1024)S(1)}, u32[]{:S(2)}) copy-start(f32[1024]{0:T(1024)S(1)} %add_rsqrt_fusion) | copy-start | bytes 12292
  327.8 35.5 %copy-start.38 = (f32[1024]{0:T(1024)}, f32[1024]{0:T(1024)S(1)}, u32[]{:S(2)}) copy-start(f32[1024]{0:T(1024)S(1)} %broadcast_multiply_fusion.2) | copy-start | bytes 12292
  327.8 35.5 %copy-start.40 = (f32[1024]{0:T(1024)}, f32[1024]{0:T(1024)S(1)}, u32[]{:S(2)}) copy-start(f32[1024]{0:T(1024)S(1)} %broadcast_multiply_fusion.3) | copy-start | bytes 12292
  411.3 8.6 %copy-start.32 = (bf16[768,4,192]{0,2,1:T(8,128)(2,1)S(1)}, bf16[768,4,192]{0,2,1:T(8,128)(2,1)}, u32[]{:S(2)}) copy-start(bf16[768,4,192]{0,2,1:T(8,128)(2,1)} %fusion.88) | copy-start | bytes 3538948
  443.5 189.4 %reduce-scatter.12.cloned.1.call-start = ((), (), s32[]{:S(2)}) async-start(), calls=%async_computation.7 | async-start | bytes 3981312
  568.8 11.7 %copy-start.7 = (bf16[4,1024,3,64]{1,3,2,0:T(8,128)(2,1)}, bf16[4,1024,3,64]{1,3,2,0:T(8,128)(2,1)S(1)}, u32[]{:S(2)}) copy-start(bf16[4,1024,3,64]{1,3,2,0:T(8,128)(2,1)S(1)} %get-tuple-element.125) | copy-start | bytes 4718596
  584.8 109.2 %reduce-scatter.8.cloned.1.call-start = ((), (), s32[]{:S(2)}) async-start(), calls=%async_computation.5 | async-start | bytes 2211840 | tf_op jit(solution)/shard_map/reduce_scatter | solution.py:167
  590.8 43.8 %copy-start.18 = (bf16[96,4,1728]{2,1,0:T(4,128)(2,1)S(1)}, bf16[96,4,1728]{2,1,0:T(4,128)(2,1)}, u32[]{:S(2)}) copy-start(bf16[96,4,1728]{2,1,0:T(4,128)(2,1)} %copy.182) | copy-start | bytes 3981316
  646.6 54.3 %copy-start.1 = (s32[4,1024]{1,0:T(4,128)S(1)}, s32[4,1024]{1,0:T(4,128)}, u32[]{:S(2)}) copy-start(s32[4,1024]{1,0:T(4,128)} %param.23) | copy-start | bytes 49156
  (38 other events, 89.0 us)
Sparse Core Ops, SparseCore 0:
  17.1 53.1 all-gather.4
  72.5 88.4 all-gather.6
  443.6 80.8 reduce-scatter.9
  585.0 47.8 reduce-scatter.11
  637.2 38.7 reduce-scatter.7

commit v5 on v4

--- a/solution.py
+++ b/solution.py
@@ -125,59 +125,46 @@
 def gather_shards(first_pieces, second_pieces):
     dp_count = lax.axis_size("dp")
     core = lax.rem(lax.axis_index("dp"), 2)
-
-    def flat(pieces):
-        return jnp.concatenate([piece.reshape(-1) for piece in pieces]).reshape(-1, 128)
-
-    first, second = flat(first_pieces), flat(second_pieces)
+    first, second = jnp.stack(first_pieces), jnp.stack(second_pieces)
     mine = jnp.where(core == 0, first, second)
     gathered = lax.all_gather(mine, "tensor", axis=0, tiled=False)
     other = lax.ppermute(gathered, "dp", perm=[(i, i ^ 1) for i in range(dp_count)])
     halves = (jnp.where(core == 0, gathered, other), jnp.where(core == 0, other, gathered))
-    shards = []
-    for half, pieces in zip(halves, (first_pieces, second_pieces)):
-        half = half.reshape(half.shape[0], -1)
-        start = 0
-        for piece in pieces:
-            size = piece.size
-            shards.append(half[:, start : start + size].reshape((half.shape[0],) + piece.shape))
-            start += size
-    return shards
-
-
-def join_columns(shards):
-    count, rows, cols = shards.shape
-    return shards.transpose(1, 0, 2).reshape(rows, count * cols)
-
-
-def join_rows(shards):
-    count, rows, cols = shards.shape
-    return shards.reshape(count * rows, cols)
-
-
-def scatter_rows(grads):
-    joined = jnp.concatenate(grads, axis=2).astype(jnp.bfloat16)
-    rows, parts, width = joined.shape
-    summed = lax.psum_scatter(joined.reshape(rows, parts * width), "dp", scatter_dimension=0, tiled=True)
-    return summed.reshape(-1, parts, width)
-
-
-def scatter_parts(partials, grads):
-    joined = jnp.concatenate(partials, axis=2)
+    return [half[:, index] for half in halves for index in range(half.shape[1])]
+
+
+def by_parts(grads):
+    parts = lax.axis_size("tensor")
+    columns = []
+    for part in range(parts):
+        used = 0
+        for grad in grads:
+            width = grad.shape[1] // parts
+            columns.append(grad[:, part * width : (part + 1) * width].astype(jnp.bfloat16))
+            used += width
+        if used % 128:
+            columns.append(jnp.zeros((grads[0].shape[0], 128 - used % 128), jnp.bfloat16))
+    return jnp.concatenate(columns, axis=1)
+
+
+def scatter_rows(joined):
+    return lax.psum_scatter(joined, "dp", scatter_dimension=0, tiled=True)
+
+
+def scatter_parts(partials, widths):
+    parts = lax.axis_size("tensor")
+    joined = jnp.concatenate(
+        [partial.reshape(partial.shape[0], parts, -1) for partial in partials], axis=2
+    )
     summed = lax.psum_scatter(joined, "tensor", scatter_dimension=1, tiled=True)[:, 0]
     pieces = []
     start = 0
-    for grad in grads:
-        width = grad.shape[2]
-        pieces.append(summed[:, start : start + width].astype(jnp.float32))
-        start += width
+    for partial, group in zip(partials, widths):
+        for width in group:
+            pieces.append(summed[:, start : start + width].astype(jnp.float32))
+            start += width
+        start += partial.shape[1] // parts - sum(group)
     return pieces
-
-
-def split_tensor(grad):
-    rows, cols = grad.shape
-    parts = lax.axis_size("tensor")
-    return grad.reshape(rows, parts, cols // parts)
 
 
 def on_device(
@@ -210,48 +197,48 @@
         jnp.float32
     )
 
-    q_sh, k_sh, v_sh, o_sh = gather_shards(
-        [query_weight, key_weight], [value_weight, output_weight]
+    qt_sh, kt_sh, vt_sh, o_sh = gather_shards(
+        [query_weight.T, key_weight.T], [value_weight.T, output_weight]
     )
     u_sh, d_sh = gather_shards([up_weight], [down_weight])
     bias_sh = lax.all_gather(
         jnp.concatenate([query_bias, value_bias, up_bias]), "tensor", axis=0, tiled=False
     )
-    qw = join_columns(q_sh)
-    kw = join_columns(k_sh)
-    vw = join_columns(v_sh)
-    ow = join_rows(o_sh)
-    uw = join_columns(u_sh)
-    dw = join_rows(d_sh)
     head_width = query_bias.shape[0]
     qb = bias_sh[:, :head_width].reshape(-1)
     vb = bias_sh[:, head_width : 2 * head_width].reshape(-1)
-    ub = bias_sh[:, 2 * head_width :].reshape(-1)
+    ub = bias_sh[:, 2 * head_width :]
+    width = qt_sh.shape[2]
+    qt_full = qt_sh.reshape(-1, width)
+    kt_full = kt_sh.reshape(-1, width)
+    vt_full = vt_sh.reshape(-1, width)
 
     input_f32 = input_rows.astype(jnp.float32)
-    queries = (product(input_rows, qw) + qb).astype(jnp.bfloat16)
-    key_side = product(input_rows, kw).astype(jnp.bfloat16)
-    value_proj = (product(input_rows, vw) + vb).astype(jnp.bfloat16)
+    queries = (contract_last(input_rows, qt_full) + qb).astype(jnp.bfloat16)
+    key_side = contract_last(input_rows, kt_full).astype(jnp.bfloat16)
+    value_proj = (contract_last(input_rows, vt_full) + vb).astype(jnp.bfloat16)
     context, log_total = attend(queries, key_side, value_proj, segment_row)
 
-    group_width = ow.shape[0] // part_count
+    group_width = o_sh.shape[1]
     attn_total = input_f32
     for member in range(part_count):
         cols = slice(member * group_width, (member + 1) * group_width)
-        attn_total = attn_total + product(context[:, cols], ow[cols]).astype(
+        attn_total = attn_total + product(context[:, cols], o_sh[member]).astype(
             jnp.bfloat16
         ).astype(jnp.float32)
     first_in = attn_total + output_bias
     first_out, first_unit, first_inv = normalize(first_in, first_gain, first_shift)
     first_low = first_out.astype(jnp.bfloat16)
-    pre_act = product(first_low, uw) + ub
-    gelu_out, pull_gelu = jax.vjp(gelu_tanh, pre_act)
-    hidden_low = gelu_out.astype(jnp.bfloat16)
-    unit_width = dw.shape[0] // part_count
     second_in = first_out
+    pulls = []
+    hidden_parts = []
     for member in range(part_count):
-        units = slice(member * unit_width, (member + 1) * unit_width)
-        second_in = second_in + product(hidden_low[:, units], dw[units]).astype(
+        pre_part = product(first_low, u_sh[member]) + ub[member]
+        gelu_out, pull_gelu = jax.vjp(gelu_tanh, pre_part)
+        pulls.append(pull_gelu)
+        hidden_part = gelu_out.astype(jnp.bfloat16)
+        hidden_parts.append(hidden_part)
+        second_in = second_in + product(hidden_part, d_sh[member]).astype(
             jnp.bfloat16
         ).astype(jnp.float32)
     second_in = second_in + down_bias
@@ -263,23 +250,32 @@
     grad_second_shift = jnp.sum(grad_out, 0)
     grad_down_bias = jnp.sum(grad_second, 0)
     down_low = grad_second.astype(jnp.bfloat16)
-    grad_hidden = contract_last(down_low, dw)
-    grad_pre = pull_gelu(grad_hidden)[0].astype(jnp.bfloat16)
+    first_grad = grad_second
+    grad_pre_parts = []
+    for member in range(part_count):
+        grad_hidden = contract_last(down_low, d_sh[member])
+        grad_pre = pulls[member](grad_hidden)[0].astype(jnp.bfloat16)
+        grad_pre_parts.append(grad_pre)
+        first_grad = first_grad + contract_last(grad_pre, u_sh[member])
+    grad_pre = jnp.concatenate(grad_pre_parts, axis=1)
+    hidden_low = jnp.concatenate(hidden_parts, axis=1)
     grad_up_bias = jnp.sum(grad_pre, 0, dtype=jnp.float32)
-    first_grad = contract_last(grad_pre, uw) + grad_second
     grad_first_gain = jnp.sum(first_grad * first_unit, 0)
     grad_first_shift = jnp.sum(first_grad, 0)
     attn_grad = normalize_back(first_grad, first_unit, first_inv, first_gain)
     grad_output_bias = jnp.sum(attn_grad, 0)
     attn_grad_low = attn_grad.astype(jnp.bfloat16)
-    grad_context = contract_last(attn_grad_low, ow).astype(jnp.bfloat16)
+    grad_context = contract_last(attn_grad_low, o_sh.reshape(-1, o_sh.shape[2])).astype(
+        jnp.bfloat16
+    )
     ffn_grads = [
-        split_tensor(contract_rows(first_low, grad_pre)),
-        split_tensor(contract_rows(down_low, hidden_low)),
-        split_tensor(contract_rows(attn_grad_low, context)),
+        contract_rows(first_low, grad_pre),
+        contract_rows(down_low, hidden_low),
+        contract_rows(attn_grad_low, context),
     ]
-    ffn_grads, grad_context = lax.optimization_barrier((ffn_grads, grad_context))
-    ffn_rows = scatter_rows(ffn_grads)
+    ffn_widths = [grad.shape[1] // part_count for grad in ffn_grads]
+    ffn_joined, grad_context = lax.optimization_barrier((by_parts(ffn_grads), grad_context))
+    ffn_rows = scatter_rows(ffn_joined)
     query_low, key_low, value_low = attend_back(
         queries, key_side, value_proj, segment_row, log_total, grad_context
     )
@@ -289,19 +285,19 @@
     grad_query_bias = jnp.sum(query_low, 0, dtype=jnp.float32)
     grad_value_bias = jnp.sum(value_low, 0, dtype=jnp.float32)
     qkv_low = jnp.stack([query_low, key_low, value_low], axis=1)
-    qkv_grads = lax.dot_general(
-        input_rows, qkv_low, (((0,), (0,)), ((), ())), preferred_element_type=jnp.float32
-    )
-    qkv_grads = qkv_grads.reshape(qkv_grads.shape[0], 3, part_count, -1).transpose(0, 2, 1, 3)
-    qkv_grads = qkv_grads.reshape(qkv_grads.shape[0], part_count, -1)
-    summed = scatter_parts([ffn_rows, scatter_rows([qkv_grads])], ffn_grads + [qkv_grads])
+    qkv_low = qkv_low.reshape(row_len, 3, part_count, -1).transpose(0, 2, 1, 3)
+    qkv_grads = contract_rows(input_rows, qkv_low.reshape(row_len, -1)).astype(jnp.bfloat16)
+    qkv_widths = [qkv_grads.shape[1] // part_count]
+    summed = scatter_parts(
+        [ffn_rows, scatter_rows(qkv_grads)], [ffn_widths, qkv_widths]
+    )
     ffn_summed = summed[:3]
     attn_summed = summed[3].reshape(summed[3].shape[0], 3, -1)
     input_grad = (
         attn_grad
-        + contract_last(query_low, qw)
-        + contract_last(key_low, kw)
-        + contract_last(value_low, vw)
+        + product(query_low, qt_full)
+        + product(key_low, kt_full)
+        + product(value_low, vt_full)
     )
     small = lax.psum(
         jnp.concatenate(

time: 715 us -> 619 us (0.87)
  local copies, waits for them, and re-layouts: 205 us -> 64.6 us
  waiting for transfers between devices: 111 us -> 152 us
    reduce_scatter x0 -> x2, waiting for transfers between devices: none -> 42.8 us  [scatter_rows(): return lax.psum_scatter(joined, 'dp', scatter_dimension=0, tiled=True)]
    unnamed x7 -> x5, waiting for transfers between devices: 39.4 us -> 0.08 us
    all_gather x2, waiting for transfers between devices: 71.2 us -> 109 us  [gather_shards(): gathered = lax.all_gather(mine, 'tensor', axis=0, tiled=False)]
    reshape x9 -> x2, local copies, waits for them, and re-layouts: 43.3 us -> 5.73 us  [scatter_parts(): partial.reshape(partial.shape[0], parts, -1)]
    unnamed x146 -> x144, local copies, waits for them, and re-layouts: 55.7 us -> 22 us
    slice x13 -> x6, local copies, waits for them, and re-layouts: 35.6 us -> 11.8 us  [the longest x3 8.69 us: by_parts(): grad[:, part * width:(part + 1) * width].astype(jnp.bfloat16)]
    another operation x7 -> x5, local copies, waits for them, and re-layouts: 25.2 us -> 3.11 us  [the longest x2 11.3 us: join_rows(): return shards.reshape(count * rows, cols)]
    optimization_barrier x3 -> x1, local copies, waits for them, and re-layouts: 18.7 us -> 1.81 us  [on_device(): lax.optimization_barrier((by_parts(ffn_grads), grad_context))]
  transfers between devices with their start and end apart: 7 -> 7, of which waited for: 3 -> 3; matrix products, arithmetic and copies ran while one was open for 41% -> 38% of each run, Pallas kernels for 0% -> 0%
where the time goes in v5:
time: 619 us; the launch traced here: 608 us
  matrix products  235 us (38%)
  waiting for transfers between devices  152 us (25%)
  other arithmetic  83.9 us (14%)
  local copies, waits for them, and re-layouts  64.6 us (10%)
  blocking collectives  56.2 us (9%)
  between operations  15.2 us (2%)
    all_gather x2, waiting for transfers between devices, gather_shards(): gathered = lax.all_gather(mine, 'tensor', axis=0, tiled=False)  109 us
    psum x1, blocking collectives, on_device(): lax.psum(jnp.concatenate([grad_query_bias, grad_value_bias, grad_up_bias,...  43 us
    reduce_scatter x2, waiting for transfers between devices, scatter_rows(): return lax.psum_scatter(joined, 'dp', scatter_dimension=0, tiled=True)  42.8 us
    dot_general x12, matrix products, contract_last(): lax.dot_general(left_side, right_side, (((1,), (1,)), ((), ())), preferre...  41.1 us
    dot_general x15, matrix products, product(): return jnp.dot(left_side, right_side, preferred_element_type=jnp.float32)  39.7 us
    dot_general x4, matrix products, one_group(): jnp.einsum('qhd,khd->hqk', grad_group, value_group, preferred_element_typ...  32.6 us
    dot_general x4, matrix products, contract_rows(): lax.dot_general(left_side, right_side, (((0,), (0,)), ((), ())), preferre...  29.8 us
    dot_general x8, matrix products, score_group(): jnp.einsum('qhd,khd->hqk', query_group, key_group, preferred_element_type...  29.6 us
  transfers between devices with their start and end apart: 7, of which 3 were waited for; matrix products, arithmetic and copies ran while one was open for 38% of the time, Pallas kernels for 0%

profile of v5, /device:TPU:0, one launch (start us, length us, event | category | flops | bytes accessed | tf_op | source)
XLA Modules:
  0.0 608.0 jit_solution(17808393045407284383)
XLA Ops:
  11.0 52.5 %all-gather.6.cloned.1.call-done = bf16[4,2,192,768]{3,2,1,0:T(8,128)(2,1)} async-done(((bf16[1,2,192,768]{3,2,1,0:T(8,128)(2,1)}), bf16[4,2,192,768]{3,2,1,0:T(8,128)(2,1)}) %all-gather.6.cloned.1.call-update) | async-done | bytes 2359312 | tf_op jit(solution)/shard_map/all_gather | solution.py:130
  63.5 13.1 %all-gather.2 = f32[4,1,1152]{2,1,0:T(1,128)S(1)} all-gather(f32[1,1,1152]{2,1,0:T(1,128)S(1)} %reshape.322), channel_id=2, replica_groups=mesh['dp'=8,'tensor'=4] {'tensor'}, dimensions={0}, use_global_device_ids=true | all-gather | bytes 23040 | tf_op jit(solution)/shard_map/all_gather | solution.py:204
  96.3 57.0 %all-gather.8.cloned.1.call-done = bf16[3072,768]{1,0:T(8,128)(2,1)} async-done(((bf16[768,768]{1,0:T(8,128)(2,1)}), bf16[3072,768]{1,0:T(8,128)(2,1)}) %all-gather.8.cloned.1.call-update) | async-done | bytes 4718608 | tf_op jit(solution)/shard_map/all_gather | solution.py:130
  154.6 58.7 %while.26 = (s32[]{:T(128)}, bf16[4,1024,3,64]{1,3,2,0:T(8,128)(2,1)}, f32[4,3,1024]{2,1,0:T(4,128)S(1)}, bf16[4,1024,3,64]{1,3,2,0:T(8,128)(2,1)}, s32[1024]{0:...) while((s32[]{:T(128)}, ...), condition=%wide.region_3.4_spmd, body=%wide.region_0.3_spmd.sunk | while | flops 844297216 | bytes 47827068 | solution.py:78
  155.3 4.2 fusion.194
  163.4 5.8 fusion.196
  169.9 4.2 fusion.194
  178.0 5.7 fusion.196
  192.6 5.7 fusion.196
  207.1 5.7 fusion.196
  223.2 6.6 %broadcast_select_fusion = (bf16[4,1,768,768]{3,2,0,1:T(8,128)(2,1)}, bf16[4,1,768,768]{3,2,0,1:T(8,128)(2,1)S(1)}) fusion(bf16[4,1,768,768]{3,2,0,1:T(8,128)(2,1)} %collective-permute-done.1, bf16[4,1,768,768]{3,2,0,1:T(8,128)(2,1)} %bitcast.300, pred[]{:T(512)S(6)} %eq.42), kind=kLoop, calls=%fused_computation.81 | loop fusion | flops 4718592 | bytes 18874368 | tf_op jit(solution)/shard_map/jit(_where)/select_n | solution.py:132
  229.8 5.4 multiply_convert_fusion.1
  260.3 10.4 %fusion.67 = bf16[768,3072]{1,0:T(8,128)(2,1)} fusion(bf16[1024,768]{0,1:T(8,128)(2,1)} %get-tuple-element.232, bf16[1024,768]{0,1:T(8,128)(2,1)} %copy-done.53, bf16[1024,768]{0,1:T(8,128)(2,1)} %copy-done.54, bf16[1024,768]{0,1:T(8,128)(2,1)} %copy-done.55, bf16[1024,768]{0,1:T(8,128)(2,1)} %copy-done.56), kind=kOutput, calls=%fused_computation.75 | convolution fusion | flops 4859363328 | bytes 12582912 | tf_op jit(solution)/shard_map/dot_general | solution.py:17
  270.7 5.2 fusion.82
  282.9 4.9 fusion.103
  299.4 12.3 %convolution_convert_fusion = bf16[768,3072]{1,0:T(8,128)(2,1)} fusion(bf16[1024,768]{0,1:T(8,128)(2,1)} %fusion.105, bf16[1024,768]{0,1:T(8,128)(2,1)S(1)} %fusion.103, bf16[1024,768]{0,1:T(8,128)(2,1)} %copy-done.26, bf16[1024,768]{0,1:T(8,128)(2,1)S(1)} %copy-done.25, bf16[1024,768]{0,1:T(8,128)(2,1)S(1)} %copy-done.23), kind=kOutput, calls=%fused_computation.74 | convolution fusion | flops 4859363328 | bytes 12582912 | tf_op jit(solution)/shard_map/dot_general | solution.py:17
  311.8 5.0 fusion.130
  318.6 4.4 multiply_reduce_fusion.1
  331.6 16.2 %concatenate.36 = bf16[768,7168]{1,0:T(8,128)(2,1)} concatenate(bf16[768,768]{1,0:T(8,128)(2,1)} %get-tuple-element.240, bf16[768,768]{1,0:T(8,128)(2,1)} %get-tuple-element.236, bf16[768,192]{1,0:T(8,128)(2,1)} %get-tuple-element.251, bf16[768,64]{1,0:T(8,128)(2,1)S(1)} %broadcast.165, bf16[768,768]{1,0:T(8,128)(2,1)} %get-tuple-element.239, ...), dimensions={1} | concatenate | bytes 22020096 | tf_op jit(solution)/shard_map/concatenate | solution.py:147
  352.8 115.8 %while.27 = (s32[]{:T(128)}, bf16[4,1024,3,64]{1,3,2,0:T(8,128)(2,1)S(1)}, bf16[4,1024,3,64]{1,3,2,0:T(8,128)(2,1)}, bf16[4,1024,3,64]{1,3,2,0:T(8,128)(2,1)S(1)...) while((s32[]{:T(128)}, ...), condition=%wide.region_15.16_spmd, body=%wide.region_13.15_spmd.sunk | while | flops 2062480384 | bytes 108893328 | solution.py:112
  360.4 8.2 %multiply_reduce_fusion.7 = (f32[3,1024]{1,0:T(4,128)S(1)}, f32[3,1024,1024]{1,2,0:T(8,128)}) fusion(f32[3,1024,1024]{1,2,0:T(8,128)S(1)} %fusion.205, f32[3,1024]{1,0:T(4,128)S(1)} %dynamic-slice_bitcast_fusion.2, pred[1024,1024]{0,1:T(8,128)(4,1)S(1)} %broadcast_compare_fusion.5, bf16[4,1024,3,64]{1,3,2,0:T(8,128)(2,1)} %get-tuple-element.451, ...), kind=kOutput, calls=%fused_computation.23.clone.1 | convolution fusion | flops 418378752 | bytes 27030528 | tf_op jit(solution)/shard_map/while/body/eval_jaxpr/qhd,khd->hqk/dot_general | solution.py:89
  368.6 7.6 %multiply_convert_fusion.6 = bf16[3,1024,1024]{1,2,0:T(8,128)(2,1)S(1)} fusion(f32[3,1024,1024]{1,2,0:T(8,128)} %get-tuple-element.394, f32[3,1024,1024]{1,2,0:T(8,128)S(1)} %fusion.205, f32[3,1024]{1,0:T(4,128)S(1)} %get-tuple-element.395, f32[3,1024]{1,0:T(4,128)S(1)} %dynamic-slice_bitcast_fusion.2, pred[1024,1024]{0,1:T(8,128)(4,1)S(1)} %broadcast_compare_fusion.5), kind=kLoop, calls=%fused_computation.22.clone.1 | loop fusion | flops 18874368 | bytes 32530432 | tf_op jit(solution)/shard_map/while/body/eval_jaxpr/convert_element_type | solution.py:93
  389.8 8.1 %multiply_reduce_fusion.7 = (f32[3,1024]{1,0:T(4,128)S(1)}, f32[3,1024,1024]{1,2,0:T(8,128)}) fusion(f32[3,1024,1024]{1,2,0:T(8,128)S(1)} %fusion.205, f32[3,1024]{1,0:T(4,128)S(1)} %dynamic-slice_bitcast_fusion.2, pred[1024,1024]{0,1:T(8,128)(4,1)S(1)} %broadcast_compare_fusion.5, bf16[4,1024,3,64]{1,3,2,0:T(8,128)(2,1)} %get-tuple-element.451, ...), kind=kOutput, calls=%fused_computation.23.clone.1 | convolution fusion | flops 418378752 | bytes 27030528 | tf_op jit(solution)/shard_map/while/body/eval_jaxpr/qhd,khd->hqk/dot_general | solution.py:89
  397.9 7.1 %multiply_convert_fusion.6 = bf16[3,1024,1024]{1,2,0:T(8,128)(2,1)S(1)} fusion(f32[3,1024,1024]{1,2,0:T(8,128)} %get-tuple-element.394, f32[3,1024,1024]{1,2,0:T(8,128)S(1)} %fusion.205, f32[3,1024]{1,0:T(4,128)S(1)} %get-tuple-element.395, f32[3,1024]{1,0:T(4,128)S(1)} %dynamic-slice_bitcast_fusion.2, pred[1024,1024]{0,1:T(8,128)(4,1)S(1)} %broadcast_compare_fusion.5), kind=kLoop, calls=%fused_computation.22.clone.1 | loop fusion | flops 18874368 | bytes 32530432 | tf_op jit(solution)/shard_map/while/body/eval_jaxpr/convert_element_type | solution.py:93
  418.8 8.1 %multiply_reduce_fusion.7 = (f32[3,1024]{1,0:T(4,128)S(1)}, f32[3,1024,1024]{1,2,0:T(8,128)}) fusion(f32[3,1024,1024]{1,2,0:T(8,128)S(1)} %fusion.205, f32[3,1024]{1,0:T(4,128)S(1)} %dynamic-slice_bitcast_fusion.2, pred[1024,1024]{0,1:T(8,128)(4,1)S(1)} %broadcast_compare_fusion.5, bf16[4,1024,3,64]{1,3,2,0:T(8,128)(2,1)} %get-tuple-element.451, ...), kind=kOutput, calls=%fused_computation.23.clone.1 | convolution fusion | flops 418378752 | bytes 27030528 | tf_op jit(solution)/shard_map/while/body/eval_jaxpr/qhd,khd->hqk/dot_general | solution.py:89
  427.0 7.0 %multiply_convert_fusion.6 = bf16[3,1024,1024]{1,2,0:T(8,128)(2,1)S(1)} fusion(f32[3,1024,1024]{1,2,0:T(8,128)} %get-tuple-element.394, f32[3,1024,1024]{1,2,0:T(8,128)S(1)} %fusion.205, f32[3,1024]{1,0:T(4,128)S(1)} %get-tuple-element.395, f32[3,1024]{1,0:T(4,128)S(1)} %dynamic-slice_bitcast_fusion.2, pred[1024,1024]{0,1:T(8,128)(4,1)S(1)} %broadcast_compare_fusion.5), kind=kLoop, calls=%fused_computation.22.clone.1 | loop fusion | flops 18874368 | bytes 32530432 | tf_op jit(solution)/shard_map/while/body/eval_jaxpr/convert_element_type | solution.py:93
  447.5 8.1 %multiply_reduce_fusion.7 = (f32[3,1024]{1,0:T(4,128)S(1)}, f32[3,1024,1024]{1,2,0:T(8,128)}) fusion(f32[3,1024,1024]{1,2,0:T(8,128)S(1)} %fusion.205, f32[3,1024]{1,0:T(4,128)S(1)} %dynamic-slice_bitcast_fusion.2, pred[1024,1024]{0,1:T(8,128)(4,1)S(1)} %broadcast_compare_fusion.5, bf16[4,1024,3,64]{1,3,2,0:T(8,128)(2,1)} %get-tuple-element.451, ...), kind=kOutput, calls=%fused_computation.23.clone.1 | convolution fusion | flops 418378752 | bytes 27030528 | tf_op jit(solution)/shard_map/while/body/eval_jaxpr/qhd,khd->hqk/dot_general | solution.py:89
  455.6 6.9 %multiply_convert_fusion.6 = bf16[3,1024,1024]{1,2,0:T(8,128)(2,1)S(1)} fusion(f32[3,1024,1024]{1,2,0:T(8,128)} %get-tuple-element.394, f32[3,1024,1024]{1,2,0:T(8,128)S(1)} %fusion.205, f32[3,1024]{1,0:T(4,128)S(1)} %get-tuple-element.395, f32[3,1024]{1,0:T(4,128)S(1)} %dynamic-slice_bitcast_fusion.2, pred[1024,1024]{0,1:T(8,128)(4,1)S(1)} %broadcast_compare_fusion.5), kind=kLoop, calls=%fused_computation.22.clone.1 | loop fusion | flops 18874368 | bytes 32530432 | tf_op jit(solution)/shard_map/while/body/eval_jaxpr/convert_element_type | solution.py:93
  470.5 5.7 convolution_convert_fusion.1
  480.0 42.8 %reduce-scatter.6.cloned.1.call-done = bf16[96,2304]{1,0:T(8,128)(2,1)} async-done(((bf16[768,2304]{1,0:T(8,128)(2,1)}), bf16[96,2304]{1,0:T(8,128)(2,1)}) %reduce-scatter.6.cloned.1.call-update) | async-done | bytes 442384 | tf_op jit(solution)/shard_map/reduce_scatter | solution.py:151
  528.5 4.3 convert_reduce_fusion
  536.2 43.0 %psum.7 = f32[9216]{0:T(1024)S(1)} all-reduce(f32[9216]{0:T(1024)S(1)} %constant_dynamic-update-slice_fusion), channel_id=1, replica_groups=mesh['dp'=8,'tensor'=4] {'dp','tensor'}, use_global_device_ids=true, to_apply=%region_27.28 | all-reduce | flops 9216 | bytes 73728 | tf_op jit(solution)/shard_map/psum | solution.py:302
  (293 shorter events, 210.3 us)
Async XLA Ops:
  7.2 76.1 %copy-start = (s32[4,1024]{1,0:T(4,128)S(1)}, s32[4,1024]{1,0:T(4,128)}, u32[]{:S(2)}) copy-start(s32[4,1024]{1,0:T(4,128)} %param.23) | copy-start | bytes 49156
  7.2 56.2 %all-gather.6.cloned.1.call-start = ((), (), s32[]{:S(2)}) async-start(), calls=%async_computation.3 | async-start | bytes 2949120 | tf_op jit(solution)/shard_map/all_gather | solution.py:130
  7.3 56.1 %copy-start.45 = (f32[768]{0:T(1024)S(1)}, f32[768]{0:T(1024)}, u32[]{:S(2)}) copy-start(f32[768]{0:T(1024)} %param.34) | copy-start | bytes 9220
  7.3 56.1 %copy-start.50 = (f32[192]{0:T(256)S(1)}, f32[192]{0:T(256)}, u32[]{:S(2)}) copy-start(f32[192]{0:T(256)} %param.25) | copy-start | bytes 2308
  7.3 56.1 %copy-start.51 = (f32[192]{0:T(256)S(1)}, f32[192]{0:T(256)}, u32[]{:S(2)}) copy-start(f32[192]{0:T(256)} %param.28) | copy-start | bytes 2308
  9.6 143.6 %all-gather.8.cloned.1.call-start = ((), (), s32[]{:S(2)}) async-start(), calls=%async_computation.7 | async-start | bytes 5898240 | tf_op jit(solution)/shard_map/all_gather | solution.py:130
  10.9 457.7 %reduce-scatter.4.cloned.1.call-start = ((), (), s32[]{:S(2)}) async-start(), calls=%async_computation.4 | async-start | bytes 12386304 | tf_op jit(solution)/shard_map/reduce_scatter | solution.py:151
  63.4 20.5 %collective-permute-start = (bf16[4,2,192,768]{3,2,1,0:T(8,128)(2,1)}, bf16[4,2,192,768]{3,2,1,0:T(8,128)(2,1)}, u32[]{:S(2)}, u32[]{:S(2)}) collective-permute-start(bf16[4,2,192,768]{3,2,1,0:T(8,128)(2,1)} %all-gather.6.cloned.1.call-done), channel_id=1, source_target_pairs={{0,4},{4,0},{8,12},{12,8},{16,20},{20,16},{24,28},{28,24},{1,5},{5... | collective-permute-start | bytes 7077896 | tf_op jit(solution)/shard_map/ppermute | solution.py:131
  81.6 12.1 %copy-start.10 = (bf16[1024,768]{1,0:T(8,128)(2,1)}, bf16[1024,768]{1,0:T(8,128)(2,1)S(1)}, u32[]{:S(2)}) copy-start(bf16[1024,768]{1,0:T(8,128)(2,1)S(1)} %constant_dynamic-slice_fusion.3) | copy-start | bytes 4718596
  88.5 5.2 copy-start.28
  153.3 69.9 %collective-permute-start.1 = (bf16[4,1,768,768]{3,2,0,1:T(8,128)(2,1)}, bf16[4,1,768,768]{3,2,0,1:T(8,128)(2,1)}, u32[]{:S(2)}, u32[]{:S(2)}) collective-permute-start(bf16[4,1,768,768]{3,2,0,1:T(8,128)(2,1)} %bitcast.299), channel_id=1, source_target_pairs={{0,4},{4,0},{8,12},{12,8},{16,20},{20,16},{24,28},{28,24},{1,5},{5... | collective-permute-start | bytes 14155784 | tf_op jit(solution)/shard_map/ppermute | solution.py:131
  213.3 5.2 copy-start.12
  213.3 5.2 copy-start.43
  223.2 6.6 %copy-start.46 = (f32[768]{0:T(1024)S(1)}, f32[768]{0:T(1024)}, u32[]{:S(2)}) copy-start(f32[768]{0:T(1024)} %get-tuple-element.186) | copy-start | bytes 9220
  229.8 5.4 copy-start.27
  229.8 5.4 copy-start.47
  235.2 16.3 %copy-start.53 = (bf16[1024,768]{0,1:T(8,128)(2,1)}, bf16[1024,768]{0,1:T(8,128)(2,1)S(1)}, u32[]{:S(2)}) copy-start(bf16[1024,768]{0,1:T(8,128)(2,1)S(1)} %get-tuple-element.277) | copy-start | bytes 4718596
  235.2 7.8 %slice-start.2 = ((s8[4718592]{0:T(1024)(128)(4,1)}), s8[4194304]{0:T(1024)(128)(4,1)S(1)}, s32[]{:S(2)}) async-start(s8[4718592]{0:T(1024)(128)(4,1)} %bitcast.301), calls=%async_computation.10 | async-start | bytes 8388608
  270.7 5.2 copy-start.20
  270.7 5.3 copy-start.59
  275.9 14.3 %copy-start.22 = (bf16[1024,768]{0,1:T(8,128)(2,1)}, bf16[1024,768]{0,1:T(8,128)(2,1)S(1)}, u32[]{:S(2)}) copy-start(bf16[1024,768]{0,1:T(8,128)(2,1)S(1)} %fusion.82) | copy-start | bytes 4718596
  279.2 14.0 %copy-start.24 = (bf16[1024,768]{0,1:T(8,128)(2,1)}, bf16[1024,768]{0,1:T(8,128)(2,1)S(1)}, u32[]{:S(2)}) copy-start(bf16[1024,768]{0,1:T(8,128)(2,1)S(1)} %fusion.89) | copy-start | bytes 4718596
  279.3 8.6 %slice-start = ((s8[4718592]{0:T(1024)(128)(4,1)}), s8[4194304]{0:T(1024)(128)(4,1)S(1)}, s32[]{:S(2)}) async-start(s8[4718592]{0:T(1024)(128)(4,1)} %bitcast.296), calls=%async_computation.8 | async-start | bytes 8388608
  282.9 13.4 %copy-start.26 = (bf16[1024,768]{0,1:T(8,128)(2,1)}, bf16[1024,768]{0,1:T(8,128)(2,1)S(1)}, u32[]{:S(2)}) copy-start(bf16[1024,768]{0,1:T(8,128)(2,1)S(1)} %fusion.96) | copy-start | bytes 4718596
  282.9 5.0 slice-start.1
  287.9 28.8 %copy-start.8 = (bf16[1024,768]{0,1:T(8,128)(2,1)}, bf16[1024,768]{0,1:T(8,128)(2,1)S(1)}, u32[]{:S(2)}) copy-start(bf16[1024,768]{0,1:T(8,128)(2,1)S(1)} %fusion.103) | copy-start | bytes 4718596
  311.7 5.0 copy-start.17
  311.7 5.9 copy-start.18
  311.8 6.9 %copy-start.19 = (f32[1024,768]{0,1:T(8,128)S(1)}, f32[1024,768]{0,1:T(8,128)}, u32[]{:S(2)}) copy-start(f32[1024,768]{0,1:T(8,128)} %fusion.112) | copy-start | bytes 9437188
  347.9 174.9 %reduce-scatter.6.cloned.1.call-start = ((), (), s32[]{:S(2)}) async-start(), calls=%async_computation.5 | async-start | bytes 3981312 | tf_op jit(solution)/shard_map/reduce_scatter | solution.py:151
  476.2 117.3 %reduce-scatter.8.cloned.1.call-start = ((), (), s32[]{:S(2)}) async-start(), calls=%async_computation.6 | async-start | bytes 3031040 | tf_op jit(solution)/shard_map/reduce_scatter | solution.py:159
  588.1 12.9 %copy-start.1 = (s32[4,1024]{1,0:T(4,128)S(1)}, s32[4,1024]{1,0:T(4,128)}, u32[]{:S(2)}) copy-start(s32[4,1024]{1,0:T(4,128)} %param.23) | copy-start | bytes 49156
  (45 other events, 119.9 us)
Sparse Core Ops, SparseCore 0:
  10.2 53.1 all-gather.5
  65.0 88.2 all-gather.7
  348.0 82.6 reduce-scatter.3
  476.4 46.3 reduce-scatter.5
  528.6 49.9 reduce-scatter.7

commit v6 on v5

--- a/solution.py
+++ b/solution.py
@@ -122,12 +122,14 @@
     return (join_groups(grad_query), join_groups(grad_key), join_groups(grad_value))
 
 
-def gather_shards(first_pieces, second_pieces):
+def gather_shards(first_pieces, second_pieces, after=None):
     dp_count = lax.axis_size("dp")
     core = lax.rem(lax.axis_index("dp"), 2)
     first, second = jnp.stack(first_pieces), jnp.stack(second_pieces)
     mine = jnp.where(core == 0, first, second)
     gathered = lax.all_gather(mine, "tensor", axis=0, tiled=False)
+    if after is not None:
+        gathered, after = lax.optimization_barrier((gathered, after))
     other = lax.ppermute(gathered, "dp", perm=[(i, i ^ 1) for i in range(dp_count)])
     halves = (jnp.where(core == 0, gathered, other), jnp.where(core == 0, other, gathered))
     return [half[:, index] for half in halves for index in range(half.shape[1])]
@@ -200,7 +202,6 @@
     qt_sh, kt_sh, vt_sh, o_sh = gather_shards(
         [query_weight.T, key_weight.T], [value_weight.T, output_weight]
     )
-    u_sh, d_sh = gather_shards([up_weight], [down_weight])
     bias_sh = lax.all_gather(
         jnp.concatenate([query_bias, value_bias, up_bias]), "tensor", axis=0, tiled=False
     )
@@ -218,6 +219,7 @@
     key_side = contract_last(input_rows, kt_full).astype(jnp.bfloat16)
     value_proj = (contract_last(input_rows, vt_full) + vb).astype(jnp.bfloat16)
     context, log_total = attend(queries, key_side, value_proj, segment_row)
+    u_sh, d_sh = gather_shards([up_weight], [down_weight], after=context)
 
     group_width = o_sh.shape[1]
     attn_total = input_f32

time: 619 us -> 569 us (0.919)
  waiting for transfers between devices: 152 us -> 99.2 us
    all_gather x2, waiting for transfers between devices: 109 us -> 56.3 us  [gather_shards(): gathered = lax.all_gather(mine, 'tensor', axis=0, tiled=False)]
    unnamed x144 -> x134, local copies, waits for them, and re-layouts: 22 us -> 22.5 us
  transfers between devices with their start and end apart: 7 -> 7, of which waited for: 3 -> 3; matrix products, arithmetic and copies ran while one was open for 38% -> 42% of each run, Pallas kernels for 0% -> 0%
where the time goes in v6:
time: 569 us; the launch traced here: 557 us
  matrix products  235 us (41%)
  waiting for transfers between devices  99.2 us (17%)
  other arithmetic  84.2 us (15%)
  local copies, waits for them, and re-layouts  66.6 us (12%)
  blocking collectives  56.2 us (10%)
  between operations  15.2 us (3%)
    all_gather x2, waiting for transfers between devices, gather_shards(): gathered = lax.all_gather(mine, 'tensor', axis=0, tiled=False)  56.3 us
    psum x1, blocking collectives, on_device(): lax.psum(jnp.concatenate([grad_query_bias, grad_value_bias, grad_up_bias,...  43 us
    reduce_scatter x2, waiting for transfers between devices, scatter_rows(): return lax.psum_scatter(joined, 'dp', scatter_dimension=0, tiled=True)  42.8 us
    dot_general x12, matrix products, contract_last(): lax.dot_general(left_side, right_side, (((1,), (1,)), ((), ())), preferre...  41.1 us
    dot_general x15, matrix products, product(): return jnp.dot(left_side, right_side, preferred_element_type=jnp.float32)  39.3 us
    dot_general x4, matrix products, one_group(): jnp.einsum('qhd,khd->hqk', grad_group, value_group, preferred_element_typ...  32.6 us
    dot_general x4, matrix products, contract_rows(): lax.dot_general(left_side, right_side, (((0,), (0,)), ((), ())), preferre...  30.7 us
    dot_general x8, matrix products, score_group(): jnp.einsum('qhd,khd->hqk', query_group, key_group, preferred_element_type...  29.6 us
  transfers between devices with their start and end apart: 7, of which 3 were waited for; matrix products, arithmetic and copies ran while one was open for 42% of the time, Pallas kernels for 0%

profile of v6, /device:TPU:0, one launch (start us, length us, event | category | flops | bytes accessed | tf_op | source)
XLA Modules:
  0.0 557.2 jit_solution(13600906481293349874)
XLA Ops:
  9.6 53.8 %all-gather.6.cloned.1.call-done = bf16[4,2,192,768]{3,2,1,0:T(8,128)(2,1)} async-done(((bf16[1,2,192,768]{3,2,1,0:T(8,128)(2,1)}), bf16[4,2,192,768]{3,2,1,0:T(8,128)(2,1)}) %all-gather.6.cloned.1.call-update) | async-done | bytes 2359312 | tf_op jit(solution)/shard_map/all_gather | solution.py:130
  65.5 13.2 %all-gather.2 = f32[4,1,1152]{2,1,0:T(1,128)S(1)} all-gather(f32[1,1,1152]{2,1,0:T(1,128)S(1)} %reshape.322), channel_id=2, replica_groups=mesh['dp'=8,'tensor'=4] {'tensor'}, dimensions={0}, use_global_device_ids=true | all-gather | bytes 23040 | tf_op jit(solution)/shard_map/all_gather | solution.py:205
  93.9 58.2 %while.26 = (s32[]{:T(128)}, bf16[4,1024,3,64]{1,3,2,0:T(8,128)(2,1)}, f32[4,3,1024]{2,1,0:T(4,128)S(1)}, bf16[4,1024,3,64]{1,3,2,0:T(8,128)(2,1)}, s32[1024]{0:...) while((s32[]{:T(128)}, ...), condition=%wide.region_3.4_spmd, body=%wide.region_0.3_spmd.sunk | while | flops 844297216 | bytes 47827068 | solution.py:78
  94.5 4.2 fusion.194
  102.7 5.7 %fusion.196 = bf16[4,1024,3,64]{1,3,2,0:T(8,128)(2,1)} fusion(bf16[4,1024,3,64]{1,3,2,0:T(8,128)(2,1)} %get-tuple-element.407, s32[]{:T(128)S(6)} %copy.149, f32[3,1024,1024]{1,2,0:T(8,128)S(1)} %get-tuple-element.384, f32[3,1024]{1,0:T(4,128)S(1)} %fusion.195, f32[3,1024]{1,0:T(4,128)S(1)} %get-tuple-element.385, pred[1024,1024]{0,1:T(8,128)(4,1)} %copy-done.2, ...), kind=kOutput, calls=%fused_computation.9.clone.1 | convolution fusion | flops 418578432 | bytes 14443520 | tf_op jit(solution)/shard_map/while/body/eval_jaxpr/hqk,khd->qhd/dot_general | solution.py:73
  117.2 5.7 %fusion.196 = bf16[4,1024,3,64]{1,3,2,0:T(8,128)(2,1)} fusion(bf16[4,1024,3,64]{1,3,2,0:T(8,128)(2,1)} %get-tuple-element.407, s32[]{:T(128)S(6)} %copy.149, f32[3,1024,1024]{1,2,0:T(8,128)S(1)} %get-tuple-element.384, f32[3,1024]{1,0:T(4,128)S(1)} %fusion.195, f32[3,1024]{1,0:T(4,128)S(1)} %get-tuple-element.385, pred[1024,1024]{0,1:T(8,128)(4,1)} %copy-done.2, ...), kind=kOutput, calls=%fused_computation.9.clone.1 | convolution fusion | flops 418578432 | bytes 14443520 | tf_op jit(solution)/shard_map/while/body/eval_jaxpr/hqk,khd->qhd/dot_general | solution.py:73
  123.6 4.2 fusion.194
  131.8 5.7 %fusion.196 = bf16[4,1024,3,64]{1,3,2,0:T(8,128)(2,1)} fusion(bf16[4,1024,3,64]{1,3,2,0:T(8,128)(2,1)} %get-tuple-element.407, s32[]{:T(128)S(6)} %copy.149, f32[3,1024,1024]{1,2,0:T(8,128)S(1)} %get-tuple-element.384, f32[3,1024]{1,0:T(4,128)S(1)} %fusion.195, f32[3,1024]{1,0:T(4,128)S(1)} %get-tuple-element.385, pred[1024,1024]{0,1:T(8,128)(4,1)} %copy-done.2, ...), kind=kOutput, calls=%fused_computation.9.clone.1 | convolution fusion | flops 418578432 | bytes 14443520 | tf_op jit(solution)/shard_map/while/body/eval_jaxpr/hqk,khd->qhd/dot_general | solution.py:73
  138.2 4.2 fusion.194
  146.3 5.7 %fusion.196 = bf16[4,1024,3,64]{1,3,2,0:T(8,128)(2,1)} fusion(bf16[4,1024,3,64]{1,3,2,0:T(8,128)(2,1)} %get-tuple-element.407, s32[]{:T(128)S(6)} %copy.149, f32[3,1024,1024]{1,2,0:T(8,128)S(1)} %get-tuple-element.384, f32[3,1024]{1,0:T(4,128)S(1)} %fusion.195, f32[3,1024]{1,0:T(4,128)S(1)} %get-tuple-element.385, pred[1024,1024]{0,1:T(8,128)(4,1)} %copy-done.2, ...), kind=kOutput, calls=%fused_computation.9.clone.1 | convolution fusion | flops 418578432 | bytes 14443520 | tf_op jit(solution)/shard_map/while/body/eval_jaxpr/hqk,khd->qhd/dot_general | solution.py:73
  170.6 8.6 %broadcast_select_fusion = (bf16[4,1,768,768]{3,2,0,1:T(8,128)(2,1)}, bf16[4,1,768,768]{3,2,0,1:T(8,128)(2,1)}) fusion(bf16[4,1,768,768]{3,2,0,1:T(8,128)(2,1)} %collective-permute-done.1, bf16[4,1,768,768]{3,2,0,1:T(8,128)(2,1)} %bitcast.300, pred[]{:T(512)S(6)} %eq.42), kind=kLoop, calls=%fused_computation.81 | loop fusion | flops 4718592 | bytes 18874368 | tf_op jit(solution)/shard_map/jit(_where)/select_n | solution.py:134
  179.2 5.3 multiply_convert_fusion.1
  208.7 11.3 %fusion.67 = bf16[768,3072]{1,0:T(8,128)(2,1)} fusion(bf16[1024,768]{0,1:T(8,128)(2,1)S(1)} %get-tuple-element.234, bf16[1024,768]{0,1:T(8,128)(2,1)S(1)} %get-tuple-element.279, bf16[1024,768]{0,1:T(8,128)(2,1)S(1)} %copy-done.47, bf16[1024,768]{0,1:T(8,128)(2,1)} %copy-done.48, bf16[1024,768]{0,1:T(8,128)(2,1)} %copy-done.49), kind=kOutput, calls=%fused_computation.75 | convolution fusion | flops 4859363328 | bytes 12582912 | tf_op jit(solution)/shard_map/dot_general | solution.py:17
  220.0 5.2 fusion.82
  225.2 4.9 fusion.89
  248.8 12.3 %convolution_convert_fusion = bf16[768,3072]{1,0:T(8,128)(2,1)} fusion(bf16[1024,768]{0,1:T(8,128)(2,1)} %copy-done.26, bf16[1024,768]{0,1:T(8,128)(2,1)S(1)} %fusion.103, bf16[1024,768]{0,1:T(8,128)(2,1)} %copy-done.25, bf16[1024,768]{0,1:T(8,128)(2,1)S(1)} %copy-done.24, bf16[1024,768]{0,1:T(8,128)(2,1)S(1)} %fusion.82), kind=kOutput, calls=%fused_computation.74 | convolution fusion | flops 4859363328 | bytes 12582912 | tf_op jit(solution)/shard_map/dot_general | solution.py:17
  261.1 5.0 fusion.130
  268.0 4.4 multiply_reduce_fusion.1
  281.0 16.3 %concatenate.36 = bf16[768,7168]{1,0:T(8,128)(2,1)} concatenate(bf16[768,768]{1,0:T(8,128)(2,1)} %get-tuple-element.242, bf16[768,768]{1,0:T(8,128)(2,1)} %get-tuple-element.238, bf16[768,192]{1,0:T(8,128)(2,1)} %get-tuple-element.253, bf16[768,64]{1,0:T(8,128)(2,1)S(1)} %broadcast.165, bf16[768,768]{1,0:T(8,128)(2,1)} %get-tuple-element.241, ...), dimensions={1} | concatenate | bytes 22020096 | tf_op jit(solution)/shard_map/concatenate | solution.py:149
  302.2 115.7 %while.27 = (s32[]{:T(128)}, bf16[4,1024,3,64]{1,3,2,0:T(8,128)(2,1)S(1)}, bf16[4,1024,3,64]{1,3,2,0:T(8,128)(2,1)}, bf16[4,1024,3,64]{1,3,2,0:T(8,128)(2,1)S(1)...) while((s32[]{:T(128)}, ...), condition=%wide.region_15.16_spmd, body=%wide.region_13.15_spmd.sunk | while | flops 2062480384 | bytes 108893328 | solution.py:112
  309.8 8.2 %multiply_reduce_fusion.7 = (f32[3,1024]{1,0:T(4,128)S(1)}, f32[3,1024,1024]{1,2,0:T(8,128)}) fusion(f32[3,1024,1024]{1,2,0:T(8,128)S(1)} %fusion.205, f32[3,1024]{1,0:T(4,128)S(1)} %dynamic-slice_bitcast_fusion.2, pred[1024,1024]{0,1:T(8,128)(4,1)S(1)} %broadcast_compare_fusion.5, bf16[4,1024,3,64]{1,3,2,0:T(8,128)(2,1)} %get-tuple-element.453, ...), kind=kOutput, calls=%fused_computation.23.clone.1 | convolution fusion | flops 418378752 | bytes 27030528 | tf_op jit(solution)/shard_map/while/body/eval_jaxpr/qhd,khd->hqk/dot_general | solution.py:89
  318.0 7.6 %multiply_convert_fusion.6 = bf16[3,1024,1024]{1,2,0:T(8,128)(2,1)S(1)} fusion(f32[3,1024,1024]{1,2,0:T(8,128)} %get-tuple-element.396, f32[3,1024,1024]{1,2,0:T(8,128)S(1)} %fusion.205, f32[3,1024]{1,0:T(4,128)S(1)} %get-tuple-element.397, f32[3,1024]{1,0:T(4,128)S(1)} %dynamic-slice_bitcast_fusion.2, pred[1024,1024]{0,1:T(8,128)(4,1)S(1)} %broadcast_compare_fusion.5), kind=kLoop, calls=%fused_computation.22.clone.1 | loop fusion | flops 18874368 | bytes 32530432 | tf_op jit(solution)/shard_map/while/body/eval_jaxpr/convert_element_type | solution.py:93
  339.1 8.1 %multiply_reduce_fusion.7 = (f32[3,1024]{1,0:T(4,128)S(1)}, f32[3,1024,1024]{1,2,0:T(8,128)}) fusion(f32[3,1024,1024]{1,2,0:T(8,128)S(1)} %fusion.205, f32[3,1024]{1,0:T(4,128)S(1)} %dynamic-slice_bitcast_fusion.2, pred[1024,1024]{0,1:T(8,128)(4,1)S(1)} %broadcast_compare_fusion.5, bf16[4,1024,3,64]{1,3,2,0:T(8,128)(2,1)} %get-tuple-element.453, ...), kind=kOutput, calls=%fused_computation.23.clone.1 | convolution fusion | flops 418378752 | bytes 27030528 | tf_op jit(solution)/shard_map/while/body/eval_jaxpr/qhd,khd->hqk/dot_general | solution.py:89
  347.2 7.1 %multiply_convert_fusion.6 = bf16[3,1024,1024]{1,2,0:T(8,128)(2,1)S(1)} fusion(f32[3,1024,1024]{1,2,0:T(8,128)} %get-tuple-element.396, f32[3,1024,1024]{1,2,0:T(8,128)S(1)} %fusion.205, f32[3,1024]{1,0:T(4,128)S(1)} %get-tuple-element.397, f32[3,1024]{1,0:T(4,128)S(1)} %dynamic-slice_bitcast_fusion.2, pred[1024,1024]{0,1:T(8,128)(4,1)S(1)} %broadcast_compare_fusion.5), kind=kLoop, calls=%fused_computation.22.clone.1 | loop fusion | flops 18874368 | bytes 32530432 | tf_op jit(solution)/shard_map/while/body/eval_jaxpr/convert_element_type | solution.py:93
  368.1 8.1 %multiply_reduce_fusion.7 = (f32[3,1024]{1,0:T(4,128)S(1)}, f32[3,1024,1024]{1,2,0:T(8,128)}) fusion(f32[3,1024,1024]{1,2,0:T(8,128)S(1)} %fusion.205, f32[3,1024]{1,0:T(4,128)S(1)} %dynamic-slice_bitcast_fusion.2, pred[1024,1024]{0,1:T(8,128)(4,1)S(1)} %broadcast_compare_fusion.5, bf16[4,1024,3,64]{1,3,2,0:T(8,128)(2,1)} %get-tuple-element.453, ...), kind=kOutput, calls=%fused_computation.23.clone.1 | convolution fusion | flops 418378752 | bytes 27030528 | tf_op jit(solution)/shard_map/while/body/eval_jaxpr/qhd,khd->hqk/dot_general | solution.py:89
  376.3 7.0 %multiply_convert_fusion.6 = bf16[3,1024,1024]{1,2,0:T(8,128)(2,1)S(1)} fusion(f32[3,1024,1024]{1,2,0:T(8,128)} %get-tuple-element.396, f32[3,1024,1024]{1,2,0:T(8,128)S(1)} %fusion.205, f32[3,1024]{1,0:T(4,128)S(1)} %get-tuple-element.397, f32[3,1024]{1,0:T(4,128)S(1)} %dynamic-slice_bitcast_fusion.2, pred[1024,1024]{0,1:T(8,128)(4,1)S(1)} %broadcast_compare_fusion.5), kind=kLoop, calls=%fused_computation.22.clone.1 | loop fusion | flops 18874368 | bytes 32530432 | tf_op jit(solution)/shard_map/while/body/eval_jaxpr/convert_element_type | solution.py:93
  396.8 8.1 %multiply_reduce_fusion.7 = (f32[3,1024]{1,0:T(4,128)S(1)}, f32[3,1024,1024]{1,2,0:T(8,128)}) fusion(f32[3,1024,1024]{1,2,0:T(8,128)S(1)} %fusion.205, f32[3,1024]{1,0:T(4,128)S(1)} %dynamic-slice_bitcast_fusion.2, pred[1024,1024]{0,1:T(8,128)(4,1)S(1)} %broadcast_compare_fusion.5, bf16[4,1024,3,64]{1,3,2,0:T(8,128)(2,1)} %get-tuple-element.453, ...), kind=kOutput, calls=%fused_computation.23.clone.1 | convolution fusion | flops 418378752 | bytes 27030528 | tf_op jit(solution)/shard_map/while/body/eval_jaxpr/qhd,khd->hqk/dot_general | solution.py:89
  404.9 6.9 %multiply_convert_fusion.6 = bf16[3,1024,1024]{1,2,0:T(8,128)(2,1)S(1)} fusion(f32[3,1024,1024]{1,2,0:T(8,128)} %get-tuple-element.396, f32[3,1024,1024]{1,2,0:T(8,128)S(1)} %fusion.205, f32[3,1024]{1,0:T(4,128)S(1)} %get-tuple-element.397, f32[3,1024]{1,0:T(4,128)S(1)} %dynamic-slice_bitcast_fusion.2, pred[1024,1024]{0,1:T(8,128)(4,1)S(1)} %broadcast_compare_fusion.5), kind=kLoop, calls=%fused_computation.22.clone.1 | loop fusion | flops 18874368 | bytes 32530432 | tf_op jit(solution)/shard_map/while/body/eval_jaxpr/convert_element_type | solution.py:93
  419.8 5.7 %convolution_convert_fusion.1 = bf16[768,2304]{1,0:T(8,128)(2,1)} fusion(bf16[1024,768]{1,0:T(8,128)(2,1)S(1)} %copy-done.11, bf16[1024,2304]{0,1:T(8,128)(2,1)S(1)} %bitcast.298), kind=kOutput, calls=%fused_computation.76 | convolution fusion | flops 3625648128 | bytes 9830400 | tf_op jit(solution)/shard_map/dot_general | solution.py:17
  429.3 42.8 %reduce-scatter.6.cloned.1.call-done = bf16[96,2304]{1,0:T(8,128)(2,1)} async-done(((bf16[768,2304]{1,0:T(8,128)(2,1)}), bf16[96,2304]{1,0:T(8,128)(2,1)}) %reduce-scatter.6.cloned.1.call-update) | async-done | bytes 442384 | tf_op jit(solution)/shard_map/reduce_scatter | solution.py:153
  477.7 4.3 convert_reduce_fusion
  485.5 43.0 %psum.7 = f32[9216]{0:T(1024)S(1)} all-reduce(f32[9216]{0:T(1024)S(1)} %constant_dynamic-update-slice_fusion), channel_id=1, replica_groups=mesh['dp'=8,'tensor'=4] {'dp','tensor'}, use_global_device_ids=true, to_apply=%region_27.28 | all-reduce | flops 9216 | bytes 73728 | tf_op jit(solution)/shard_map/psum | solution.py:304
  (284 shorter events, 208.6 us)
Async XLA Ops:
  7.2 71.7 %copy-start = (s32[4,1024]{1,0:T(4,128)S(1)}, s32[4,1024]{1,0:T(4,128)}, u32[]{:S(2)}) copy-start(s32[4,1024]{1,0:T(4,128)} %param.23) | copy-start | bytes 49156
  7.2 56.2 %copy-start.31 = (bf16[768,768]{1,0:T(8,128)(2,1)S(1)}, bf16[768,768]{1,0:T(8,128)(2,1)}, u32[]{:S(2)}) copy-start(bf16[768,768]{1,0:T(8,128)(2,1)} %param.33) | copy-start | bytes 3538948
  7.2 56.2 %all-gather.6.cloned.1.call-start = ((), (), s32[]{:S(2)}) async-start(), calls=%async_computation.3 | async-start | bytes 2949120 | tf_op jit(solution)/shard_map/all_gather | solution.py:130
  9.5 145.0 %all-gather.8.cloned.1.call-start = ((), (), s32[]{:S(2)}) async-start(), calls=%async_computation.7 | async-start | bytes 5898240 | tf_op jit(solution)/shard_map/all_gather | solution.py:130
  63.4 17.1 %copy-start.20 = (bf16[4,2,192,768]{3,2,1,0:T(8,128)(2,1)S(1)}, bf16[4,2,192,768]{3,2,1,0:T(8,128)(2,1)}, u32[]{:S(2)}) copy-start(bf16[4,2,192,768]{3,2,1,0:T(8,128)(2,1)} %all-gather.6.cloned.1.call-done) | copy-start | bytes 7077892
  63.4 17.0 %collective-permute-start = (bf16[4,2,192,768]{3,2,1,0:T(8,128)(2,1)}, bf16[4,2,192,768]{3,2,1,0:T(8,128)(2,1)}, u32[]{:S(2)}, u32[]{:S(2)}) collective-permute-start(bf16[4,2,192,768]{3,2,1,0:T(8,128)(2,1)} %all-gather.6.cloned.1.call-done), channel_id=1, source_target_pairs={{0,4},{4,0},{8,12},{12,8},{16,20},{20,16},{24,28},{28,24},{1,5},{5... | collective-permute-start | bytes 7077896 | tf_op jit(solution)/shard_map/ppermute | solution.py:133
  64.6 353.3 %reduce-scatter.4.cloned.1.call-start = ((), (), s32[]{:S(2)}) async-start(), calls=%async_computation.4 | async-start | bytes 12386304 | tf_op jit(solution)/shard_map/reduce_scatter | solution.py:153
  80.4 9.4 %copy-start.10 = (bf16[1024,768]{1,0:T(8,128)(2,1)}, bf16[1024,768]{1,0:T(8,128)(2,1)S(1)}, u32[]{:S(2)}) copy-start(bf16[1024,768]{1,0:T(8,128)(2,1)S(1)} %constant_dynamic-slice_fusion.3) | copy-start | bytes 4718596
  84.7 5.2 copy-start.27
  154.5 16.0 %collective-permute-start.1 = (bf16[4,1,768,768]{3,2,0,1:T(8,128)(2,1)}, bf16[4,1,768,768]{3,2,0,1:T(8,128)(2,1)}, u32[]{:S(2)}, u32[]{:S(2)}) collective-permute-start(bf16[4,1,768,768]{3,2,0,1:T(8,128)(2,1)} %bitcast.299), channel_id=1, source_target_pairs={{0,4},{4,0},{8,12},{12,8},{16,20},{20,16},{24,28},{28,24},{1,5},{5... | collective-permute-start | bytes 14155784 | tf_op jit(solution)/shard_map/ppermute | solution.py:133
  157.1 5.0 copy-start.33
  157.1 5.0 copy-start.9
  162.1 4.9 copy-start.12
  162.1 4.9 copy-start.43
  170.6 24.9 %copy-start.26 = (bf16[1024,768]{0,1:T(8,128)(2,1)}, bf16[1024,768]{0,1:T(8,128)(2,1)S(1)}, u32[]{:S(2)}) copy-start(bf16[1024,768]{0,1:T(8,128)(2,1)S(1)} %fusion.105) | copy-start | bytes 4718596
  179.2 5.3 copy-start.7
  184.5 7.8 %slice-start.2 = ((s8[4718592]{0:T(1024)(128)(4,1)}), s8[4194304]{0:T(1024)(128)(4,1)S(1)}, s32[]{:S(2)}) async-start(s8[4718592]{0:T(1024)(128)(4,1)} %bitcast.301), calls=%async_computation.10 | async-start | bytes 8388608
  220.0 5.2 copy-start.52
  220.0 10.2 %slice-start.4 = ((s8[4718592]{0:T(1024)(128)(4,1)}), s8[4194304]{0:T(1024)(128)(4,1)S(1)}, s32[]{:S(2)}) async-start(s8[4718592]{0:T(1024)(128)(4,1)} %bitcast.303), calls=%async_computation.12 | async-start | bytes 8388608
  225.2 23.6 %copy-start.22 = (bf16[1024,768]{0,1:T(8,128)(2,1)}, bf16[1024,768]{0,1:T(8,128)(2,1)S(1)}, u32[]{:S(2)}) copy-start(bf16[1024,768]{0,1:T(8,128)(2,1)S(1)} %fusion.82) | copy-start | bytes 4718596
  225.2 5.0 slice-start.5
  225.2 5.0 copy-start.51
  230.2 12.4 %copy-start.23 = (bf16[1024,768]{0,1:T(8,128)(2,1)}, bf16[1024,768]{0,1:T(8,128)(2,1)S(1)}, u32[]{:S(2)}) copy-start(bf16[1024,768]{0,1:T(8,128)(2,1)S(1)} %fusion.89) | copy-start | bytes 4718596
  230.2 7.0 %slice-start = ((s8[4718592]{0:T(1024)(128)(4,1)}), s8[4194304]{0:T(1024)(128)(4,1)S(1)}, s32[]{:S(2)}) async-start(s8[4718592]{0:T(1024)(128)(4,1)} %bitcast.296), calls=%async_computation.8 | async-start | bytes 8388608
  233.5 12.2 %copy-start.25 = (bf16[1024,768]{0,1:T(8,128)(2,1)}, bf16[1024,768]{0,1:T(8,128)(2,1)S(1)}, u32[]{:S(2)}) copy-start(bf16[1024,768]{0,1:T(8,128)(2,1)S(1)} %fusion.96) | copy-start | bytes 4718596
  237.2 28.9 %copy-start.8 = (bf16[1024,768]{0,1:T(8,128)(2,1)}, bf16[1024,768]{0,1:T(8,128)(2,1)S(1)}, u32[]{:S(2)}) copy-start(bf16[1024,768]{0,1:T(8,128)(2,1)S(1)} %fusion.103) | copy-start | bytes 4718596
  261.1 5.0 copy-start.17
  261.1 5.9 %copy-start.18 = (f32[1024,768]{0,1:T(8,128)S(1)}, f32[1024,768]{0,1:T(8,128)}, u32[]{:S(2)}) copy-start(f32[1024,768]{0,1:T(8,128)} %fusion.109) | copy-start | bytes 9437188
  261.1 6.9 %copy-start.19 = (f32[1024,768]{0,1:T(8,128)S(1)}, f32[1024,768]{0,1:T(8,128)}, u32[]{:S(2)}) copy-start(f32[1024,768]{0,1:T(8,128)} %fusion.112) | copy-start | bytes 9437188
  297.3 174.8 %reduce-scatter.6.cloned.1.call-start = ((), (), s32[]{:S(2)}) async-start(), calls=%async_computation.5 | async-start | bytes 3981312 | tf_op jit(solution)/shard_map/reduce_scatter | solution.py:153
  425.5 117.3 %reduce-scatter.8.cloned.1.call-start = ((), (), s32[]{:S(2)}) async-start(), calls=%async_computation.6 | async-start | bytes 3031040 | tf_op jit(solution)/shard_map/reduce_scatter | solution.py:161
  537.3 12.9 %copy-start.1 = (s32[4,1024]{1,0:T(4,128)S(1)}, s32[4,1024]{1,0:T(4,128)}, u32[]{:S(2)}) copy-start(s32[4,1024]{1,0:T(4,128)} %param.23) | copy-start | bytes 49156
  (40 other events, 110.6 us)
Sparse Core Ops, SparseCore 0:
  10.2 53.1 all-gather.5
  65.6 88.9 all-gather.7
  297.4 82.7 reduce-scatter.3
  425.6 46.3 reduce-scatter.5
  477.8 49.9 reduce-scatter.7

commit v7 on v6

--- a/solution.py
+++ b/solution.py
@@ -1,6 +1,8 @@
 import jax
 import jax.numpy as jnp
 from jax import lax
+from jax.experimental import pallas as pl
+from jax.experimental.pallas import tpu as pltpu
 from jax.sharding import PartitionSpec as P
 
 HEAD_DIM = 64
@@ -43,83 +45,106 @@
     return jax.nn.gelu(pre_act, approximate=True)
 
 
-def score_group(query_group, key_group, segment_row):
-    scores = jnp.einsum(
-        "qhd,khd->hqk", query_group, key_group, preferred_element_type=jnp.float32
-    ) * HEAD_DIM ** (-0.5)
-    linked = segment_row[:, None] == segment_row[None, :]
-    return jnp.where(linked[None], scores, -1e30)
-
-
-def split_groups(rows_by_width):
-    length, width = rows_by_width.shape
-    groups = width // (GROUP_HEADS * HEAD_DIM)
-    return rows_by_width.reshape(length, groups, GROUP_HEADS, HEAD_DIM).transpose(1, 0, 2, 3)
-
-
-def join_groups(grouped):
-    groups, length, heads, dim = grouped.shape
-    return grouped.transpose(1, 0, 2, 3).reshape(length, groups * heads * dim)
-
-
-def attend(queries, key_side, value_proj, segment_row):
-    def one_group(inputs):
-        query_group, key_group, value_group = inputs
-        scores = score_group(query_group, key_group, segment_row)
-        row_max = jnp.max(scores, -1, keepdims=True)
-        exp_scores = jnp.exp(scores - row_max)
-        row_total = jnp.sum(exp_scores, -1, keepdims=True)
-        prob_low = (exp_scores / row_total).astype(jnp.bfloat16)
-        context = jnp.einsum(
-            "hqk,khd->qhd", prob_low, value_group, preferred_element_type=jnp.float32
-        )
-        return (context.astype(jnp.bfloat16), (row_max + jnp.log(row_total))[..., 0])
-
-    context, log_total = lax.map(
-        one_group, (split_groups(queries), split_groups(key_side), split_groups(value_proj))
-    )
-    return (join_groups(context), log_total)
-
-
-def attend_back(queries, key_side, value_proj, segment_row, log_total, grad_context):
-    def one_group(inputs):
-        query_group, key_group, value_group, log_group, grad_group = inputs
-        scores = score_group(query_group, key_group, segment_row)
-        probs_full = jnp.exp(scores - log_group[..., None])
-        grad_probs = jnp.einsum(
-            "qhd,khd->hqk", grad_group, value_group, preferred_element_type=jnp.float32
-        )
-        inner_sum = jnp.sum(probs_full * grad_probs, -1, keepdims=True)
-        grad_scores = (probs_full * (grad_probs - inner_sum)).astype(jnp.bfloat16)
-        grad_query = jnp.einsum(
-            "hqk,khd->qhd", grad_scores, key_group, preferred_element_type=jnp.float32
-        ) * HEAD_DIM ** (-0.5)
-        grad_key = jnp.einsum(
-            "hqk,qhd->khd", grad_scores, query_group, preferred_element_type=jnp.float32
-        ) * HEAD_DIM ** (-0.5)
-        grad_value = jnp.einsum(
-            "hqk,qhd->khd",
-            probs_full.astype(jnp.bfloat16),
-            grad_group,
-            preferred_element_type=jnp.float32,
-        )
-        return (
-            grad_query.astype(jnp.bfloat16),
-            grad_key.astype(jnp.bfloat16),
-            grad_value.astype(jnp.bfloat16),
-        )
-
-    grad_query, grad_key, grad_value = lax.map(
-        one_group,
-        (
-            split_groups(queries),
-            split_groups(key_side),
-            split_groups(value_proj),
-            log_total,
-            split_groups(grad_context),
-        ),
-    )
-    return (join_groups(grad_query), join_groups(grad_key), join_groups(grad_value))
+SCALE = HEAD_DIM ** (-0.5)
+STATS = 128
+
+
+def _scores(q, k, linked):
+    s = lax.dot_general(q, k, (((1,), (1,)), ((), ())), preferred_element_type=jnp.float32) * SCALE
+    return jnp.where(linked, s, -1e30)
+
+
+def attn_fwd_kernel(q_ref, k_ref, v_ref, segq_ref, segk_ref, ctx_ref, stats_ref):
+    linked = segq_ref[...] == segk_ref[...]
+    heads = q_ref.shape[1] // HEAD_DIM
+    half = STATS // 2
+    for h in range(heads):
+        cols = slice(h * HEAD_DIM, (h + 1) * HEAD_DIM)
+        s = _scores(q_ref[:, cols], k_ref[:, cols], linked)
+        m = jnp.max(s, axis=1, keepdims=True)
+        e = jnp.exp(s - m)
+        l = jnp.sum(e, axis=1, keepdims=True)
+        p = (e / l).astype(jnp.bfloat16)
+        ctx = jnp.dot(p, v_ref[:, cols], preferred_element_type=jnp.float32)
+        ctx_ref[:, cols] = ctx.astype(ctx_ref.dtype)
+        stats_ref[:, h : h + 1] = m
+        stats_ref[:, half + h : half + h + 1] = l
+
+
+def attn_bwd_kernel(q_ref, k_ref, v_ref, dctx_ref, segq_ref, segk_ref, stats_ref,
+                    dq_ref, dk_ref, dv_ref, dk_acc, dv_acc):
+    step = pl.program_id(0)
+
+    @pl.when(step == 0)
+    def _():
+        dk_acc[...] = jnp.zeros_like(dk_acc)
+        dv_acc[...] = jnp.zeros_like(dv_acc)
+
+    linked = segq_ref[...] == segk_ref[...]
+    heads = q_ref.shape[1] // HEAD_DIM
+    half = STATS // 2
+    for h in range(heads):
+        cols = slice(h * HEAD_DIM, (h + 1) * HEAD_DIM)
+        q = q_ref[:, cols]
+        k = k_ref[:, cols]
+        dctx = dctx_ref[:, cols]
+        s = _scores(q, k, linked)
+        p = jnp.exp(s - stats_ref[:, h : h + 1]) / stats_ref[:, half + h : half + h + 1]
+        dp = lax.dot_general(dctx, v_ref[:, cols], (((1,), (1,)), ((), ())), preferred_element_type=jnp.float32)
+        inner = jnp.sum(p * dp, axis=1, keepdims=True)
+        ds = (p * (dp - inner)).astype(jnp.bfloat16)
+        dq = jnp.dot(ds, k, preferred_element_type=jnp.float32) * SCALE
+        dq_ref[:, cols] = dq.astype(dq_ref.dtype)
+        dk_acc[:, cols] += lax.dot_general(ds, q, (((0,), (0,)), ((), ())), preferred_element_type=jnp.float32)
+        dv_acc[:, cols] += lax.dot_general(p.astype(jnp.bfloat16), dctx, (((0,), (0,)), ((), ())), preferred_element_type=jnp.float32)
+
+    @pl.when(step == pl.num_programs(0) - 1)
+    def _():
+        dk_ref[...] = (dk_acc[...] * SCALE).astype(dk_ref.dtype)
+        dv_ref[...] = dv_acc[...].astype(dv_ref.dtype)
+
+
+def attention_forward(queries, key_side, value_proj, segment_row, block=256):
+    length, width = queries.shape
+    segq = segment_row.reshape(length, 1)
+    segk = segment_row.reshape(1, length)
+    full = pl.BlockSpec((length, width), lambda i: (0, 0))
+    return pl.pallas_call(
+        attn_fwd_kernel,
+        out_shape=(jax.ShapeDtypeStruct((length, width), jnp.bfloat16),
+                   jax.ShapeDtypeStruct((length, STATS), jnp.float32)),
+        grid=(length // block,),
+        in_specs=[pl.BlockSpec((block, width), lambda i: (i, 0)), full, full,
+                  pl.BlockSpec((block, 1), lambda i: (i, 0)),
+                  pl.BlockSpec((1, length), lambda i: (0, 0))],
+        out_specs=(pl.BlockSpec((block, width), lambda i: (i, 0)),
+                   pl.BlockSpec((block, STATS), lambda i: (i, 0))),
+        compiler_params=pltpu.CompilerParams(dimension_semantics=("arbitrary",)),
+        cost_estimate=pl.CostEstimate(flops=4 * length * length * width, transcendentals=length * length * width // HEAD_DIM,
+                                      bytes_accessed=8 * length * width),
+    )(queries, key_side, value_proj, segq, segk)
+
+
+def attention_backward(queries, key_side, value_proj, segment_row, stats, grad_context, block=256):
+    length, width = queries.shape
+    segq = segment_row.reshape(length, 1)
+    segk = segment_row.reshape(1, length)
+    full = pl.BlockSpec((length, width), lambda i: (0, 0))
+    rows = pl.BlockSpec((block, width), lambda i: (i, 0))
+    return pl.pallas_call(
+        attn_bwd_kernel,
+        out_shape=tuple(jax.ShapeDtypeStruct((length, width), jnp.bfloat16) for _ in range(3)),
+        grid=(length // block,),
+        in_specs=[rows, full, full, rows,
+                  pl.BlockSpec((block, 1), lambda i: (i, 0)),
+                  pl.BlockSpec((1, length), lambda i: (0, 0)),
+                  pl.BlockSpec((block, STATS), lambda i: (i, 0))],
+        out_specs=(rows, full, full),
+        scratch_shapes=[pltpu.VMEM((length, width), jnp.float32), pltpu.VMEM((length, width), jnp.float32)],
+        compiler_params=pltpu.CompilerParams(dimension_semantics=("arbitrary",)),
+        cost_estimate=pl.CostEstimate(flops=10 * length * length * width, transcendentals=length * length * width // HEAD_DIM,
+                                      bytes_accessed=14 * length * width),
+    )(queries, key_side, value_proj, grad_context, segq, segk, stats)
 
 
 def gather_shards(first_pieces, second_pieces, after=None):
@@ -218,7 +243,7 @@
     queries = (contract_last(input_rows, qt_full) + qb).astype(jnp.bfloat16)
     key_side = contract_last(input_rows, kt_full).astype(jnp.bfloat16)
     value_proj = (contract_last(input_rows, vt_full) + vb).astype(jnp.bfloat16)
-    context, log_total = attend(queries, key_side, value_proj, segment_row)
+    context, softmax_stats = attention_forward(queries, key_side, value_proj, segment_row)
     u_sh, d_sh = gather_shards([up_weight], [down_weight], after=context)
 
     group_width = o_sh.shape[1]
@@ -278,8 +303,8 @@
     ffn_widths = [grad.shape[1] // part_count for grad in ffn_grads]
     ffn_joined, grad_context = lax.optimization_barrier((by_parts(ffn_grads), grad_context))
     ffn_rows = scatter_rows(ffn_joined)
-    query_low, key_low, value_low = attend_back(
-        queries, key_side, value_proj, segment_row, log_total, grad_context
+    query_low, key_low, value_low = attention_backward(
+        queries, key_side, value_proj, segment_row, softmax_stats, grad_context
     )
     ffn_rows, query_low, key_low, value_low = lax.optimization_barrier(
         (ffn_rows, query_low, key_low, value_low)

time: 569 us -> 525 us (0.923); the launches traced: 557 us -> 519 us
  matrix products: 235 us -> 112 us
  Pallas kernels: 0 us -> 95.3 us
  other arithmetic: 84.2 us -> 35.3 us
  waiting for transfers between devices: 99.2 us -> 146 us
  local copies, waits for them, and re-layouts: 66.6 us -> 58.3 us
    dot_general x28 -> x0, matrix products: 124 us -> none  [the longest x4 32.6 us: one_group(): jnp.einsum('qhd,khd->hqk', grad_group, value_group, preferred_element_typ...]
    pallas_call x0 -> x2, Pallas kernels: none -> 95.3 us  [the longest x1 60.2 us: attention_backward(): pl.pallas_call(attn_bwd_kernel, out_shape=tuple((jax.ShapeDtypeStruct((le...]
    convert_element_type x4 -> x0, other arithmetic: 28.6 us -> none  [one_group(): grad_scores = (probs_full * (grad_probs - inner_sum)).astype(jnp.bfloat16)]
    reduce_scatter x2, waiting for transfers between devices: 42.8 us -> 67.5 us  [scatter_rows(): return lax.psum_scatter(joined, 'dp', scatter_dimension=0, tiled=True)]
    all_gather x2, waiting for transfers between devices: 56.3 us -> 78.2 us  [gather_shards(): gathered = lax.all_gather(mine, 'tensor', axis=0, tiled=False)]
    reduce_sum x4 -> x0, other arithmetic: 15.5 us -> none  [one_group(): row_total = jnp.sum(exp_scores, -1, keepdims=True)]
    unnamed x134 -> x126, local copies, waits for them, and re-layouts: 22.5 us -> 16.9 us
  transfers between devices with their start and end apart: 7 -> 7, of which waited for: 3 -> 4; matrix products, arithmetic and copies ran while one was open for 42% -> 10% of each run, Pallas kernels for 0% -> 18%
where the time goes in v7:
time: 525 us; the launch traced here: 519 us
  waiting for transfers between devices  146 us (28%)
  matrix products  112 us (21%)
  Pallas kernels  95.3 us (18%)
  local copies, waits for them, and re-layouts  58.3 us (11%)
  blocking collectives  57 us (11%)
  other arithmetic  35.3 us (7%)
  between operations  14.9 us (3%)
    all_gather x2, waiting for transfers between devices, gather_shards(): gathered = lax.all_gather(mine, 'tensor', axis=0, tiled=False)  78.2 us
    reduce_scatter x2, waiting for transfers between devices, scatter_rows(): return lax.psum_scatter(joined, 'dp', scatter_dimension=0, tiled=True)  67.5 us
    pallas_call x1, Pallas kernels, attention_backward(): pl.pallas_call(attn_bwd_kernel, out_shape=tuple((jax.ShapeDtypeStruct((le...  60.2 us
    psum x1, blocking collectives, on_device(): lax.psum(jnp.concatenate([grad_query_bias, grad_value_bias, grad_up_bias,...  43.8 us
    dot_general x12, matrix products, contract_last(): lax.dot_general(left_side, right_side, (((1,), (1,)), ((), ())), preferre...  42.8 us
    dot_general x15, matrix products, product(): return jnp.dot(left_side, right_side, preferred_element_type=jnp.float32)  40.3 us
    pallas_call x1, Pallas kernels, attention_forward(): pl.pallas_call(attn_fwd_kernel, out_shape=(jax.ShapeDtypeStruct((length,...  35.2 us
    dot_general x4, matrix products, contract_rows(): lax.dot_general(left_side, right_side, (((0,), (0,)), ((), ())), preferre...  29.3 us
  transfers between devices with their start and end apart: 7, of which 4 were waited for; matrix products, arithmetic and copies ran while one was open for 10% of the time, Pallas kernels for 18%

profile of v7, /device:TPU:0, one launch (start us, length us, event | category | flops | bytes accessed | tf_op | source)
XLA Modules:
  0.0 519.2 jit_solution(15118932134622324969)
XLA Ops:
  10.9 52.5 %all-gather.6.cloned.1.call-done = bf16[4,2,192,768]{3,2,1,0:T(8,128)(2,1)} async-done(((bf16[1,2,192,768]{3,2,1,0:T(8,128)(2,1)}), bf16[4,2,192,768]{3,2,1,0:T(8,128)(2,1)}) %all-gather.6.cloned.1.call-update) | async-done | bytes 2359312 | tf_op jit(solution)/shard_map/all_gather | solution.py:155
  63.5 13.1 %all-gather.2 = f32[4,1,1152]{2,1,0:T(1,128)S(1)} all-gather(f32[1,1,1152]{2,1,0:T(1,128)S(1)} %reshape.215), channel_id=2, replica_groups=mesh['dp'=8,'tensor'=4] {'tensor'}, dimensions={0}, use_global_device_ids=true | all-gather | bytes 23040 | tf_op jit(solution)/shard_map/all_gather | solution.py:230
  92.4 35.2 %shard_map.305 = (bf16[1024,768]{1,0:T(8,128)(2,1)}, f32[1024,128]{1,0:T(8,128)}) custom-call(bf16[1024,768]{1,0:T(8,128)(2,1)} %add_convert_fusion.2.q_ref, bf16[1024,768]{1,0:T(8,128)(2,1)} %convolution_convert_fusion.11.k_ref, bf16[1024,768]{1,0:T(8,128)(2,1)} %add_convert_fusion.1.v_ref, s32[1024,1]{1,0:T(8,128)} %copy.87.segq_ref, ...), custom_call_target="tpu_custom_call" | custom-call | flops 3221225472 | bytes 6291456 | tf_op jit(solution)/shard_map/pallas_call | solution.py:112
  127.6 25.7 %all-gather.8.cloned.1.call-done = bf16[3072,768]{1,0:T(8,128)(2,1)} async-done(((bf16[768,768]{1,0:T(8,128)(2,1)}), bf16[3072,768]{1,0:T(8,128)(2,1)}) %all-gather.8.cloned.1.call-update) | async-done | bytes 4718608 | tf_op jit(solution)/shard_map/all_gather | solution.py:155
  166.6 8.5 %broadcast_select_fusion = (bf16[4,1,768,768]{3,2,0,1:T(8,128)(2,1)}, bf16[4,1,768,768]{3,2,0,1:T(8,128)(2,1)}) fusion(bf16[4,1,768,768]{3,2,0,1:T(8,128)(2,1)} %collective-permute-done.1, bf16[4,1,768,768]{3,2,0,1:T(8,128)(2,1)} %bitcast.165, pred[]{:T(512)S(6)} %eq.2), kind=kLoop, calls=%fused_computation.17 | loop fusion | flops 4718592 | bytes 18874368 | tf_op jit(solution)/shard_map/jit(_where)/select_n | solution.py:159
  175.1 5.4 %multiply_convert_fusion.3 = (bf16[1024,768]{0,1:T(8,128)(2,1)S(1)}, f32[1024,768]{0,1:T(8,128)}) fusion(f32[768]{0:T(1024)S(1)} %get-tuple-element.104, bf16[1024,768]{0,1:T(8,128)(2,1)S(1)} %fusion.46, bf16[4,1,768,768]{3,2,0,1:T(8,128)(2,1)} %get-tuple-element.108), kind=kOutput, calls=%fused_computation.75 | convolution fusion | flops 1215823872 | bytes 7474176 | tf_op jit(solution)/shard_map/dot_general | solution.py:15
  180.5 3.9 multiply_convert_fusion.2
  187.4 4.3 multiply_convert_fusion.1
  193.2 3.9 multiply_convert_fusion
  201.2 3.4 fusion.45
  204.6 10.5 %fusion.8 = bf16[768,3072]{1,0:T(8,128)(2,1)} fusion(bf16[1024,768]{0,1:T(8,128)(2,1)} %get-tuple-element.109, bf16[1024,768]{0,1:T(8,128)(2,1)} %copy-done.40, bf16[1024,768]{0,1:T(8,128)(2,1)} %copy-done.43, bf16[1024,768]{0,1:T(8,128)(2,1)} %copy-done.42, bf16[1024,768]{0,1:T(8,128)(2,1)} %copy-done.41), kind=kOutput, calls=%fused_computation.11 | convolution fusion | flops 4859363328 | bytes 12582912 | tf_op jit(solution)/shard_map/dot_general | solution.py:19
  215.1 5.2 %fusion.23 = bf16[1024,768]{0,1:T(8,128)(2,1)S(1)} fusion(f32[1024,768]{0,1:T(8,128)} %get-tuple-element.153, f32[768]{0:T(1024)S(1)} %get-tuple-element.104, bf16[1024,768]{0,1:T(8,128)(2,1)} %get-tuple-element.109, bf16[4,1,768,768]{3,2,0,1:T(8,128)(2,1)S(1)} %bitcast.167), kind=kOutput, calls=%fused_computation.39 | convolution fusion | flops 1224474624 | bytes 7475200 | tf_op jit(solution)/shard_map/dot_general | solution.py:25
  220.3 3.2 fusion.30
  223.6 3.6 fusion.37
  227.2 4.9 fusion.44
  232.2 3.0 fusion.47
  235.2 3.0 fusion.50
  238.3 3.0 fusion.53
  241.3 12.1 %convolution_convert_fusion = bf16[768,3072]{1,0:T(8,128)(2,1)} fusion(bf16[1024,768]{0,1:T(8,128)(2,1)} %copy-done.24, bf16[1024,768]{0,1:T(8,128)(2,1)S(1)} %fusion.44, bf16[1024,768]{0,1:T(8,128)(2,1)} %copy-done.23, bf16[1024,768]{0,1:T(8,128)(2,1)S(1)} %copy-done.22, bf16[1024,768]{0,1:T(8,128)(2,1)S(1)} %copy-done.20), kind=kOutput, calls=%fused_computation.10 | convolution fusion | flops 4859363328 | bytes 12582912 | tf_op jit(solution)/shard_map/dot_general | solution.py:19
  253.4 6.2 %multiply_reduce_fusion = (f32[768]{0:T(1024)S(1)}, f32[1024]{0:T(1024)S(1)}, f32[1024]{0:T(1024)S(1)}, f32[768]{0:T(1024)S(1)}, f32[1024,768]{0,1:T(8,128)S(1)}) fusion(f32[1024,768]{0,1:T(8,128)S(1)} %get-tuple-element.147, f32[1024]{0:T(1024)S(1)} %add_rsqrt_fusion.1, f32[1024]{0:T(1024)S(1)} %broadcast_multiply_fusion.5, f32[768]{0:T(1024)S(1)} %copy-done.32, ...), kind=kOutput, calls=%fused_computation.62 | convolution fusion | flops 1224471040 | bytes 23246848 | tf_op jit(solution)/shard_map/dot_general | solution.py:25
  271.2 16.2 %concatenate.36 = bf16[768,7168]{1,0:T(8,128)(2,1)} concatenate(bf16[768,768]{1,0:T(8,128)(2,1)} %get-tuple-element.117, bf16[768,768]{1,0:T(8,128)(2,1)} %get-tuple-element.113, bf16[768,192]{1,0:T(8,128)(2,1)} %get-tuple-element.128, bf16[768,64]{1,0:T(8,128)(2,1)S(1)} %broadcast.108, bf16[768,768]{1,0:T(8,128)(2,1)} %get-tuple-element.116, ...), dimensions={1} | concatenate | bytes 22020096 | tf_op jit(solution)/shard_map/concatenate | solution.py:174
  287.5 60.2 %shard_map.306 = (bf16[1024,768]{1,0:T(8,128)(2,1)}, bf16[1024,768]{1,0:T(8,128)(2,1)}, bf16[1024,768]{1,0:T(8,128)(2,1)}) custom-call(bf16[1024,768]{1,0:T(8,128)(2,1)} %add_convert_fusion.2.q_ref, bf16[1024,768]{1,0:T(8,128)(2,1)} %convolution_convert_fusion.11.k_ref, bf16[1024,768]{1,0:T(8,128)(2,1)} %add_convert_fusion.1.v_ref, ...), custom_call_target="tpu_custom_call" | custom-call | flops 8053063680 | bytes 11010048 | tf_op jit(solution)/shard_map/pallas_call | solution.py:134
  347.7 22.5 %reduce-scatter.4.cloned.1.call-done = bf16[96,7168]{1,0:T(8,128)(2,1)} async-done(((bf16[768,7168]{1,0:T(8,128)(2,1)}), bf16[96,7168]{1,0:T(8,128)(2,1)}) %reduce-scatter.4.cloned.1.call-update) | async-done | bytes 1376272 | tf_op jit(solution)/shard_map/reduce_scatter | solution.py:178
  379.9 5.4 %convolution_convert_fusion.1 = bf16[768,2304]{1,0:T(8,128)(2,1)} fusion(bf16[1024,768]{1,0:T(8,128)(2,1)S(1)} %copy-done.11, bf16[1024,2304]{0,1:T(8,128)(2,1)S(1)} %bitcast.163), kind=kOutput, calls=%fused_computation.12 | convolution fusion | flops 3625648128 | bytes 9830400 | tf_op jit(solution)/shard_map/dot_general | solution.py:19
  385.4 3.2 copy.127
  388.6 45.0 %reduce-scatter.6.cloned.1.call-done = bf16[96,2304]{1,0:T(8,128)(2,1)} async-done(((bf16[768,2304]{1,0:T(8,128)(2,1)}), bf16[96,2304]{1,0:T(8,128)(2,1)}) %reduce-scatter.6.cloned.1.call-update) | async-done | bytes 442384 | tf_op jit(solution)/shard_map/reduce_scatter | solution.py:178
  435.7 3.0 pad_maximum_fusion.1
  438.7 4.5 convert_reduce_fusion
  447.0 43.8 %psum.7 = f32[9216]{0:T(1024)S(1)} all-reduce(f32[9216]{0:T(1024)S(1)} %constant_dynamic-update-slice_fusion), channel_id=1, replica_groups=mesh['dp'=8,'tensor'=4] {'dp','tensor'}, use_global_device_ids=true, to_apply=%region_20.21 | all-reduce | flops 9216 | bytes 73728 | tf_op jit(solution)/shard_map/psum | solution.py:329
  490.9 2.9 fusion.80
  496.0 3.5 add_add_fusion
  499.5 3.6 copy.109
  (208 shorter events, 79.9 us)
Async XLA Ops:
  7.2 69.7 %copy-start = (s32[4,1024]{1,0:T(4,128)S(1)}, s32[4,1024]{1,0:T(4,128)}, u32[]{:S(2)}) copy-start(s32[4,1024]{1,0:T(4,128)} %param.19) | copy-start | bytes 49156
  7.2 56.2 %all-gather.6.cloned.1.call-start = ((), (), s32[]{:S(2)}) async-start(), calls=%async_computation.3 | async-start | bytes 2949120 | tf_op jit(solution)/shard_map/all_gather | solution.py:155
  7.3 56.1 %copy-start.36 = (f32[768]{0:T(1024)S(1)}, f32[768]{0:T(1024)}, u32[]{:S(2)}) copy-start(f32[768]{0:T(1024)} %param.30) | copy-start | bytes 9220
  7.3 56.1 %copy-start.37 = (f32[192]{0:T(256)S(1)}, f32[192]{0:T(256)}, u32[]{:S(2)}) copy-start(f32[192]{0:T(256)} %param.21) | copy-start | bytes 2308
  7.3 56.1 %copy-start.38 = (f32[192]{0:T(256)S(1)}, f32[192]{0:T(256)}, u32[]{:S(2)}) copy-start(f32[192]{0:T(256)} %param.24) | copy-start | bytes 2308
  9.6 143.6 %all-gather.8.cloned.1.call-start = ((), (), s32[]{:S(2)}) async-start(), calls=%async_computation.7 | async-start | bytes 5898240 | tf_op jit(solution)/shard_map/all_gather | solution.py:155
  10.9 359.4 %reduce-scatter.4.cloned.1.call-start = ((), (), s32[]{:S(2)}) async-start(), calls=%async_computation.4 | async-start | bytes 12386304 | tf_op jit(solution)/shard_map/reduce_scatter | solution.py:178
  63.4 16.8 %collective-permute-start = (bf16[4,2,192,768]{3,2,1,0:T(8,128)(2,1)}, bf16[4,2,192,768]{3,2,1,0:T(8,128)(2,1)}, u32[]{:S(2)}, u32[]{:S(2)}) collective-permute-start(bf16[4,2,192,768]{3,2,1,0:T(8,128)(2,1)} %all-gather.6.cloned.1.call-done), channel_id=1, source_target_pairs={{0,4},{4,0},{8,12},{12,8},{16,20},{20,16},{24,28},{28,24},{1,5},{5... | collective-permute-start | bytes 7077896 | tf_op jit(solution)/shard_map/ppermute | solution.py:158
  80.2 73.1 %copy-start.10 = (bf16[1024,768]{1,0:T(8,128)(2,1)}, bf16[1024,768]{1,0:T(8,128)(2,1)S(1)}, u32[]{:S(2)}) copy-start(bf16[1024,768]{1,0:T(8,128)(2,1)S(1)} %constant_dynamic-slice_fusion.3) | copy-start | bytes 4718596
  84.5 5.3 %copy-start.27 = (bf16[4,1,192,768]{3,2,1,0:T(8,128)(2,1)}, bf16[4,1,192,768]{3,2,1,0:T(8,128)(2,1)S(1)}, u32[]{:S(2)}) copy-start(bf16[4,1,192,768]{3,2,1,0:T(8,128)(2,1)S(1)} %get-tuple-element.159) | copy-start | bytes 3538948
  153.3 13.3 %collective-permute-start.1 = (bf16[4,1,768,768]{3,2,0,1:T(8,128)(2,1)}, bf16[4,1,768,768]{3,2,0,1:T(8,128)(2,1)}, u32[]{:S(2)}, u32[]{:S(2)}) collective-permute-start(bf16[4,1,768,768]{3,2,0,1:T(8,128)(2,1)} %bitcast.164), channel_id=1, source_target_pairs={{0,4},{4,0},{8,12},{12,8},{16,20},{20,16},{24,28},{28,24},{1,5},{5... | collective-permute-start | bytes 14155784 | tf_op jit(solution)/shard_map/ppermute | solution.py:158
  157.4 3.9 copy-start.15
  157.4 5.5 %copy-start.12 = (bf16[1024,768]{0,1:T(8,128)(2,1)S(1)}, bf16[1024,768]{0,1:T(8,128)(2,1)}, u32[]{:S(2)}) copy-start(bf16[1024,768]{0,1:T(8,128)(2,1)} %copy.130) | copy-start | bytes 4718596
  157.4 5.5 %copy-start.34 = (f32[768]{0:T(1024)S(1)}, f32[768]{0:T(1024)}, u32[]{:S(2)}) copy-start(f32[768]{0:T(1024)} %param.26) | copy-start | bytes 9220
  166.6 26.6 %copy-start.24 = (bf16[1024,768]{0,1:T(8,128)(2,1)}, bf16[1024,768]{0,1:T(8,128)(2,1)S(1)}, u32[]{:S(2)}) copy-start(bf16[1024,768]{0,1:T(8,128)(2,1)S(1)} %fusion.46) | copy-start | bytes 4718596
  175.1 5.4 %copy-start.6 = (bf16[4,1,768,768]{3,2,0,1:T(8,128)(2,1)S(1)}, bf16[4,1,768,768]{3,2,0,1:T(8,128)(2,1)}, u32[]{:S(2)}) copy-start(bf16[4,1,768,768]{3,2,0,1:T(8,128)(2,1)} %get-tuple-element.108) | copy-start | bytes 14155780
  175.1 9.3 %slice-start.4 = ((s8[4718592]{0:T(1024)(128)(4,1)}), s8[4194304]{0:T(1024)(128)(4,1)S(1)}, s32[]{:S(2)}) async-start(s8[4718592]{0:T(1024)(128)(4,1)} %bitcast.166), calls=%async_computation.12 | async-start | bytes 8388608
  193.2 3.9 copy-start.39
  215.1 5.2 %copy-start.17 = (bf16[1024,768]{0,1:T(8,128)(2,1)S(1)}, bf16[1024,768]{0,1:T(8,128)(2,1)}, u32[]{:S(2)}) copy-start(bf16[1024,768]{0,1:T(8,128)(2,1)} %get-tuple-element.109) | copy-start | bytes 4718596
  215.1 5.3 %copy-start.44 = (f32[1024,768]{0,1:T(8,128)S(1)}, f32[1024,768]{0,1:T(8,128)}, u32[]{:S(2)}) copy-start(f32[1024,768]{0,1:T(8,128)} %get-tuple-element.151) | copy-start | bytes 9437188
  220.3 11.9 %copy-start.19 = (bf16[1024,768]{0,1:T(8,128)(2,1)}, bf16[1024,768]{0,1:T(8,128)(2,1)S(1)}, u32[]{:S(2)}) copy-start(bf16[1024,768]{0,1:T(8,128)(2,1)S(1)} %fusion.23) | copy-start | bytes 4718596
  223.6 11.7 %copy-start.21 = (bf16[1024,768]{0,1:T(8,128)(2,1)}, bf16[1024,768]{0,1:T(8,128)(2,1)S(1)}, u32[]{:S(2)}) copy-start(bf16[1024,768]{0,1:T(8,128)(2,1)S(1)} %fusion.30) | copy-start | bytes 4718596
  227.2 11.0 %copy-start.23 = (bf16[1024,768]{0,1:T(8,128)(2,1)}, bf16[1024,768]{0,1:T(8,128)(2,1)S(1)}, u32[]{:S(2)}) copy-start(bf16[1024,768]{0,1:T(8,128)(2,1)S(1)} %fusion.37) | copy-start | bytes 4718596
  232.2 21.2 %copy-start.8 = (bf16[1024,768]{0,1:T(8,128)(2,1)}, bf16[1024,768]{0,1:T(8,128)(2,1)S(1)}, u32[]{:S(2)}) copy-start(bf16[1024,768]{0,1:T(8,128)(2,1)S(1)} %fusion.44) | copy-start | bytes 4718596
  259.6 7.5 %slice-start = ((s8[4718592]{0:T(1024)(128)(4,1)}), s8[4194304]{0:T(1024)(128)(4,1)S(1)}, s32[]{:S(2)}) async-start(s8[4718592]{0:T(1024)(128)(4,1)} %bitcast.159), calls=%async_computation.8 | async-start | bytes 8388608
  260.8 6.4 %slice-start.1 = ((s8[4718592]{0:T(1024)(128)(4,1)}), s8[524288]{0:T(1024)(128)(4,1)S(1)}, s32[]{:S(2)}) async-start(s8[4718592]{0:T(1024)(128)(4,1)} %bitcast.159), calls=%async_computation.9 | async-start | bytes 1048576
  287.5 146.2 %reduce-scatter.6.cloned.1.call-start = ((), (), s32[]{:S(2)}) async-start(), calls=%async_computation.5 | async-start | bytes 3981312 | tf_op jit(solution)/shard_map/reduce_scatter | solution.py:178
  370.2 4.5 copy-start.3
  385.4 119.6 %reduce-scatter.8.cloned.1.call-start = ((), (), s32[]{:S(2)}) async-start(), calls=%async_computation.6 | async-start | bytes 3031040 | tf_op jit(solution)/shard_map/reduce_scatter | solution.py:186
  438.7 4.5 copy-start.7
  444.8 46.1 %copy-start.9 = (bf16[1024,768]{1,0:T(8,128)(2,1)S(1)}, bf16[1024,768]{1,0:T(8,128)(2,1)}, u32[]{:S(2)}) copy-start(bf16[1024,768]{1,0:T(8,128)(2,1)} %get-tuple-element.37) | copy-start | bytes 4718596
  499.5 12.9 %copy-start.1 = (s32[4,1024]{1,0:T(4,128)S(1)}, s32[4,1024]{1,0:T(4,128)}, u32[]{:S(2)}) copy-start(s32[4,1024]{1,0:T(4,128)} %param.19) | copy-start | bytes 49156
  (28 other events, 64.1 us)
Sparse Core Ops, SparseCore 0:
  10.2 53.1 all-gather.5
  65.0 88.2 all-gather.7
  287.6 82.5 reduce-scatter.3
  385.5 48.0 reduce-scatter.5
  438.8 49.9 reduce-scatter.7

commit v8 on v7

--- a/solution.py
+++ b/solution.py
@@ -160,37 +160,28 @@
     return [half[:, index] for half in halves for index in range(half.shape[1])]
 
 
-def by_parts(grads):
+def scatter_rows(grads):
+    joined = jnp.concatenate([grad.astype(jnp.bfloat16) for grad in grads], axis=1)
+    return lax.psum_scatter(joined, "dp", scatter_dimension=0, tiled=True)
+
+
+def scatter_parts(partials, counts):
     parts = lax.axis_size("tensor")
-    columns = []
-    for part in range(parts):
-        used = 0
-        for grad in grads:
-            width = grad.shape[1] // parts
-            columns.append(grad[:, part * width : (part + 1) * width].astype(jnp.bfloat16))
-            used += width
-        if used % 128:
-            columns.append(jnp.zeros((grads[0].shape[0], 128 - used % 128), jnp.bfloat16))
-    return jnp.concatenate(columns, axis=1)
-
-
-def scatter_rows(joined):
-    return lax.psum_scatter(joined, "dp", scatter_dimension=0, tiled=True)
-
-
-def scatter_parts(partials, widths):
-    parts = lax.axis_size("tensor")
-    joined = jnp.concatenate(
-        [partial.reshape(partial.shape[0], parts, -1) for partial in partials], axis=2
-    )
-    summed = lax.psum_scatter(joined, "tensor", scatter_dimension=1, tiled=True)[:, 0]
+    flat = []
+    for partial, count in zip(partials, counts):
+        rows, width = partial.shape
+        split = partial.reshape(rows, count, parts, width // (count * parts)).transpose(2, 1, 0, 3)
+        flat.append(split.reshape(parts, -1))
+    joined = jnp.concatenate(flat, axis=1).reshape(-1, 128)
+    summed = lax.psum_scatter(joined, "tensor", scatter_dimension=0, tiled=True).reshape(-1)
     pieces = []
     start = 0
-    for partial, group in zip(partials, widths):
-        for width in group:
-            pieces.append(summed[:, start : start + width].astype(jnp.float32))
-            start += width
-        start += partial.shape[1] // parts - sum(group)
+    for partial, count in zip(partials, counts):
+        rows, width = partial.shape
+        size = rows * width // parts
+        block = summed[start : start + size].reshape(count, rows, -1).astype(jnp.float32)
+        pieces.extend(block[index] for index in range(count))
+        start += size
     return pieces
 
 
@@ -287,6 +278,11 @@
     grad_pre = jnp.concatenate(grad_pre_parts, axis=1)
     hidden_low = jnp.concatenate(hidden_parts, axis=1)
     grad_up_bias = jnp.sum(grad_pre, 0, dtype=jnp.float32)
+    ffn_grads = [contract_rows(first_low, grad_pre), contract_rows(down_low, hidden_low)]
+    ffn_joined, first_grad = lax.optimization_barrier(
+        (jnp.concatenate([grad.astype(jnp.bfloat16) for grad in ffn_grads], axis=1), first_grad)
+    )
+    ffn_rows = scatter_rows([ffn_joined])
     grad_first_gain = jnp.sum(first_grad * first_unit, 0)
     grad_first_shift = jnp.sum(first_grad, 0)
     attn_grad = normalize_back(first_grad, first_unit, first_inv, first_gain)
@@ -295,14 +291,7 @@
     grad_context = contract_last(attn_grad_low, o_sh.reshape(-1, o_sh.shape[2])).astype(
         jnp.bfloat16
     )
-    ffn_grads = [
-        contract_rows(first_low, grad_pre),
-        contract_rows(down_low, hidden_low),
-        contract_rows(attn_grad_low, context),
-    ]
-    ffn_widths = [grad.shape[1] // part_count for grad in ffn_grads]
-    ffn_joined, grad_context = lax.optimization_barrier((by_parts(ffn_grads), grad_context))
-    ffn_rows = scatter_rows(ffn_joined)
+    output_grad_t = contract_rows(attn_grad_low, context)
     query_low, key_low, value_low = attention_backward(
         queries, key_side, value_proj, segment_row, softmax_stats, grad_context
     )
@@ -311,15 +300,15 @@
     )
     grad_query_bias = jnp.sum(query_low, 0, dtype=jnp.float32)
     grad_value_bias = jnp.sum(value_low, 0, dtype=jnp.float32)
-    qkv_low = jnp.stack([query_low, key_low, value_low], axis=1)
-    qkv_low = qkv_low.reshape(row_len, 3, part_count, -1).transpose(0, 2, 1, 3)
-    qkv_grads = contract_rows(input_rows, qkv_low.reshape(row_len, -1)).astype(jnp.bfloat16)
-    qkv_widths = [qkv_grads.shape[1] // part_count]
-    summed = scatter_parts(
-        [ffn_rows, scatter_rows(qkv_grads)], [ffn_widths, qkv_widths]
-    )
-    ffn_summed = summed[:3]
-    attn_summed = summed[3].reshape(summed[3].shape[0], 3, -1)
+    attn_rows = scatter_rows(
+        [
+            contract_rows(input_rows, query_low),
+            contract_rows(input_rows, key_low),
+            contract_rows(input_rows, value_low),
+            output_grad_t,
+        ]
+    )
+    summed = scatter_parts([ffn_rows, attn_rows], [2, 4])
     input_grad = (
         attn_grad
         + product(query_low, qt_full)
@@ -358,18 +347,18 @@
     return (
         layer_output,
         input_grad,
-        attn_summed[:, 0],
+        summed[2],
         query_bias_grad,
-        attn_summed[:, 1],
-        attn_summed[:, 2],
+        summed[3],
+        summed[4],
         value_bias_grad,
-        ffn_summed[2].T,
+        summed[5].T,
         shared[0],
         shared[1],
         shared[2],
-        ffn_summed[0],
+        summed[0],
         up_bias_grad,
-        ffn_summed[1].T,
+        summed[1].T,
         shared[3],
         shared[4],
         shared[5],

time: 525 us -> 496 us (0.945)
  waiting for transfers between devices: 146 us -> 125 us
  local copies, waits for them, and re-layouts: 58.3 us -> 46.6 us
  other arithmetic: 35.3 us -> 41.3 us
    reduce_scatter x2 -> x1, waiting for transfers between devices: 67.5 us -> 3.81 us  [scatter_rows(): return lax.psum_scatter(joined, 'dp', scatter_dimension=0, tiled=True)]
    unnamed x5 -> x6, waiting for transfers between devices: 0.08 us -> 42.5 us
    concatenate x1 -> x0, local copies, waits for them, and re-layouts: 16.2 us -> none  [by_parts(): return jnp.concatenate(columns, axis=1)]
    unnamed x126 -> x127, local copies, waits for them, and re-layouts: 16.9 us -> 27.3 us
    concatenate x1 -> x3, other arithmetic: 2.98 us -> 10.2 us  [the longest x1 3.95 us: on_device(): jnp.concatenate([grad.astype(jnp.bfloat16) for grad in ffn_grads], axis=1)]
    optimization_barrier x3 -> x0, local copies, waits for them, and re-layouts: 6.15 us -> none  [on_device(): lax.optimization_barrier((ffn_rows, query_low, key_low, value_low))]
    slice x4 -> x2, local copies, waits for them, and re-layouts: 6.11 us -> 0.06 us  [scatter_parts(): pieces.extend((block[index] for index in range(count)))]
    dot_general x4 -> x6, matrix products: 29.3 us -> 26.4 us  [contract_rows(): lax.dot_general(left_side, right_side, (((0,), (0,)), ((), ())), preferre...]
  transfers between devices with their start and end apart: 7 -> 7, of which waited for: 4 -> 4; matrix products, arithmetic and copies ran while one was open for 10% -> 13% of each run, Pallas kernels for 18% -> 20%
where the time goes in v8:
time: 496 us; the launch traced here: 491 us
  waiting for transfers between devices  125 us (25%)
  matrix products  109 us (22%)
  Pallas kernels  96.5 us (19%)
  blocking collectives  56.9 us (11%)
  local copies, waits for them, and re-layouts  46.6 us (9%)
  other arithmetic  41.3 us (8%)
  between operations  15.2 us (3%)
    all_gather x2, waiting for transfers between devices, gather_shards(): gathered = lax.all_gather(mine, 'tensor', axis=0, tiled=False)  78.8 us
    pallas_call x1, Pallas kernels, attention_backward(): pl.pallas_call(attn_bwd_kernel, out_shape=tuple((jax.ShapeDtypeStruct((le...  61.3 us
    dot_general x12, matrix products, contract_last(): lax.dot_general(left_side, right_side, (((1,), (1,)), ((), ())), preferre...  46.2 us
    psum x1, blocking collectives, on_device(): lax.psum(jnp.concatenate([grad_query_bias, grad_value_bias, grad_up_bias,...  43.8 us
    unnamed x6, waiting for transfers between devices  42.5 us
    dot_general x15, matrix products, product(): return jnp.dot(left_side, right_side, preferred_element_type=jnp.float32)  36.2 us
    pallas_call x1, Pallas kernels, attention_forward(): pl.pallas_call(attn_fwd_kernel, out_shape=(jax.ShapeDtypeStruct((length,...  35.2 us
    unnamed x127, local copies, waits for them, and re-layouts  27.3 us
  transfers between devices with their start and end apart: 7, of which 4 were waited for; matrix products, arithmetic and copies ran while one was open for 13% of the time, Pallas kernels for 20%

profile of v8, /device:TPU:0, one launch (start us, length us, event | category | flops | bytes accessed | tf_op | source)
XLA Modules:
  0.0 490.7 jit_solution(13372248217387494667)
XLA Ops:
  10.9 52.5 %all-gather.6.cloned.1.call-done = bf16[4,2,192,768]{3,2,1,0:T(8,128)(2,1)} async-done(((bf16[1,2,192,768]{3,2,1,0:T(8,128)(2,1)}), bf16[4,2,192,768]{3,2,1,0:T(8,128)(2,1)}) %all-gather.6.cloned.1.call-update) | async-done | bytes 2359312 | tf_op jit(solution)/shard_map/all_gather | solution.py:155
  63.5 13.1 %all-gather.2 = f32[4,1,1152]{2,1,0:T(1,128)S(1)} all-gather(f32[1,1,1152]{2,1,0:T(1,128)S(1)} %reshape.227), channel_id=2, replica_groups=mesh['dp'=8,'tensor'=4] {'tensor'}, dimensions={0}, use_global_device_ids=true | all-gather | bytes 23040 | tf_op jit(solution)/shard_map/all_gather | solution.py:221
  92.3 35.2 %shard_map.305 = (bf16[1024,768]{1,0:T(8,128)(2,1)}, f32[1024,128]{1,0:T(8,128)}) custom-call(bf16[1024,768]{1,0:T(8,128)(2,1)} %add_convert_fusion.2.q_ref, bf16[1024,768]{1,0:T(8,128)(2,1)} %convolution_convert_fusion.10.k_ref, bf16[1024,768]{1,0:T(8,128)(2,1)} %add_convert_fusion.1.v_ref, s32[1024,1]{1,0:T(8,128)} %copy.63.segq_ref, ...), custom_call_target="tpu_custom_call" | custom-call | flops 3221225472 | bytes 6291456 | tf_op jit(solution)/shard_map/pallas_call | solution.py:112
  127.5 26.3 %all-gather.8.cloned.1.call-done = bf16[3072,768]{1,0:T(8,128)(2,1)} async-done(((bf16[768,768]{1,0:T(8,128)(2,1)}), bf16[3072,768]{1,0:T(8,128)(2,1)}) %all-gather.8.cloned.1.call-update) | async-done | bytes 4718608 | tf_op jit(solution)/shard_map/all_gather | solution.py:155
  170.0 7.1 %broadcast_select_fusion = (bf16[4,1,768,768]{3,2,0,1:T(8,128)(2,1)}, bf16[4,1,768,768]{3,2,0,1:T(8,128)(2,1)S(1)}) fusion(bf16[4,1,768,768]{3,2,0,1:T(8,128)(2,1)} %collective-permute-done.1, bf16[4,1,768,768]{3,2,0,1:T(8,128)(2,1)} %bitcast.150, pred[]{:T(512)S(6)} %eq.2), kind=kLoop, calls=%fused_computation.17 | loop fusion | flops 4718592 | bytes 18874368 | tf_op jit(solution)/shard_map/jit(_where)/select_n | solution.py:159
  177.1 3.9 multiply_convert_fusion
  181.0 3.9 multiply_convert_fusion.1
  184.9 3.9 multiply_convert_fusion.2
  192.2 3.9 multiply_convert_fusion.3
  203.7 3.1 fusion.45
  206.8 8.9 %fusion.8 = bf16[768,3072]{1,0:T(8,128)(2,1)S(1)} fusion(bf16[1024,768]{0,1:T(8,128)(2,1)S(1)} %get-tuple-element.109, bf16[1024,768]{0,1:T(8,128)(2,1)} %copy-done.45, bf16[1024,768]{0,1:T(8,128)(2,1)} %copy-done.46, bf16[1024,768]{0,1:T(8,128)(2,1)} %copy-done.47, bf16[1024,768]{0,1:T(8,128)(2,1)} %copy-done.48), kind=kOutput, calls=%fused_computation.12 | convolution fusion | flops 4859363328 | bytes 12582912 | tf_op jit(solution)/shard_map/dot_general | solution.py:19
  215.7 4.7 fusion.23
  220.4 3.2 fusion.30
  223.7 3.2 fusion.37
  227.0 5.6 %fusion.44 = bf16[1024,768]{0,1:T(8,128)(2,1)S(1)} fusion(f32[1024,768]{0,1:T(8,128)S(1)} %copy-done.49, f32[768]{0:T(1024)S(1)} %get-tuple-element.101, bf16[1024,768]{0,1:T(8,128)(2,1)} %copy-done.21, bf16[4,1,768,768]{3,2,0,1:T(8,128)(2,1)S(1)} %bitcast.152), kind=kOutput, calls=%fused_computation.60 | convolution fusion | flops 1224474624 | bytes 7475200 | tf_op jit(solution)/shard_map/dot_general | solution.py:25
  232.7 3.1 fusion.47
  235.7 3.0 fusion.50
  238.8 3.1 fusion.53
  241.8 9.2 %convolution_convert_fusion = bf16[768,3072]{1,0:T(8,128)(2,1)S(1)} fusion(bf16[1024,768]{0,1:T(8,128)(2,1)} %copy-done.27, bf16[1024,768]{0,1:T(8,128)(2,1)S(1)} %fusion.44, bf16[1024,768]{0,1:T(8,128)(2,1)} %copy-done.26, bf16[1024,768]{0,1:T(8,128)(2,1)} %copy-done.25, bf16[1024,768]{0,1:T(8,128)(2,1)} %copy-done.24), kind=kOutput, calls=%fused_computation.11 | convolution fusion | flops 4859363328 | bytes 12582912 | tf_op jit(solution)/shard_map/dot_general | solution.py:19
  251.0 4.0 pad_maximum_fusion
  254.9 9.6 %add_add_fusion.1 = f32[1024,768]{0,1:T(8,128)} fusion(f32[1024,768]{0,1:T(8,128)} %fusion.53, f32[1024,768]{0,1:T(8,128)} %fusion.50, f32[1024,768]{0,1:T(8,128)} %fusion.47, bf16[1024,768]{0,1:T(8,128)(2,1)} %copy-done.12, bf16[4,1,768,768]{3,2,0,1:T(8,128)(2,1)} %copy-done.8, f32[1024]{0:T(1024)S(1)} %broadcast_multiply_fusion.2, ...), kind=kOutput, calls=%fused_computation.68 | convolution fusion | flops 1217396736 | bytes 20073472 | tf_op jit(solution)/shard_map/dot_general | solution.py:25
  264.7 3.2 multiply_reduce_fusion
  274.7 61.3 %shard_map.306 = (bf16[1024,768]{1,0:T(8,128)(2,1)}, bf16[1024,768]{1,0:T(8,128)(2,1)}, bf16[1024,768]{1,0:T(8,128)(2,1)}) custom-call(bf16[1024,768]{1,0:T(8,128)(2,1)} %add_convert_fusion.2.q_ref, bf16[1024,768]{1,0:T(8,128)(2,1)} %convolution_convert_fusion.10.k_ref, bf16[1024,768]{1,0:T(8,128)(2,1)} %add_convert_fusion.1.v_ref, ...), custom_call_target="tpu_custom_call" | custom-call | flops 8053063680 | bytes 11010048 | tf_op jit(solution)/shard_map/pallas_call | solution.py:134
  336.0 3.8 reduce-scatter.6.cloned.1.call-done
  339.9 3.0 convolution_convert_fusion.13
  348.3 6.6 %copy.85 = bf16[768,3072]{1,0:T(8,128)(2,1)} copy(bf16[768,3072]{0,1:T(8,128)(2,1)} %pad_maximum_fusion.2) | data formatting | bytes 9437184
  357.9 4.5 convert_reduce_fusion
  366.6 42.4 %reduce-scatter.10.cloned.1.call-done = bf16[96,3072]{1,0:T(8,128)(2,1)} async-done(((bf16[768,3072]{1,0:T(8,128)(2,1)}), bf16[96,3072]{1,0:T(8,128)(2,1)}) %reduce-scatter.10.cloned.1.call-update) | async-done | bytes 589840
  412.5 3.7 pad_maximum_fusion.3
  416.2 3.0 reshape.224
  421.4 43.8 %psum.7 = f32[9216]{0:T(1024)S(1)} all-reduce(f32[9216]{0:T(1024)S(1)} %constant_dynamic-update-slice_fusion), channel_id=1, replica_groups=mesh['dp'=8,'tensor'=4] {'dp','tensor'}, use_global_device_ids=true, to_apply=%region_20.21 | all-reduce | flops 9216 | bytes 73728 | tf_op jit(solution)/shard_map/psum | solution.py:318
  465.3 3.0 fusion.80
  (210 shorter events, 86.6 us)
Async XLA Ops:
  7.2 69.7 %copy-start = (s32[4,1024]{1,0:T(4,128)S(1)}, s32[4,1024]{1,0:T(4,128)}, u32[]{:S(2)}) copy-start(s32[4,1024]{1,0:T(4,128)} %param.19) | copy-start | bytes 49156
  7.2 56.2 %all-gather.6.cloned.1.call-start = ((), (), s32[]{:S(2)}) async-start(), calls=%async_computation.3 | async-start | bytes 2949120 | tf_op jit(solution)/shard_map/all_gather | solution.py:155
  7.3 56.1 %copy-start.41 = (f32[768]{0:T(1024)S(1)}, f32[768]{0:T(1024)}, u32[]{:S(2)}) copy-start(f32[768]{0:T(1024)} %param.30) | copy-start | bytes 9220
  7.3 56.1 %copy-start.42 = (f32[192]{0:T(256)S(1)}, f32[192]{0:T(256)}, u32[]{:S(2)}) copy-start(f32[192]{0:T(256)} %param.21) | copy-start | bytes 2308
  7.3 56.1 %copy-start.43 = (f32[192]{0:T(256)S(1)}, f32[192]{0:T(256)}, u32[]{:S(2)}) copy-start(f32[192]{0:T(256)} %param.24) | copy-start | bytes 2308
  9.6 144.2 %all-gather.8.cloned.1.call-start = ((), (), s32[]{:S(2)}) async-start(), calls=%async_computation.6 | async-start | bytes 5898240 | tf_op jit(solution)/shard_map/all_gather | solution.py:155
  10.9 329.0 %reduce-scatter.6.cloned.1.call-start = ((), (), s32[]{:S(2)}) async-start(), calls=%async_computation.4 | async-start | bytes 10616832 | tf_op jit(solution)/shard_map/reduce_scatter | solution.py:165
  63.4 16.8 %collective-permute-start = (bf16[4,2,192,768]{3,2,1,0:T(8,128)(2,1)}, bf16[4,2,192,768]{3,2,1,0:T(8,128)(2,1)}, u32[]{:S(2)}, u32[]{:S(2)}) collective-permute-start(bf16[4,2,192,768]{3,2,1,0:T(8,128)(2,1)} %all-gather.6.cloned.1.call-done), channel_id=1, source_target_pairs={{0,4},{4,0},{8,12},{12,8},{16,20},{20,16},{24,28},{28,24},{1,5},{5... | collective-permute-start | bytes 7077896 | tf_op jit(solution)/shard_map/ppermute | solution.py:158
  80.2 9.5 %copy-start.13 = (bf16[1024,768]{1,0:T(8,128)(2,1)}, bf16[1024,768]{1,0:T(8,128)(2,1)S(1)}, u32[]{:S(2)}) copy-start(bf16[1024,768]{1,0:T(8,128)(2,1)S(1)} %constant_dynamic-slice_fusion.3) | copy-start | bytes 4718596
  82.8 82.9 %copy-start.5 = (bf16[4,2,192,768]{3,2,1,0:T(8,128)(2,1)}, bf16[4,2,192,768]{3,2,1,0:T(8,128)(2,1)S(1)}, u32[]{:S(2)}) copy-start(bf16[4,2,192,768]{3,2,1,0:T(8,128)(2,1)S(1)} %get-tuple-element.110) | copy-start | bytes 7077892
  84.4 5.3 %copy-start.28 = (bf16[4,1,192,768]{3,2,1,0:T(8,128)(2,1)}, bf16[4,1,192,768]{3,2,1,0:T(8,128)(2,1)S(1)}, u32[]{:S(2)}) copy-start(bf16[4,1,192,768]{3,2,1,0:T(8,128)(2,1)S(1)} %get-tuple-element.147) | copy-start | bytes 3538948
  153.8 16.2 %collective-permute-start.1 = (bf16[4,1,768,768]{3,2,0,1:T(8,128)(2,1)}, bf16[4,1,768,768]{3,2,0,1:T(8,128)(2,1)}, u32[]{:S(2)}, u32[]{:S(2)}) collective-permute-start(bf16[4,1,768,768]{3,2,0,1:T(8,128)(2,1)} %bitcast.149), channel_id=1, source_target_pairs={{0,4},{4,0},{8,12},{12,8},{16,20},{20,16},{24,28},{28,24},{1,5},{5... | collective-permute-start | bytes 14155784 | tf_op jit(solution)/shard_map/ppermute | solution.py:158
  161.9 3.8 copy-start.18
  161.9 4.4 copy-start.15
  162.0 4.4 copy-start.39
  170.0 22.2 %copy-start.27 = (bf16[1024,768]{0,1:T(8,128)(2,1)}, bf16[1024,768]{0,1:T(8,128)(2,1)S(1)}, u32[]{:S(2)}) copy-start(bf16[1024,768]{0,1:T(8,128)(2,1)S(1)} %fusion.46) | copy-start | bytes 4718596
  177.1 61.6 %copy-start.8 = (bf16[4,1,768,768]{3,2,0,1:T(8,128)(2,1)}, bf16[4,1,768,768]{3,2,0,1:T(8,128)(2,1)S(1)}, u32[]{:S(2)}) copy-start(bf16[4,1,768,768]{3,2,0,1:T(8,128)(2,1)S(1)} %get-tuple-element.108) | copy-start | bytes 14155780
  181.0 16.6 %copy-start.45 = (bf16[1024,768]{0,1:T(8,128)(2,1)}, bf16[1024,768]{0,1:T(8,128)(2,1)S(1)}, u32[]{:S(2)}) copy-start(bf16[1024,768]{0,1:T(8,128)(2,1)S(1)} %get-tuple-element.143) | copy-start | bytes 4718596
  181.0 7.8 %slice-start = ((s8[4718592]{0:T(1024)(128)(4,1)}), s8[4194304]{0:T(1024)(128)(4,1)S(1)}, s32[]{:S(2)}) async-start(s8[4718592]{0:T(1024)(128)(4,1)} %bitcast.151), calls=%async_computation.8 | async-start | bytes 8388608
  184.9 3.9 copy-start.46
  184.9 3.9 slice-start.1
  206.8 16.9 %copy-start.21 = (bf16[1024,768]{0,1:T(8,128)(2,1)}, bf16[1024,768]{0,1:T(8,128)(2,1)S(1)}, u32[]{:S(2)}) copy-start(bf16[1024,768]{0,1:T(8,128)(2,1)S(1)} %get-tuple-element.109) | copy-start | bytes 4718596
  215.6 4.8 copy-start.51
  220.4 12.2 %copy-start.24 = (bf16[1024,768]{0,1:T(8,128)(2,1)}, bf16[1024,768]{0,1:T(8,128)(2,1)S(1)}, u32[]{:S(2)}) copy-start(bf16[1024,768]{0,1:T(8,128)(2,1)S(1)} %fusion.23) | copy-start | bytes 4718596
  223.7 12.1 %copy-start.25 = (bf16[1024,768]{0,1:T(8,128)(2,1)}, bf16[1024,768]{0,1:T(8,128)(2,1)S(1)}, u32[]{:S(2)}) copy-start(bf16[1024,768]{0,1:T(8,128)(2,1)S(1)} %fusion.30) | copy-start | bytes 4718596
  227.0 11.8 %copy-start.26 = (bf16[1024,768]{0,1:T(8,128)(2,1)}, bf16[1024,768]{0,1:T(8,128)(2,1)S(1)}, u32[]{:S(2)}) copy-start(bf16[1024,768]{0,1:T(8,128)(2,1)S(1)} %fusion.37) | copy-start | bytes 4718596
  232.6 9.2 %copy-start.12 = (bf16[1024,768]{0,1:T(8,128)(2,1)}, bf16[1024,768]{0,1:T(8,128)(2,1)S(1)}, u32[]{:S(2)}) copy-start(bf16[1024,768]{0,1:T(8,128)(2,1)S(1)} %fusion.44) | copy-start | bytes 4718596
  264.6 144.4 %reduce-scatter.10.cloned.1.call-start = ((), (), s32[]{:S(2)}) async-start(), calls=%async_computation.7 | async-start | bytes 5308416
  274.7 65.1 %copy-start.14 = (bf16[1024,768]{1,0:T(8,128)(2,1)S(1)}, bf16[1024,768]{1,0:T(8,128)(2,1)}, u32[]{:S(2)}) copy-start(bf16[1024,768]{1,0:T(8,128)(2,1)} %copy-done.13) | copy-start | bytes 4718596
  354.9 122.3 %reduce-scatter.8.cloned.1.call-start = ((), (), s32[]{:S(2)}) async-start(), calls=%async_computation.5 | async-start | bytes 2211840 | tf_op jit(solution)/shard_map/reduce_scatter | solution.py:176
  419.2 46.0 %copy-start.31 = (bf16[4,1,192,768]{3,2,1,0:T(8,128)(2,1)S(1)}, bf16[4,1,192,768]{3,2,1,0:T(8,128)(2,1)}, u32[]{:S(2)}) copy-start(bf16[4,1,192,768]{3,2,1,0:T(8,128)(2,1)} %copy-done.30) | copy-start | bytes 3538948
  472.9 10.8 %copy-start.1 = (s32[4,1024]{1,0:T(4,128)S(1)}, s32[4,1024]{1,0:T(4,128)}, u32[]{:S(2)}) copy-start(s32[4,1024]{1,0:T(4,128)} %param.19) | copy-start | bytes 49156
  (29 other events, 67.6 us)
Sparse Core Ops, SparseCore 0:
  10.2 53.1 all-gather.5
  65.6 88.2 all-gather.7
  264.7 75.0 reduce-scatter.5
  355.0 53.8 reduce-scatter.9
  419.4 39.4 reduce-scatter.7

commit v9 on v8

--- a/solution.py
+++ b/solution.py
@@ -71,18 +71,21 @@
         stats_ref[:, half + h : half + h + 1] = l
 
 
-def attn_bwd_kernel(q_ref, k_ref, v_ref, dctx_ref, segq_ref, segk_ref, stats_ref,
-                    dq_ref, dk_ref, dv_ref, dk_acc, dv_acc):
+def attn_bwd_kernel(q_ref, k_ref, v_ref, dctx_ref, segq_ref, segk_ref, stats_ref, x_ref, xall_ref,
+                    out_t_ref, dq_ref, dk_ref, dv_ref, wgrad_ref, bias_ref, dk_acc, dv_acc, dwq_acc):
     step = pl.program_id(0)
 
     @pl.when(step == 0)
     def _():
         dk_acc[...] = jnp.zeros_like(dk_acc)
         dv_acc[...] = jnp.zeros_like(dv_acc)
+        dwq_acc[...] = jnp.zeros_like(dwq_acc)
+        bias_ref[...] = jnp.zeros_like(bias_ref)
 
     linked = segq_ref[...] == segk_ref[...]
     heads = q_ref.shape[1] // HEAD_DIM
     half = STATS // 2
+    dq_parts = []
     for h in range(heads):
         cols = slice(h * HEAD_DIM, (h + 1) * HEAD_DIM)
         q = q_ref[:, cols]
@@ -93,15 +96,30 @@
         dp = lax.dot_general(dctx, v_ref[:, cols], (((1,), (1,)), ((), ())), preferred_element_type=jnp.float32)
         inner = jnp.sum(p * dp, axis=1, keepdims=True)
         ds = (p * (dp - inner)).astype(jnp.bfloat16)
-        dq = jnp.dot(ds, k, preferred_element_type=jnp.float32) * SCALE
-        dq_ref[:, cols] = dq.astype(dq_ref.dtype)
+        dq = (jnp.dot(ds, k, preferred_element_type=jnp.float32) * SCALE).astype(dq_ref.dtype)
+        dq_ref[:, cols] = dq
+        dq_parts.append(dq)
         dk_acc[:, cols] += lax.dot_general(ds, q, (((0,), (0,)), ((), ())), preferred_element_type=jnp.float32)
         dv_acc[:, cols] += lax.dot_general(p.astype(jnp.bfloat16), dctx, (((0,), (0,)), ((), ())), preferred_element_type=jnp.float32)
+    dq_block = jnp.concatenate(dq_parts, axis=1)
+    dwq_acc[...] += lax.dot_general(x_ref[...], dq_block, (((0,), (0,)), ((), ())), preferred_element_type=jnp.float32)
+    bias_ref[0:1, :] += jnp.sum(dq_block.astype(jnp.float32), axis=0, keepdims=True)
 
     @pl.when(step == pl.num_programs(0) - 1)
     def _():
-        dk_ref[...] = (dk_acc[...] * SCALE).astype(dk_ref.dtype)
-        dv_ref[...] = dv_acc[...].astype(dv_ref.dtype)
+        width = dk_ref.shape[1]
+        dk = (dk_acc[...] * SCALE).astype(dk_ref.dtype)
+        dv = dv_acc[...].astype(dv_ref.dtype)
+        dk_ref[...] = dk
+        dv_ref[...] = dv
+        bias_ref[1:2, :] = jnp.sum(dv.astype(jnp.float32), axis=0, keepdims=True)
+        xall = xall_ref[...]
+        wgrad_ref[:, 0:width] = dwq_acc[...].astype(wgrad_ref.dtype)
+        wgrad_ref[:, width : 2 * width] = lax.dot_general(
+            xall, dk, (((0,), (0,)), ((), ())), preferred_element_type=jnp.float32).astype(wgrad_ref.dtype)
+        wgrad_ref[:, 2 * width : 3 * width] = lax.dot_general(
+            xall, dv, (((0,), (0,)), ((), ())), preferred_element_type=jnp.float32).astype(wgrad_ref.dtype)
+        wgrad_ref[:, 3 * width : 4 * width] = out_t_ref[...]
 
 
 def attention_forward(queries, key_side, value_proj, segment_row, block=256):
@@ -125,26 +143,36 @@
     )(queries, key_side, value_proj, segq, segk)
 
 
-def attention_backward(queries, key_side, value_proj, segment_row, stats, grad_context, block=256):
+def attention_backward(queries, key_side, value_proj, segment_row, stats, grad_context, inputs, out_t, block=256):
     length, width = queries.shape
+    features = inputs.shape[1]
     segq = segment_row.reshape(length, 1)
     segk = segment_row.reshape(1, length)
     full = pl.BlockSpec((length, width), lambda i: (0, 0))
     rows = pl.BlockSpec((block, width), lambda i: (i, 0))
     return pl.pallas_call(
         attn_bwd_kernel,
-        out_shape=tuple(jax.ShapeDtypeStruct((length, width), jnp.bfloat16) for _ in range(3)),
+        out_shape=tuple(jax.ShapeDtypeStruct((length, width), jnp.bfloat16) for _ in range(3))
+        + (jax.ShapeDtypeStruct((features, 4 * width), jnp.bfloat16),
+           jax.ShapeDtypeStruct((8, width), jnp.float32)),
         grid=(length // block,),
         in_specs=[rows, full, full, rows,
                   pl.BlockSpec((block, 1), lambda i: (i, 0)),
                   pl.BlockSpec((1, length), lambda i: (0, 0)),
-                  pl.BlockSpec((block, STATS), lambda i: (i, 0))],
-        out_specs=(rows, full, full),
-        scratch_shapes=[pltpu.VMEM((length, width), jnp.float32), pltpu.VMEM((length, width), jnp.float32)],
-        compiler_params=pltpu.CompilerParams(dimension_semantics=("arbitrary",)),
-        cost_estimate=pl.CostEstimate(flops=10 * length * length * width, transcendentals=length * length * width // HEAD_DIM,
-                                      bytes_accessed=14 * length * width),
-    )(queries, key_side, value_proj, grad_context, segq, segk, stats)
+                  pl.BlockSpec((block, STATS), lambda i: (i, 0)),
+                  pl.BlockSpec((block, features), lambda i: (i, 0)),
+                  pl.BlockSpec((length, features), lambda i: (0, 0)),
+                  pl.BlockSpec((features, width), lambda i: (0, 0))],
+        out_specs=(rows, full, full,
+                   pl.BlockSpec((features, 4 * width), lambda i: (0, 0)),
+                   pl.BlockSpec((8, width), lambda i: (0, 0))),
+        scratch_shapes=[pltpu.VMEM((length, width), jnp.float32), pltpu.VMEM((length, width), jnp.float32),
+                        pltpu.VMEM((features, width), jnp.float32)],
+        compiler_params=pltpu.CompilerParams(dimension_semantics=("arbitrary",), vmem_limit_bytes=60 * 1024 * 1024),
+        cost_estimate=pl.CostEstimate(flops=10 * length * length * width + 6 * length * features * width,
+                                      transcendentals=length * length * width // HEAD_DIM,
+                                      bytes_accessed=14 * length * width + 10 * features * width),
+    )(queries, key_side, value_proj, grad_context, segq, segk, stats, inputs, inputs, out_t)
 
 
 def gather_shards(first_pieces, second_pieces, after=None):
@@ -291,30 +319,15 @@
     grad_context = contract_last(attn_grad_low, o_sh.reshape(-1, o_sh.shape[2])).astype(
         jnp.bfloat16
     )
-    output_grad_t = contract_rows(attn_grad_low, context)
-    query_low, key_low, value_low = attention_backward(
-        queries, key_side, value_proj, segment_row, softmax_stats, grad_context
-    )
-    ffn_rows, query_low, key_low, value_low = lax.optimization_barrier(
-        (ffn_rows, query_low, key_low, value_low)
-    )
-    grad_query_bias = jnp.sum(query_low, 0, dtype=jnp.float32)
-    grad_value_bias = jnp.sum(value_low, 0, dtype=jnp.float32)
-    attn_rows = scatter_rows(
-        [
-            contract_rows(input_rows, query_low),
-            contract_rows(input_rows, key_low),
-            contract_rows(input_rows, value_low),
-            output_grad_t,
-        ]
-    )
-    summed = scatter_parts([ffn_rows, attn_rows], [2, 4])
-    input_grad = (
-        attn_grad
-        + product(query_low, qt_full)
-        + product(key_low, kt_full)
-        + product(value_low, vt_full)
-    )
+    output_grad_t = contract_rows(attn_grad_low, context).astype(jnp.bfloat16)
+    query_low, key_low, value_low, attn_joined, qv_bias = attention_backward(
+        queries, key_side, value_proj, segment_row, softmax_stats, grad_context, input_rows,
+        output_grad_t,
+    )
+    ffn_rows, attn_joined, qv_bias = lax.optimization_barrier((ffn_rows, attn_joined, qv_bias))
+    grad_query_bias = qv_bias[0]
+    grad_value_bias = qv_bias[1]
+    attn_rows = scatter_rows([attn_joined])
     small = lax.psum(
         jnp.concatenate(
             [
@@ -331,6 +344,14 @@
         ),
         ("dp", "tensor"),
     )
+    input_grad = (
+        attn_grad
+        + product(query_low, qt_full)
+        + product(key_low, kt_full)
+        + product(value_low, vt_full)
+    )
+    attn_rows, small, input_grad = lax.optimization_barrier((attn_rows, small, input_grad))
+    summed = scatter_parts([ffn_rows, attn_rows], [2, 4])
     split_width = 2 * head_width * part_count + up_bias.shape[0] * part_count
     split = small[:split_width]
     shared = small[split_width:].reshape(6, -1)

time: 496 us -> 469 us (0.946)
  local copies, waits for them, and re-layouts: 46.6 us -> 26.9 us
  waiting for transfers between devices: 125 us -> 116 us
  Pallas kernels: 96.5 us -> 104 us
  matrix products: 109 us -> 102 us
    unnamed x6 -> x5, waiting for transfers between devices: 42.5 us -> 0.08 us
    reduce_scatter x1, waiting for transfers between devices: 0.01 us -> 36.9 us  [scatter_parts(): lax.psum_scatter(joined, 'tensor', scatter_dimension=0, tiled=True)]
    unnamed x127 -> x126, local copies, waits for them, and re-layouts: 27.3 us -> 7.38 us
    pallas_call x1, Pallas kernels: 61.3 us -> 68.9 us  [attention_backward(): pl.pallas_call(attn_bwd_kernel, out_shape=tuple((jax.ShapeDtypeStruct((le...]
    dot_general x6 -> x3, matrix products: 26.4 us -> 20.9 us  [contract_rows(): lax.dot_general(left_side, right_side, (((0,), (0,)), ((), ())), preferre...]
    concatenate x1, other arithmetic: 3.71 us -> 8.86 us  [scatter_parts(): joined = jnp.concatenate(flat, axis=1).reshape(-1, 128)]
  transfers between devices with their start and end apart: 7 -> 7, of which waited for: 4 -> 4; matrix products, arithmetic and copies ran while one was open for 13% -> 11% of each run, Pallas kernels for 20% -> 23%
where the time goes in v9:
time: 469 us; the launch traced here: 460 us
  waiting for transfers between devices  116 us (25%)
  Pallas kernels  104 us (22%)
  matrix products  102 us (22%)
  blocking collectives  52.3 us (11%)
  other arithmetic  43.1 us (9%)
  local copies, waits for them, and re-layouts  26.9 us (6%)
  between operations  15.2 us (3%)
    all_gather x2, waiting for transfers between devices, gather_shards(): gathered = lax.all_gather(mine, 'tensor', axis=0, tiled=False)  78.8 us
    pallas_call x1, Pallas kernels, attention_backward(): pl.pallas_call(attn_bwd_kernel, out_shape=tuple((jax.ShapeDtypeStruct((le...  68.9 us
    dot_general x12, matrix products, contract_last(): lax.dot_general(left_side, right_side, (((1,), (1,)), ((), ())), preferre...  44.1 us
    psum x1, blocking collectives, on_device(): lax.psum(jnp.concatenate([grad_query_bias, grad_value_bias, grad_up_bias,...  39.1 us
    reduce_scatter x1, waiting for transfers between devices, scatter_parts(): lax.psum_scatter(joined, 'tensor', scatter_dimension=0, tiled=True)  36.9 us
    dot_general x15, matrix products, product(): return jnp.dot(left_side, right_side, preferred_element_type=jnp.float32)  36.8 us
    pallas_call x1, Pallas kernels, attention_forward(): pl.pallas_call(attn_fwd_kernel, out_shape=(jax.ShapeDtypeStruct((length,...  35.2 us
    dot_general x3, matrix products, contract_rows(): lax.dot_general(left_side, right_side, (((0,), (0,)), ((), ())), preferre...  20.9 us
  transfers between devices with their start and end apart: 7, of which 4 were waited for; matrix products, arithmetic and copies ran while one was open for 11% of the time, Pallas kernels for 23%

profile of v9, /device:TPU:0, one launch (start us, length us, event | category | flops | bytes accessed | tf_op | source)
XLA Modules:
  0.0 459.8 jit_solution(6596362905696934071)
XLA Ops:
  10.9 52.5 %all-gather.6.cloned.1.call-done = bf16[4,2,192,768]{3,2,1,0:T(8,128)(2,1)} async-done(((bf16[1,2,192,768]{3,2,1,0:T(8,128)(2,1)}), bf16[4,2,192,768]{3,2,1,0:T(8,128)(2,1)}) %all-gather.6.cloned.1.call-update) | async-done | bytes 2359312 | tf_op jit(solution)/shard_map/all_gather | solution.py:183
  63.5 13.1 %all-gather.2 = f32[4,1,1152]{2,1,0:T(1,128)S(1)} all-gather(f32[1,1,1152]{2,1,0:T(1,128)S(1)} %reshape.227), channel_id=2, replica_groups=mesh['dp'=8,'tensor'=4] {'tensor'}, dimensions={0}, use_global_device_ids=true | all-gather | bytes 23040 | tf_op jit(solution)/shard_map/all_gather | solution.py:249
  87.0 2.7 add_convert_fusion.1.v_ref
  89.7 2.6 add_convert_fusion.2.q_ref
  92.3 35.2 %shard_map.305 = (bf16[1024,768]{1,0:T(8,128)(2,1)}, f32[1024,128]{1,0:T(8,128)}) custom-call(bf16[1024,768]{1,0:T(8,128)(2,1)} %add_convert_fusion.2.q_ref, bf16[1024,768]{1,0:T(8,128)(2,1)} %convolution_convert_fusion.10.k_ref, bf16[1024,768]{1,0:T(8,128)(2,1)} %add_convert_fusion.1.v_ref, s32[1024,1]{1,0:T(8,128)} %copy.56.segq_ref, ...), custom_call_target="tpu_custom_call" | custom-call | flops 3221225472 | bytes 6291456 | tf_op jit(solution)/shard_map/pallas_call | solution.py:130
  127.5 26.3 %all-gather.8.cloned.1.call-done = bf16[3072,768]{1,0:T(8,128)(2,1)} async-done(((bf16[768,768]{1,0:T(8,128)(2,1)}), bf16[3072,768]{1,0:T(8,128)(2,1)}) %all-gather.8.cloned.1.call-update) | async-done | bytes 4718608 | tf_op jit(solution)/shard_map/all_gather | solution.py:183
  162.1 6.7 %broadcast_select_fusion = (bf16[4,1,768,768]{3,2,0,1:T(8,128)(2,1)}, bf16[4,1,768,768]{3,2,0,1:T(8,128)(2,1)S(1)}) fusion(bf16[4,1,768,768]{3,2,0,1:T(8,128)(2,1)} %collective-permute-done.1, bf16[4,1,768,768]{3,2,0,1:T(8,128)(2,1)} %bitcast.144, pred[]{:T(512)S(6)} %eq.2), kind=kLoop, calls=%fused_computation.16 | loop fusion | flops 4718592 | bytes 18874368 | tf_op jit(solution)/shard_map/jit(_where)/select_n | solution.py:187
  168.7 3.9 multiply_convert_fusion
  172.6 3.8 multiply_convert_fusion.1
  176.5 3.9 multiply_convert_fusion.2
  183.7 3.9 multiply_convert_fusion.3
  189.1 2.7 fusion.78
  198.4 9.0 %fusion.8 = bf16[768,3072]{1,0:T(8,128)(2,1)S(1)} fusion(bf16[1024,768]{1,0:T(8,128)(2,1)S(1)} %convert_element_type.149, bf16[1024,768]{0,1:T(8,128)(2,1)} %copy-done.46, bf16[1024,768]{0,1:T(8,128)(2,1)} %copy-done.47, bf16[1024,768]{0,1:T(8,128)(2,1)} %copy-done.48, bf16[1024,768]{0,1:T(8,128)(2,1)} %copy-done.49), kind=kOutput, calls=%fused_computation.12 | convolution fusion | flops 4859363328 | bytes 12582912 | tf_op jit(solution)/shard_map/dot_general | solution.py:19
  207.4 5.3 %fusion.44 = bf16[1024,768]{0,1:T(8,128)(2,1)S(1)} fusion(f32[1024,768]{0,1:T(8,128)} %get-tuple-element.137, f32[768]{0:T(1024)S(1)} %get-tuple-element.93, bf16[1024,768]{1,0:T(8,128)(2,1)} %copy-done.25, bf16[4,1,768,768]{3,2,0,1:T(8,128)(2,1)S(1)} %bitcast.146), kind=kOutput, calls=%fused_computation.59 | convolution fusion | flops 1224474624 | bytes 7475200 | tf_op jit(solution)/shard_map/dot_general | solution.py:25
  212.8 3.2 fusion.37
  216.1 3.2 fusion.30
  219.3 3.7 fusion.23
  223.0 3.1 fusion.47
  226.2 3.1 fusion.50
  229.3 3.1 fusion.53
  232.4 9.3 %convolution_convert_fusion = bf16[768,3072]{1,0:T(8,128)(2,1)S(1)} fusion(bf16[1024,768]{1,0:T(8,128)(2,1)} %copy-done.24, bf16[1024,768]{0,1:T(8,128)(2,1)S(1)} %fusion.44, bf16[1024,768]{0,1:T(8,128)(2,1)} %copy-done.18, bf16[1024,768]{0,1:T(8,128)(2,1)} %copy-done.20, bf16[1024,768]{0,1:T(8,128)(2,1)} %copy-done.22), kind=kOutput, calls=%fused_computation.11 | convolution fusion | flops 4859363328 | bytes 12582912 | tf_op jit(solution)/shard_map/dot_general | solution.py:19
  241.7 4.0 pad_maximum_fusion
  245.7 8.7 %add_add_fusion.1 = f32[1024,768]{1,0:T(8,128)} fusion(f32[1024,768]{1,0:T(8,128)} %fusion.53, f32[1024,768]{1,0:T(8,128)} %fusion.50, f32[1024,768]{1,0:T(8,128)} %copy-done.2, f32[1024,768]{1,0:T(8,128)} %fusion.47, bf16[1024,768]{0,1:T(8,128)(2,1)} %copy-done.8, bf16[4,1,768,768]{3,2,0,1:T(8,128)(2,1)} %copy-done.7), kind=kOutput, calls=%fused_computation.65 | convolution fusion | flops 1211105280 | bytes 18481152 | tf_op jit(solution)/shard_map/dot_general | solution.py:25
  254.5 3.1 multiply_reduce_fusion
  264.4 68.9 %shard_map.306 = (bf16[1024,768]{1,0:T(8,128)(2,1)}, bf16[1024,768]{1,0:T(8,128)(2,1)}, bf16[1024,768]{1,0:T(8,128)(2,1)}, bf16[768,3072]{1,0:T(8,128)(2,1)}, f32[8,768]{1,0:T(8,128)}) custom-call(bf16[1024,768]{1,0:T(8,128)(2,1)} %add_convert_fusion.2.q_ref, bf16[1024,768]{1,0:T(8,128)(2,1)} %convolution_convert_fusion.10.k_ref, ...), custom_call_target="tpu_custom_call" | custom-call | flops 11676942336 | bytes 16908288 | tf_op jit(solution)/shard_map/pallas_call | solution.py:153
  334.6 2.9 fusion.79
  340.9 5.8 %convert_reduce_fusion = f32[3072]{0:T(1024)S(1)} fusion(bf16[1024,768]{0,1:T(8,128)(2,1)S(1)} %copy-done.9, bf16[1024,768]{0,1:T(8,128)(2,1)S(1)} %copy-done.19, bf16[1024,768]{0,1:T(8,128)(2,1)S(1)} %copy-done.21, bf16[1024,768]{0,1:T(8,128)(2,1)S(1)} %copy-done.23), kind=kLoop, calls=%fused_computation | loop fusion | flops 28308480 | bytes 6303744 | tf_op jit(solution)/shard_map/reduce_sum | solution.py:308
  346.7 3.1 add_add_fusion
  352.8 39.1 %psum.7 = f32[9216]{0:T(1024)} all-reduce(f32[9216]{0:T(1024)S(1)} %constant_dynamic-update-slice_fusion), channel_id=1, replica_groups=mesh['dp'=8,'tensor'=4] {'dp','tensor'}, use_global_device_ids=true, to_apply=%region_17.18 | all-reduce | flops 9216 | bytes 73728 | tf_op jit(solution)/shard_map/psum | solution.py:331
  395.5 8.9 %pad_maximum_fusion.2 = bf16[4,221184]{1,0:T(4,128)(2,1)S(1)} fusion(bf16[4,73728]{1,0:T(4,128)(2,1)S(1)} %reshape.223, bf16[4,147456]{1,0:T(4,128)(2,1)S(1)} %bitcast.141), kind=kLoop, calls=%fused_computation.84 | loop fusion | flops 3538944 | bytes 3538944 | tf_op jit(solution)/shard_map/concatenate | solution.py:203
  404.4 3.0 reshape.224
  409.4 36.9 %reduce-scatter.8.cloned.1.call-done = bf16[1728,128]{1,0:T(8,128)(2,1)} async-done(((bf16[6912,128]{1,0:T(8,128)(2,1)}), bf16[1728,128]{1,0:T(8,128)(2,1)}) %reduce-scatter.8.cloned.1.call-update) | async-done | bytes 442384 | tf_op jit(solution)/shard_map/reduce_scatter | solution.py:204
  (207 shorter events, 59.7 us)
Async XLA Ops:
  7.2 69.7 %copy-start = (s32[4,1024]{1,0:T(4,128)S(1)}, s32[4,1024]{1,0:T(4,128)}, u32[]{:S(2)}) copy-start(s32[4,1024]{1,0:T(4,128)} %param.19) | copy-start | bytes 49156
  7.2 56.2 %all-gather.6.cloned.1.call-start = ((), (), s32[]{:S(2)}) async-start(), calls=%async_computation.3 | async-start | bytes 2949120 | tf_op jit(solution)/shard_map/all_gather | solution.py:183
  7.3 56.1 %copy-start.41 = (f32[768]{0:T(1024)S(1)}, f32[768]{0:T(1024)}, u32[]{:S(2)}) copy-start(f32[768]{0:T(1024)} %param.30) | copy-start | bytes 9220
  7.3 56.1 %copy-start.42 = (f32[192]{0:T(256)S(1)}, f32[192]{0:T(256)}, u32[]{:S(2)}) copy-start(f32[192]{0:T(256)} %param.21) | copy-start | bytes 2308
  7.3 56.1 %copy-start.43 = (f32[192]{0:T(256)S(1)}, f32[192]{0:T(256)}, u32[]{:S(2)}) copy-start(f32[192]{0:T(256)} %param.24) | copy-start | bytes 2308
  9.6 144.2 %all-gather.8.cloned.1.call-start = ((), (), s32[]{:S(2)}) async-start(), calls=%async_computation.7 | async-start | bytes 5898240 | tf_op jit(solution)/shard_map/all_gather | solution.py:183
  10.9 322.5 %reduce-scatter.4.cloned.1.call-start = ((), (), s32[]{:S(2)}) async-start(), calls=%async_computation.4 | async-start | bytes 10616832 | tf_op jit(solution)/shard_map/reduce_scatter | solution.py:193
  63.4 16.7 %collective-permute-start = (bf16[4,2,192,768]{3,2,1,0:T(8,128)(2,1)}, bf16[4,2,192,768]{3,2,1,0:T(8,128)(2,1)}, u32[]{:S(2)}, u32[]{:S(2)}) collective-permute-start(bf16[4,2,192,768]{3,2,1,0:T(8,128)(2,1)} %all-gather.6.cloned.1.call-done), channel_id=1, source_target_pairs={{0,4},{4,0},{8,12},{12,8},{16,20},{20,16},{24,28},{28,24},{1,5},{5... | collective-permute-start | bytes 7077896 | tf_op jit(solution)/shard_map/ppermute | solution.py:186
  80.2 9.5 %copy-start.10 = (bf16[1024,768]{1,0:T(8,128)(2,1)}, bf16[1024,768]{1,0:T(8,128)(2,1)S(1)}, u32[]{:S(2)}) copy-start(bf16[1024,768]{1,0:T(8,128)(2,1)S(1)} %constant_dynamic-slice_fusion.2.x_ref.xall_ref) | copy-start | bytes 4718596
  82.7 74.7 %copy-start.4 = (bf16[4,2,192,768]{3,2,1,0:T(8,128)(2,1)}, bf16[4,2,192,768]{3,2,1,0:T(8,128)(2,1)S(1)}, u32[]{:S(2)}) copy-start(bf16[4,2,192,768]{3,2,1,0:T(8,128)(2,1)S(1)} %get-tuple-element.103) | copy-start | bytes 7077892
  84.4 5.3 %copy-start.29 = (bf16[4,1,192,768]{3,2,1,0:T(8,128)(2,1)}, bf16[4,1,192,768]{3,2,1,0:T(8,128)(2,1)S(1)}, u32[]{:S(2)}) copy-start(bf16[4,1,192,768]{3,2,1,0:T(8,128)(2,1)S(1)} %get-tuple-element.140) | copy-start | bytes 3538948
  153.8 8.3 %collective-permute-start.1 = (bf16[4,1,768,768]{3,2,0,1:T(8,128)(2,1)}, bf16[4,1,768,768]{3,2,0,1:T(8,128)(2,1)}, u32[]{:S(2)}, u32[]{:S(2)}) collective-permute-start(bf16[4,1,768,768]{3,2,0,1:T(8,128)(2,1)} %bitcast.143), channel_id=1, source_target_pairs={{0,4},{4,0},{8,12},{12,8},{16,20},{20,16},{24,28},{28,24},{1,5},{5... | collective-permute-start | bytes 14155784 | tf_op jit(solution)/shard_map/ppermute | solution.py:186
  153.9 4.1 copy-start.11
  153.9 4.1 copy-start.39
  161.6 22.1 %copy-start.24 = (bf16[1024,768]{1,0:T(8,128)(2,1)}, bf16[1024,768]{1,0:T(8,128)(2,1)S(1)}, u32[]{:S(2)}) copy-start(bf16[1024,768]{1,0:T(8,128)(2,1)S(1)} %fusion.46) | copy-start | bytes 4718596
  168.7 60.5 %copy-start.7 = (bf16[4,1,768,768]{3,2,0,1:T(8,128)(2,1)}, bf16[4,1,768,768]{3,2,0,1:T(8,128)(2,1)S(1)}, u32[]{:S(2)}) copy-start(bf16[4,1,768,768]{3,2,0,1:T(8,128)(2,1)S(1)} %get-tuple-element.102) | copy-start | bytes 14155780
  172.6 16.5 %copy-start.46 = (bf16[1024,768]{0,1:T(8,128)(2,1)}, bf16[1024,768]{0,1:T(8,128)(2,1)S(1)}, u32[]{:S(2)}) copy-start(bf16[1024,768]{0,1:T(8,128)(2,1)S(1)} %get-tuple-element.136) | copy-start | bytes 4718596
  172.6 7.7 %slice-start = ((s8[4718592]{0:T(1024)(128)(4,1)}), s8[4194304]{0:T(1024)(128)(4,1)S(1)}, s32[]{:S(2)}) async-start(s8[4718592]{0:T(1024)(128)(4,1)} %bitcast.145), calls=%async_computation.8 | async-start | bytes 8388608
  176.5 3.9 copy-start.47
  176.5 3.9 slice-start.1
  198.3 9.0 %copy-start.25 = (bf16[1024,768]{1,0:T(8,128)(2,1)}, bf16[1024,768]{1,0:T(8,128)(2,1)S(1)}, u32[]{:S(2)}) copy-start(bf16[1024,768]{1,0:T(8,128)(2,1)S(1)} %convert_element_type.149) | copy-start | bytes 4718596
  207.4 5.4 %copy-start.26 = (bf16[1024,768]{1,0:T(8,128)(2,1)S(1)}, bf16[1024,768]{1,0:T(8,128)(2,1)}, u32[]{:S(2)}) copy-start(bf16[1024,768]{1,0:T(8,128)(2,1)} %copy-done.25) | copy-start | bytes 4718596
  207.4 5.4 %copy-start.51 = (f32[1024,768]{0,1:T(8,128)S(1)}, f32[1024,768]{0,1:T(8,128)}, u32[]{:S(2)}) copy-start(f32[1024,768]{0,1:T(8,128)} %get-tuple-element.131) | copy-start | bytes 9437188
  212.7 19.7 %copy-start.8 = (bf16[1024,768]{0,1:T(8,128)(2,1)}, bf16[1024,768]{0,1:T(8,128)(2,1)S(1)}, u32[]{:S(2)}) copy-start(bf16[1024,768]{0,1:T(8,128)(2,1)S(1)} %fusion.44) | copy-start | bytes 4718596
  216.0 13.2 %copy-start.18 = (bf16[1024,768]{0,1:T(8,128)(2,1)}, bf16[1024,768]{0,1:T(8,128)(2,1)S(1)}, u32[]{:S(2)}) copy-start(bf16[1024,768]{0,1:T(8,128)(2,1)S(1)} %fusion.37) | copy-start | bytes 4718596
  219.3 6.8 %copy-start.20 = (bf16[1024,768]{0,1:T(8,128)(2,1)}, bf16[1024,768]{0,1:T(8,128)(2,1)S(1)}, u32[]{:S(2)}) copy-start(bf16[1024,768]{0,1:T(8,128)(2,1)S(1)} %fusion.30) | copy-start | bytes 4718596
  254.5 137.5 %reduce-scatter.6.cloned.1.call-start = ((), (), s32[]{:S(2)}) async-start(), calls=%async_computation.5 | async-start | bytes 5308416 | tf_op jit(solution)/shard_map/reduce_scatter | solution.py:193
  333.4 112.9 %reduce-scatter.8.cloned.1.call-start = ((), (), s32[]{:S(2)}) async-start(), calls=%async_computation.6 | async-start | bytes 2211840 | tf_op jit(solution)/shard_map/reduce_scatter | solution.py:204
  340.9 5.8 %copy-start.6 = (f32[1024,768]{1,0:T(8,128)S(1)}, f32[1024,768]{1,0:T(8,128)}, u32[]{:S(2)}) copy-start(f32[1024,768]{1,0:T(8,128)} %copy-done.5) | copy-start | bytes 9437188
  340.9 5.8 %copy-start.13 = (bf16[4,1,192,768]{3,2,1,0:T(8,128)(2,1)S(1)}, bf16[4,1,192,768]{3,2,1,0:T(8,128)(2,1)}, u32[]{:S(2)}) copy-start(bf16[4,1,192,768]{3,2,1,0:T(8,128)(2,1)} %copy-done.12) | copy-start | bytes 3538948
  340.9 5.8 %copy-start.17 = (bf16[1024,768]{1,0:T(8,128)(2,1)S(1)}, bf16[1024,768]{1,0:T(8,128)(2,1)}, u32[]{:S(2)}) copy-start(bf16[1024,768]{1,0:T(8,128)(2,1)} %get-tuple-element.44) | copy-start | bytes 4718596
  407.4 45.5 %copy-start.1 = (s32[4,1024]{1,0:T(4,128)S(1)}, s32[4,1024]{1,0:T(4,128)}, u32[]{:S(2)}) copy-start(s32[4,1024]{1,0:T(4,128)} %param.19) | copy-start | bytes 49156
  (32 other events, 76.5 us)
Sparse Core Ops, SparseCore 0:
  10.2 53.1 all-gather.5
  65.6 88.2 all-gather.7
  254.6 75.0 reduce-scatter.3
  333.5 53.8 reduce-scatter.5
  407.6 38.7 reduce-scatter.7
